TPU v7x, 128 devices: a whole 4x4x4 slice. The times are simulated.
128 devices in a mesh: row: 16 (over z, x), col: 8 (over y, core).
Axes of the slice: x: 4, y: 4, z: 4, core: 2. Of those that a mesh axis runs over, the one named last changes fastest.
Arguments:
- residual: bfloat16 [512, 1024, 256], P(('row', 'col')), may hold values from -6 to 6
- interface_inverse: bfloat16 [512, 1024, 1024], P(('row', 'col'))
- modes: bfloat16 [512, 1024, 32], P(('row', 'col')), may hold values from -0.375 to 0.375
- coarse_map: int32 [16384], P(('row', 'col')), may hold values from 0 to 16383, each once
- coarse_inverse: bfloat16 [16384, 16384], P('row', 'col')
- neighbours: int32 [512, 2], P(('row', 'col')), may hold values from 0 to 511, as said below
- block_sizes: int32 [512, 2], P(('row', 'col')), may hold values from 128 to 256, as said below
- block_offsets: int32 [512, 2], P(('row', 'col')), may hold values from 0 to 384, as said below
Outputs:
- preconditioned: bfloat16 [512, 1024, 256], P(('row', 'col'))
Inputs may be any that keep to these rules, and one draw needn't show every extreme that they name: In round k the neighbour of subdomain s is (g XOR a_k) * 4 + (s mod 4) XOR b_k with g = s div 4, where a_k, b_k are the same for all subdomains, a_k is nonzero and a_0 differs from a_1; neighbours are mutual. `block_sizes`: each is 128 or 256, and equal for both sides of a shared block. `block_offsets`: the block of round k lies inside rows [k * 256, (k + 1) * 256) and starts at k * 256 or k * 256 + 256 // 2.
All inputs are finite; a program needn't handle non-finite values.
Results may differ from a plain program's by a relative error of at most 0.0052.
Values may be sent and summed in bfloat16 or wider, within the bound.
No kernel may reach another device: no remote copies, remote signals or barrier semaphores. Data moves between devices by JAX's collectives and lax.ppermute only.
A program may use at most 128 MiB of HBM per device.

v0:
```python
import jax
import jax.numpy as jnp
from jax import lax
from jax.sharding import PartitionSpec as P

MODES = 32
SHARE = 256


def from_partner(value, axis, apart):
    return lax.ppermute(value, axis, [(i, i ^ 1 << apart) for i in range(lax.axis_size(axis))])


def travel(carried, partner_bits):
    total_bits = lax.axis_size(("row", "col")).bit_length() - 1
    for level in range(total_bits):
        other = from_partner(carried, ("row", "col"), level)
        chosen = jnp.bitwise_and(jnp.right_shift(partner_bits, level), 1) == 1
        carried = jnp.where(chosen, other, carried)
    return carried


def neighbour_sum(field, neighbours, block_sizes, block_offsets):
    count = field.shape[0]
    cases = field.shape[2]
    trace_len = field.shape[1]
    half_share = SHARE // 2
    device_index = lax.axis_index(("row", "col"))
    row_index = jnp.arange(SHARE)
    summed = field.astype(jnp.float32)
    for which in range(2):
        start = which * SHARE
        region = field[:, start : start + SHARE]
        relative = block_offsets[:, which] - start
        shifted = jnp.concatenate(
            [region[:, half_share:], jnp.zeros((count, half_share, cases), jnp.bfloat16)], 1
        )
        aligned = jnp.where((relative == 0)[:, None, None], region, shifted)
        inside = (row_index[None, :] < block_sizes[:, which][:, None])[:, :, None]
        aligned = jnp.where(inside, aligned, jnp.zeros_like(aligned))
        partner_bits = jnp.bitwise_xor(neighbours[0, which] // count, device_index)
        received = travel(aligned, partner_bits)
        arrived = jnp.take(received, neighbours[:, which] % count, axis=0)
        moved = jnp.concatenate(
            [jnp.zeros((count, half_share, cases), jnp.bfloat16), arrived[:, : SHARE - half_share]],
            1,
        )
        placed = jnp.where((relative == 0)[:, None, None], arrived, moved)
        summed = summed + jnp.pad(
            placed.astype(jnp.float32), ((0, 0), (start, trace_len - start - SHARE), (0, 0))
        )
    return summed


def weights_of(block_sizes, block_offsets, trace_len):
    trace_rows = jnp.arange(trace_len)
    covered = jnp.zeros((block_sizes.shape[0], trace_len), jnp.float32)
    for which in range(2):
        lower = block_offsets[:, which][:, None]
        upper = lower + block_sizes[:, which][:, None]
        covered = covered + jnp.where(
            (trace_rows[None, :] >= lower) & (trace_rows[None, :] < upper), 1.0, 0.0
        ).astype(jnp.float32)
    return 1.0 / (1.0 + covered)


def shards(
    residual,
    interface_inverse,
    modes,
    coarse_map,
    coarse_inverse,
    neighbours,
    block_sizes,
    block_offsets,
):
    count = residual.shape[0]
    trace_len = residual.shape[1]
    cases = residual.shape[2]
    omega = weights_of(block_sizes, block_offsets, trace_len)
    weighted = (
        omega[:, :, None] * neighbour_sum(residual, neighbours, block_sizes, block_offsets)
    ).astype(jnp.bfloat16)
    local_part = jnp.einsum(
        "sij,sjr->sir", interface_inverse, weighted, preferred_element_type=jnp.float32
    )
    restricted = jnp.einsum(
        "swm,swr->smr", modes, weighted, preferred_element_type=jnp.float32
    ).astype(jnp.bfloat16)
    restricted = restricted.reshape(count * MODES, cases)
    all_rhs, all_map = (
        lax.all_gather(restricted, ("row", "col"), axis=0, tiled=True),
        lax.all_gather(coarse_map, ("row", "col"), axis=0, tiled=True),
    )
    coarse_rhs = jnp.zeros((all_map.shape[0], cases), jnp.bfloat16).at[all_map].set(all_rhs)
    columns = coarse_inverse.shape[1]
    column_part = lax.dynamic_slice_in_dim(coarse_rhs, lax.axis_index("col") * columns, columns, 0)
    partial_sum = jnp.dot(coarse_inverse, column_part, preferred_element_type=jnp.float32)
    own_rows = lax.psum_scatter(partial_sum, "col", scatter_dimension=0, tiled=True).astype(
        jnp.bfloat16
    )
    coarse_full = lax.all_gather(own_rows, ("row", "col"), axis=0, tiled=True)
    picked = jnp.take(coarse_full, coarse_map, axis=0).reshape(count, MODES, cases)
    prolonged = local_part + jnp.einsum(
        "swm,smr->swr", modes, picked, preferred_element_type=jnp.float32
    )
    corrected = (omega[:, :, None] * prolonged).astype(jnp.bfloat16)
    return neighbour_sum(corrected, neighbours, block_sizes, block_offsets).astype(jnp.bfloat16)


def solution(mesh):
    return jax.shard_map(
        shards,
        mesh=mesh,
        in_specs=(
            P(("row", "col"), None, None),
            P(("row", "col"), None, None),
            P(("row", "col"), None, None),
            P(("row", "col")),
            P("row", "col"),
            P(("row", "col"), None),
            P(("row", "col"), None),
            P(("row", "col"), None),
        ),
        out_specs=P(("row", "col"), None, None),
        check_vma=False,
    )
```

profile of v0, /device:TPU:1, one launch (start us, length us, event | category | flops | bytes accessed | tf_op | source)
XLA Modules:
  0.0 565.7 jit_solution(5247554139306587757)
XLA Ops:
  23.2 8.0 %collective-permute-done.1 = bf16[4,256,256]{1,2,0:T(8,128)(2,1)} collective-permute-done((bf16[4,256,256]{1,2,0:T(8,128)(2,1)S(1)}, bf16[4,256,256]{1,2,0:T(8,128)(2,1)}, u32[]{:S(2)}, u32[]{:S(2)}) %collective-permute-start.1) | collective-permute-done | bytes 524320 | tf_op jit(solution)/shard_map/ppermute | solution.py:11
  35.1 7.4 %collective-permute-done.8 = bf16[4,256,256]{1,2,0:T(8,128)(2,1)} collective-permute-done((bf16[4,256,256]{1,2,0:T(8,128)(2,1)S(1)}, bf16[4,256,256]{1,2,0:T(8,128)(2,1)}, u32[]{:S(2)}, u32[]{:S(2)}) %collective-permute-start.8) | collective-permute-done | bytes 524320 | tf_op jit(solution)/shard_map/ppermute | solution.py:11
  46.6 9.5 %collective-permute-done.2 = bf16[4,256,256]{1,2,0:T(8,128)(2,1)S(1)} collective-permute-done((bf16[4,256,256]{1,2,0:T(8,128)(2,1)}, bf16[4,256,256]{1,2,0:T(8,128)(2,1)S(1)}, u32[]{:S(2)}, u32[]{:S(2)}) %collective-permute-start.2) | collective-permute-done | bytes 524320 | tf_op jit(solution)/shard_map/ppermute | solution.py:11
  59.2 8.2 %collective-permute-done.9 = bf16[4,256,256]{1,2,0:T(8,128)(2,1)} collective-permute-done((bf16[4,256,256]{1,2,0:T(8,128)(2,1)S(1)}, bf16[4,256,256]{1,2,0:T(8,128)(2,1)}, u32[]{:S(2)}, u32[]{:S(2)}) %collective-permute-start.9) | collective-permute-done | bytes 524320 | tf_op jit(solution)/shard_map/ppermute | solution.py:11
  73.6 9.0 %collective-permute-done.10 = bf16[4,256,256]{1,2,0:T(8,128)(2,1)} collective-permute-done((bf16[4,256,256]{1,2,0:T(8,128)(2,1)S(1)}, bf16[4,256,256]{1,2,0:T(8,128)(2,1)}, u32[]{:S(2)}, u32[]{:S(2)}) %collective-permute-start.10) | collective-permute-done | bytes 524320 | tf_op jit(solution)/shard_map/ppermute | solution.py:11
  85.4 10.5 %collective-permute-done.4 = bf16[4,256,256]{1,2,0:T(8,128)(2,1)} collective-permute-done((bf16[4,256,256]{1,2,0:T(8,128)(2,1)S(1)}, bf16[4,256,256]{1,2,0:T(8,128)(2,1)}, u32[]{:S(2)}, u32[]{:S(2)}) %collective-permute-start.4) | collective-permute-done | bytes 524320 | tf_op jit(solution)/shard_map/ppermute | solution.py:11
  97.8 9.3 %collective-permute-done.11 = bf16[4,256,256]{1,2,0:T(8,128)(2,1)S(1)} collective-permute-done((bf16[4,256,256]{1,2,0:T(8,128)(2,1)S(1)}, bf16[4,256,256]{1,2,0:T(8,128)(2,1)S(1)}, u32[]{:S(2)}, u32[]{:S(2)}) %collective-permute-start.11) | collective-permute-done | bytes 524320 | tf_op jit(solution)/shard_map/ppermute | solution.py:11
  108.9 3.4 collective-permute-start.6
  112.4 7.6 %collective-permute-done.12 = bf16[4,256,256]{1,2,0:T(8,128)(2,1)} collective-permute-done((bf16[4,256,256]{1,2,0:T(8,128)(2,1)S(1)}, bf16[4,256,256]{1,2,0:T(8,128)(2,1)}, u32[]{:S(2)}, u32[]{:S(2)}) %collective-permute-start.12) | collective-permute-done | bytes 524320 | tf_op jit(solution)/shard_map/ppermute | solution.py:11
  120.8 3.2 collective-permute-start.13
  124.1 10.3 %collective-permute-done.6 = bf16[4,256,256]{1,2,0:T(8,128)(2,1)} collective-permute-done((bf16[4,256,256]{1,2,0:T(8,128)(2,1)S(1)}, bf16[4,256,256]{1,2,0:T(8,128)(2,1)}, u32[]{:S(2)}, u32[]{:S(2)}) %collective-permute-start.6) | collective-permute-done | bytes 524320 | tf_op jit(solution)/shard_map/ppermute | solution.py:11
  139.1 6.5 %collective-permute-done.13 = bf16[4,256,256]{1,2,0:T(8,128)(2,1)} collective-permute-done((bf16[4,256,256]{1,2,0:T(8,128)(2,1)}, bf16[4,256,256]{1,2,0:T(8,128)(2,1)}, u32[]{:S(2)}, u32[]{:S(2)}) %collective-permute-start.13) | collective-permute-done | bytes 524320 | tf_op jit(solution)/shard_map/ppermute | solution.py:11
  150.2 29.7 %all-gather = s32[128,1,128]{2,1,0:T(1,128)S(1)} all-gather(s32[1,1,128]{2,1,0:T(1,128)S(1)} %bitcast.41), channel_id=1, replica_groups=mesh['row'=16,'col'=8] {'row','col'}, dimensions={0}, use_global_device_ids=true | all-gather | bytes 66048 | tf_op jit(solution)/shard_map/all_gather | solution.py:93
  179.9 36.5 %all-gather.4.cloned.1.call-done = bf16[16384,256]{1,0:T(8,128)(2,1)} async-done(((bf16[128,256]{1,0:T(8,128)(2,1)}), bf16[16384,256]{1,0:T(8,128)(2,1)}) %all-gather.4.cloned.1.call-update) | async-done | bytes 8388624 | tf_op jit(solution)/shard_map/all_gather | solution.py:92
  216.4 74.2 %scatter_custom_fusion = bf16[16384,256]{1,0:T(8,128)(2,1)} fusion(s32[16384]{0:T(1024)S(1)} %compare_select_fusion, bf16[16384,256]{1,0:T(8,128)(2,1)} %all-gather.4.cloned.1.call-done, bf16[]{:T(256)} %constant.108.clone.1), kind=kCustom, calls=%fused_computation.8 | custom fusion | bytes 8389120 | tf_op jit(solution)/shard_map/scatter | solution.py:95
  290.6 4.8 convolution_bitcast_fusion
  295.8 26.1 %reduce-scatter.2.cloned.1.call-done = f32[128,256]{0,1:T(8,128)} async-done(((f32[1024,256]{0,1:T(8,128)}), f32[128,256]{0,1:T(8,128)}) %reduce-scatter.2.cloned.1.call-update) | async-done | bytes 131088 | tf_op jit(solution)/shard_map/reduce_scatter | solution.py:99
  323.5 7.7 %fusion.8 = f32[4,256,1024]{2,1,0:T(8,128)} fusion(bf16[4,1024,1024]{2,1,0:T(8,128)(2,1)} %param.11, bf16[4,1024,256]{1,2,0:T(8,128)(2,1)S(1)} %copy.17, bf16[4,256,256]{1,2,0:T(8,128)(2,1)S(1)} %pad_select_fusion.2, bf16[4,256,256]{1,2,0:T(8,128)(2,1)S(1)} %copy-done.4, f32[4,1024]{1,0:T(4,128)S(1)} %add_divide_fusion), kind=kOutput, calls=%fused_computation.59 | convolution fusion | flops 2154823680 | bytes 15745024 | tf_op jit(solution)/shard_map/sij,sjr->sir/dot_general | solution.py:84
  331.2 74.7 %all-gather.6.cloned.1.call-done = bf16[16384,256]{0,1:T(8,128)(2,1)} async-done(((bf16[128,256]{0,1:T(8,128)(2,1)}), bf16[16384,256]{0,1:T(8,128)(2,1)}) %all-gather.6.cloned.1.call-update) | async-done | bytes 8388624 | tf_op jit(solution)/shard_map/all_gather | solution.py:102
  406.0 11.9 %copy.23 = bf16[16384,256]{1,0:T(8,128)(2,1)} copy(bf16[16384,256]{0,1:T(8,128)(2,1)} %all-gather.6.cloned.1.call-done) | data formatting | bytes 16777216 | tf_op jit(solution)/shard_map/all_gather | solution.py:102
  417.9 5.2 gather_fusion
  430.9 11.3 %collective-permute-done.15 = bf16[4,256,256]{1,2,0:T(8,128)(2,1)S(1)} collective-permute-done((bf16[4,256,256]{1,2,0:T(8,128)(2,1)S(1)}, bf16[4,256,256]{1,2,0:T(8,128)(2,1)S(1)}, u32[]{:S(2)}, u32[]{:S(2)}) %collective-permute-start.15) | collective-permute-done | bytes 524320 | tf_op jit(solution)/shard_map/ppermute | solution.py:11
  445.1 8.4 %collective-permute-done.22 = bf16[4,256,256]{1,2,0:T(8,128)(2,1)S(1)} collective-permute-done((bf16[4,256,256]{1,2,0:T(8,128)(2,1)S(1)}, bf16[4,256,256]{1,2,0:T(8,128)(2,1)S(1)}, u32[]{:S(2)}, u32[]{:S(2)}) %collective-permute-start.22) | collective-permute-done | bytes 524320 | tf_op jit(solution)/shard_map/ppermute | solution.py:11
  456.3 10.5 %collective-permute-done.16 = bf16[4,256,256]{1,2,0:T(8,128)(2,1)S(1)} collective-permute-done((bf16[4,256,256]{1,2,0:T(8,128)(2,1)S(1)}, bf16[4,256,256]{1,2,0:T(8,128)(2,1)S(1)}, u32[]{:S(2)}, u32[]{:S(2)}) %collective-permute-start.16) | collective-permute-done | bytes 524320 | tf_op jit(solution)/shard_map/ppermute | solution.py:11
  467.9 10.2 %collective-permute-done.23 = bf16[4,256,256]{1,2,0:T(8,128)(2,1)S(1)} collective-permute-done((bf16[4,256,256]{1,2,0:T(8,128)(2,1)S(1)}, bf16[4,256,256]{1,2,0:T(8,128)(2,1)S(1)}, u32[]{:S(2)}, u32[]{:S(2)}) %collective-permute-start.23) | collective-permute-done | bytes 524320 | tf_op jit(solution)/shard_map/ppermute | solution.py:11
  481.3 9.3 %collective-permute-done.24 = bf16[4,256,256]{1,2,0:T(8,128)(2,1)S(1)} collective-permute-done((bf16[4,256,256]{1,2,0:T(8,128)(2,1)S(1)}, bf16[4,256,256]{1,2,0:T(8,128)(2,1)S(1)}, u32[]{:S(2)}, u32[]{:S(2)}) %collective-permute-start.24) | collective-permute-done | bytes 524320 | tf_op jit(solution)/shard_map/ppermute | solution.py:11
  492.2 11.1 %collective-permute-done.18 = bf16[4,256,256]{1,2,0:T(8,128)(2,1)S(1)} collective-permute-done((bf16[4,256,256]{1,2,0:T(8,128)(2,1)S(1)}, bf16[4,256,256]{1,2,0:T(8,128)(2,1)S(1)}, u32[]{:S(2)}, u32[]{:S(2)}) %collective-permute-start.18) | collective-permute-done | bytes 524320 | tf_op jit(solution)/shard_map/ppermute | solution.py:11
  503.7 10.9 %collective-permute-done.25 = bf16[4,256,256]{1,2,0:T(8,128)(2,1)S(1)} collective-permute-done((bf16[4,256,256]{1,2,0:T(8,128)(2,1)S(1)}, bf16[4,256,256]{1,2,0:T(8,128)(2,1)S(1)}, u32[]{:S(2)}, u32[]{:S(2)}) %collective-permute-start.25) | collective-permute-done | bytes 524320 | tf_op jit(solution)/shard_map/ppermute | solution.py:11
  517.2 9.0 %collective-permute-done.26 = bf16[4,256,256]{1,2,0:T(8,128)(2,1)S(1)} collective-permute-done((bf16[4,256,256]{1,2,0:T(8,128)(2,1)S(1)}, bf16[4,256,256]{1,2,0:T(8,128)(2,1)S(1)}, u32[]{:S(2)}, u32[]{:S(2)}) %collective-permute-start.26) | collective-permute-done | bytes 524320 | tf_op jit(solution)/shard_map/ppermute | solution.py:11
  528.9 9.4 %collective-permute-done.20 = bf16[4,256,256]{1,2,0:T(8,128)(2,1)S(1)} collective-permute-done((bf16[4,256,256]{1,2,0:T(8,128)(2,1)S(1)}, bf16[4,256,256]{1,2,0:T(8,128)(2,1)S(1)}, u32[]{:S(2)}, u32[]{:S(2)}) %collective-permute-start.20) | collective-permute-done | bytes 524320 | tf_op jit(solution)/shard_map/ppermute | solution.py:11
  539.3 10.3 %collective-permute-done.27 = bf16[4,256,256]{1,2,0:T(8,128)(2,1)} collective-permute-done((bf16[4,256,256]{1,2,0:T(8,128)(2,1)}, bf16[4,256,256]{1,2,0:T(8,128)(2,1)}, u32[]{:S(2)}, u32[]{:S(2)}) %collective-permute-start.27) | collective-permute-done | bytes 524320 | tf_op jit(solution)/shard_map/ppermute | solution.py:11
  555.3 3.9 copy.24
  (120 shorter events, 79.0 us)
Async XLA Ops:
  6.5 141.1 %copy-start = (bf16[4,1024,32]{1,2,0:T(8,128)(2,1)S(1)}, bf16[4,1024,32]{1,2,0:T(8,128)(2,1)}, u32[]{:S(2)}) copy-start(bf16[4,1024,32]{1,2,0:T(8,128)(2,1)} %param.12) | copy-start | bytes 786436
  6.5 209.9 %all-gather.4.cloned.1.call-start = ((), (), s32[]{:S(2)}) async-start(), calls=%async_computation.1 | async-start | bytes 8454144 | tf_op jit(solution)/shard_map/all_gather | solution.py:92
  11.8 5.0 collective-permute-start
  13.3 8.6 %collective-permute-start.7 = (bf16[4,256,256]{1,2,0:T(8,128)(2,1)S(1)}, bf16[4,256,256]{1,2,0:T(8,128)(2,1)}, u32[]{:S(2)}, u32[]{:S(2)}) collective-permute-start(bf16[4,256,256]{1,2,0:T(8,128)(2,1)S(1)} %get-tuple-element.15), channel_id=1, source_target_pairs={{0,1},{1,0},{2,3},{3,2},{4,5},{5,4},{6,7},{7,6},{8,9},{9,8},{10,11... | collective-permute-start | bytes 1572872 | tf_op jit(solution)/shard_map/ppermute | solution.py:11
  17.9 13.3 %collective-permute-start.1 = (bf16[4,256,256]{1,2,0:T(8,128)(2,1)S(1)}, bf16[4,256,256]{1,2,0:T(8,128)(2,1)}, u32[]{:S(2)}, u32[]{:S(2)}) collective-permute-start(bf16[4,256,256]{1,2,0:T(8,128)(2,1)S(1)} %broadcast_select_fusion.19), channel_id=1, source_target_pairs={{0,2},{1,3},{2,0},{3,1},{4,6},{5,7},{6,4},{7,5},{8,10},{9,11},{10,... | collective-permute-start | bytes 1572872 | tf_op jit(solution)/shard_map/ppermute | solution.py:11
  23.1 19.4 %collective-permute-start.8 = (bf16[4,256,256]{1,2,0:T(8,128)(2,1)S(1)}, bf16[4,256,256]{1,2,0:T(8,128)(2,1)}, u32[]{:S(2)}, u32[]{:S(2)}) collective-permute-start(bf16[4,256,256]{1,2,0:T(8,128)(2,1)S(1)} %broadcast_select_fusion.5), channel_id=1, source_target_pairs={{0,2},{1,3},{2,0},{3,1},{4,6},{5,7},{6,4},{7,5},{8,10},{9,11},{10,... | collective-permute-start | bytes 1572872 | tf_op jit(solution)/shard_map/ppermute | solution.py:11
  32.1 24.0 %collective-permute-start.2 = (bf16[4,256,256]{1,2,0:T(8,128)(2,1)}, bf16[4,256,256]{1,2,0:T(8,128)(2,1)S(1)}, u32[]{:S(2)}, u32[]{:S(2)}) collective-permute-start(bf16[4,256,256]{1,2,0:T(8,128)(2,1)} %broadcast_select_fusion.21), channel_id=1, source_target_pairs={{0,4},{1,5},{2,6},{3,7},{4,0},{5,1},{6,2},{7,3},{8,12},{9,13},{10,... | collective-permute-start | bytes 1572872 | tf_op jit(solution)/shard_map/ppermute | solution.py:11
  43.6 23.9 %collective-permute-start.9 = (bf16[4,256,256]{1,2,0:T(8,128)(2,1)S(1)}, bf16[4,256,256]{1,2,0:T(8,128)(2,1)}, u32[]{:S(2)}, u32[]{:S(2)}) collective-permute-start(bf16[4,256,256]{1,2,0:T(8,128)(2,1)S(1)} %broadcast_select_fusion.7), channel_id=1, source_target_pairs={{0,4},{1,5},{2,6},{3,7},{4,0},{5,1},{6,2},{7,3},{8,12},{9,13},{10,... | collective-permute-start | bytes 1572872 | tf_op jit(solution)/shard_map/ppermute | solution.py:11
  58.0 11.8 %collective-permute-start.3 = (bf16[4,256,256]{1,2,0:T(8,128)(2,1)}, bf16[4,256,256]{1,2,0:T(8,128)(2,1)}, u32[]{:S(2)}, u32[]{:S(2)}) collective-permute-start(bf16[4,256,256]{1,2,0:T(8,128)(2,1)} %broadcast_select_fusion.23), channel_id=1, source_target_pairs={{0,8},{1,9},{2,10},{3,11},{4,12},{5,13},{6,14},{7,15},{8,0},{9,1},... | collective-permute-start | bytes 1572872 | tf_op jit(solution)/shard_map/ppermute | solution.py:11
  68.6 14.0 %collective-permute-start.10 = (bf16[4,256,256]{1,2,0:T(8,128)(2,1)S(1)}, bf16[4,256,256]{1,2,0:T(8,128)(2,1)}, u32[]{:S(2)}, u32[]{:S(2)}) collective-permute-start(bf16[4,256,256]{1,2,0:T(8,128)(2,1)S(1)} %broadcast_select_fusion.9), channel_id=1, source_target_pairs={{0,8},{1,9},{2,10},{3,11},{4,12},{5,13},{6,14},{7,15},{8,0},{9,1},... | collective-permute-start | bytes 1572872 | tf_op jit(solution)/shard_map/ppermute | solution.py:11
  71.0 25.0 %collective-permute-start.4 = (bf16[4,256,256]{1,2,0:T(8,128)(2,1)S(1)}, bf16[4,256,256]{1,2,0:T(8,128)(2,1)}, u32[]{:S(2)}, u32[]{:S(2)}) collective-permute-start(bf16[4,256,256]{1,2,0:T(8,128)(2,1)S(1)} %broadcast_select_fusion.25), channel_id=1, source_target_pairs={{0,16},{1,17},{2,18},{3,19},{4,20},{5,21},{6,22},{7,23},{8,24},{9,... | collective-permute-start | bytes 1572872 | tf_op jit(solution)/shard_map/ppermute | solution.py:11
  82.6 24.5 %collective-permute-start.11 = (bf16[4,256,256]{1,2,0:T(8,128)(2,1)S(1)}, bf16[4,256,256]{1,2,0:T(8,128)(2,1)S(1)}, u32[]{:S(2)}, u32[]{:S(2)}) collective-permute-start(bf16[4,256,256]{1,2,0:T(8,128)(2,1)S(1)} %broadcast_select_fusion.11), channel_id=1, source_target_pairs={{0,16},{1,17},{2,18},{3,19},{4,20},{5,21},{6,22},{7,23},{8,24},{9,... | collective-permute-start | bytes 1572872 | tf_op jit(solution)/shard_map/ppermute | solution.py:11
  96.0 12.8 %collective-permute-start.5 = (bf16[4,256,256]{1,2,0:T(8,128)(2,1)S(1)}, bf16[4,256,256]{1,2,0:T(8,128)(2,1)S(1)}, u32[]{:S(2)}, u32[]{:S(2)}) collective-permute-start(bf16[4,256,256]{1,2,0:T(8,128)(2,1)S(1)} %broadcast_select_fusion.27), channel_id=1, source_target_pairs={{0,32},{1,33},{2,34},{3,35},{4,36},{5,37},{6,38},{7,39},{8,40},{9,... | collective-permute-start | bytes 1572872 | tf_op jit(solution)/shard_map/ppermute | solution.py:11
  107.2 12.8 %collective-permute-start.12 = (bf16[4,256,256]{1,2,0:T(8,128)(2,1)S(1)}, bf16[4,256,256]{1,2,0:T(8,128)(2,1)}, u32[]{:S(2)}, u32[]{:S(2)}) collective-permute-start(bf16[4,256,256]{1,2,0:T(8,128)(2,1)S(1)} %broadcast_select_fusion.13), channel_id=1, source_target_pairs={{0,32},{1,33},{2,34},{3,35},{4,36},{5,37},{6,38},{7,39},{8,40},{9,... | collective-permute-start | bytes 1572872 | tf_op jit(solution)/shard_map/ppermute | solution.py:11
  108.9 25.4 %collective-permute-start.6 = (bf16[4,256,256]{1,2,0:T(8,128)(2,1)S(1)}, bf16[4,256,256]{1,2,0:T(8,128)(2,1)}, u32[]{:S(2)}, u32[]{:S(2)}) collective-permute-start(bf16[4,256,256]{1,2,0:T(8,128)(2,1)S(1)} %broadcast_select_fusion.29), channel_id=1, source_target_pairs={{0,64},{1,65},{2,66},{3,67},{4,68},{5,69},{6,70},{7,71},{8,72},{9,... | collective-permute-start | bytes 1572872 | tf_op jit(solution)/shard_map/ppermute | solution.py:11
  120.8 24.7 %collective-permute-start.13 = (bf16[4,256,256]{1,2,0:T(8,128)(2,1)}, bf16[4,256,256]{1,2,0:T(8,128)(2,1)}, u32[]{:S(2)}, u32[]{:S(2)}) collective-permute-start(bf16[4,256,256]{1,2,0:T(8,128)(2,1)} %broadcast_select_fusion.15), channel_id=1, source_target_pairs={{0,64},{1,65},{2,66},{3,67},{4,68},{5,69},{6,70},{7,71},{8,72},{9,... | collective-permute-start | bytes 1572872 | tf_op jit(solution)/shard_map/ppermute | solution.py:11
  150.1 171.7 %reduce-scatter.2.cloned.1.call-start = ((), (), s32[]{:S(2)}) async-start(), calls=%async_computation.2 | async-start | bytes 1179648 | tf_op jit(solution)/shard_map/reduce_scatter | solution.py:99
  295.5 110.5 %all-gather.6.cloned.1.call-start = ((), (), s32[]{:S(2)}) async-start(), calls=%async_computation.3 | async-start | bytes 8454144 | tf_op jit(solution)/shard_map/all_gather | solution.py:102
  426.8 2.0 collective-permute-start.14
  427.2 3.0 collective-permute-start.21
  428.9 13.4 %collective-permute-start.15 = (bf16[4,256,256]{1,2,0:T(8,128)(2,1)S(1)}, bf16[4,256,256]{1,2,0:T(8,128)(2,1)S(1)}, u32[]{:S(2)}, u32[]{:S(2)}) collective-permute-start(bf16[4,256,256]{1,2,0:T(8,128)(2,1)S(1)} %broadcast_select_fusion.18), channel_id=1, source_target_pairs={{0,2},{1,3},{2,0},{3,1},{4,6},{5,7},{6,4},{7,5},{8,10},{9,11},{10,... | collective-permute-start | bytes 1572872 | tf_op jit(solution)/shard_map/ppermute | solution.py:11
  430.2 23.2 %collective-permute-start.22 = (bf16[4,256,256]{1,2,0:T(8,128)(2,1)S(1)}, bf16[4,256,256]{1,2,0:T(8,128)(2,1)S(1)}, u32[]{:S(2)}, u32[]{:S(2)}) collective-permute-start(bf16[4,256,256]{1,2,0:T(8,128)(2,1)S(1)} %broadcast_select_fusion.4), channel_id=1, source_target_pairs={{0,2},{1,3},{2,0},{3,1},{4,6},{5,7},{6,4},{7,5},{8,10},{9,11},{10,... | collective-permute-start | bytes 1572872 | tf_op jit(solution)/shard_map/ppermute | solution.py:11
  442.3 24.6 %collective-permute-start.16 = (bf16[4,256,256]{1,2,0:T(8,128)(2,1)S(1)}, bf16[4,256,256]{1,2,0:T(8,128)(2,1)S(1)}, u32[]{:S(2)}, u32[]{:S(2)}) collective-permute-start(bf16[4,256,256]{1,2,0:T(8,128)(2,1)S(1)} %broadcast_select_fusion.20), channel_id=1, source_target_pairs={{0,4},{1,5},{2,6},{3,7},{4,0},{5,1},{6,2},{7,3},{8,12},{9,13},{10,... | collective-permute-start | bytes 1572872 | tf_op jit(solution)/shard_map/ppermute | solution.py:11
  453.5 24.6 %collective-permute-start.23 = (bf16[4,256,256]{1,2,0:T(8,128)(2,1)S(1)}, bf16[4,256,256]{1,2,0:T(8,128)(2,1)S(1)}, u32[]{:S(2)}, u32[]{:S(2)}) collective-permute-start(bf16[4,256,256]{1,2,0:T(8,128)(2,1)S(1)} %broadcast_select_fusion.6), channel_id=1, source_target_pairs={{0,4},{1,5},{2,6},{3,7},{4,0},{5,1},{6,2},{7,3},{8,12},{9,13},{10,... | collective-permute-start | bytes 1572872 | tf_op jit(solution)/shard_map/ppermute | solution.py:11
  466.9 12.2 %collective-permute-start.17 = (bf16[4,256,256]{1,2,0:T(8,128)(2,1)S(1)}, bf16[4,256,256]{1,2,0:T(8,128)(2,1)S(1)}, u32[]{:S(2)}, u32[]{:S(2)}) collective-permute-start(bf16[4,256,256]{1,2,0:T(8,128)(2,1)S(1)} %broadcast_select_fusion.22), channel_id=1, source_target_pairs={{0,8},{1,9},{2,10},{3,11},{4,12},{5,13},{6,14},{7,15},{8,0},{9,1},... | collective-permute-start | bytes 1572872 | tf_op jit(solution)/shard_map/ppermute | solution.py:11
  478.2 12.4 %collective-permute-start.24 = (bf16[4,256,256]{1,2,0:T(8,128)(2,1)S(1)}, bf16[4,256,256]{1,2,0:T(8,128)(2,1)S(1)}, u32[]{:S(2)}, u32[]{:S(2)}) collective-permute-start(bf16[4,256,256]{1,2,0:T(8,128)(2,1)S(1)} %broadcast_select_fusion.8), channel_id=1, source_target_pairs={{0,8},{1,9},{2,10},{3,11},{4,12},{5,13},{6,14},{7,15},{8,0},{9,1},... | collective-permute-start | bytes 1572872 | tf_op jit(solution)/shard_map/ppermute | solution.py:11
  479.2 24.1 %collective-permute-start.18 = (bf16[4,256,256]{1,2,0:T(8,128)(2,1)S(1)}, bf16[4,256,256]{1,2,0:T(8,128)(2,1)S(1)}, u32[]{:S(2)}, u32[]{:S(2)}) collective-permute-start(bf16[4,256,256]{1,2,0:T(8,128)(2,1)S(1)} %broadcast_select_fusion.24), channel_id=1, source_target_pairs={{0,16},{1,17},{2,18},{3,19},{4,20},{5,21},{6,22},{7,23},{8,24},{9,... | collective-permute-start | bytes 1572872 | tf_op jit(solution)/shard_map/ppermute | solution.py:11
  490.7 23.9 %collective-permute-start.25 = (bf16[4,256,256]{1,2,0:T(8,128)(2,1)S(1)}, bf16[4,256,256]{1,2,0:T(8,128)(2,1)S(1)}, u32[]{:S(2)}, u32[]{:S(2)}) collective-permute-start(bf16[4,256,256]{1,2,0:T(8,128)(2,1)S(1)} %broadcast_select_fusion.10), channel_id=1, source_target_pairs={{0,16},{1,17},{2,18},{3,19},{4,20},{5,21},{6,22},{7,23},{8,24},{9,... | collective-permute-start | bytes 1572872 | tf_op jit(solution)/shard_map/ppermute | solution.py:11
  503.4 11.5 %collective-permute-start.19 = (bf16[4,256,256]{1,2,0:T(8,128)(2,1)S(1)}, bf16[4,256,256]{1,2,0:T(8,128)(2,1)S(1)}, u32[]{:S(2)}, u32[]{:S(2)}) collective-permute-start(bf16[4,256,256]{1,2,0:T(8,128)(2,1)S(1)} %broadcast_select_fusion.26), channel_id=1, source_target_pairs={{0,32},{1,33},{2,34},{3,35},{4,36},{5,37},{6,38},{7,39},{8,40},{9,... | collective-permute-start | bytes 1572872 | tf_op jit(solution)/shard_map/ppermute | solution.py:11
  514.6 11.5 %collective-permute-start.26 = (bf16[4,256,256]{1,2,0:T(8,128)(2,1)S(1)}, bf16[4,256,256]{1,2,0:T(8,128)(2,1)S(1)}, u32[]{:S(2)}, u32[]{:S(2)}) collective-permute-start(bf16[4,256,256]{1,2,0:T(8,128)(2,1)S(1)} %broadcast_select_fusion.12), channel_id=1, source_target_pairs={{0,32},{1,33},{2,34},{3,35},{4,36},{5,37},{6,38},{7,39},{8,40},{9,... | collective-permute-start | bytes 1572872 | tf_op jit(solution)/shard_map/ppermute | solution.py:11
  515.0 23.2 %collective-permute-start.20 = (bf16[4,256,256]{1,2,0:T(8,128)(2,1)S(1)}, bf16[4,256,256]{1,2,0:T(8,128)(2,1)S(1)}, u32[]{:S(2)}, u32[]{:S(2)}) collective-permute-start(bf16[4,256,256]{1,2,0:T(8,128)(2,1)S(1)} %broadcast_select_fusion.28), channel_id=1, source_target_pairs={{0,64},{1,65},{2,66},{3,67},{4,68},{5,69},{6,70},{7,71},{8,72},{9,... | collective-permute-start | bytes 1572872 | tf_op jit(solution)/shard_map/ppermute | solution.py:11
  527.0 22.6 %collective-permute-start.27 = (bf16[4,256,256]{1,2,0:T(8,128)(2,1)}, bf16[4,256,256]{1,2,0:T(8,128)(2,1)}, u32[]{:S(2)}, u32[]{:S(2)}) collective-permute-start(bf16[4,256,256]{1,2,0:T(8,128)(2,1)} %broadcast_select_fusion.14), channel_id=1, source_target_pairs={{0,64},{1,65},{2,66},{3,67},{4,68},{5,69},{6,70},{7,71},{8,72},{9,... | collective-permute-start | bytes 1572872 | tf_op jit(solution)/shard_map/ppermute | solution.py:11
  (6 other events, 69.6 us)
Sparse Core Ops, SparseCore 0:
  150.2 66.1 all-gather.3
  295.6 26.1 reduce-scatter.1
  324.6 81.3 all-gather.5
where the time goes:
time: 569 us; the launch traced here: 566 us
  waiting for transfers between devices  325 us (57%)
  local copies, waits for them, and re-layouts  104 us (18%)
  starting transfers between devices  46.1 us (8%)
  blocking collectives  29.7 us (5%)
  other arithmetic  24.2 us (4%)
  between operations  18.8 us (3%)
  matrix products  18 us (3%)
    ppermute x28, waiting for transfers between devices, from_partner(): lax.ppermute(value, axis, [(i, i ^ 1 << apart) for i in range(lax.axis_si...  188 us
    all_gather x1, waiting for transfers between devices, shards(): coarse_full = lax.all_gather(own_rows, ('row', 'col'), axis=0, tiled=True)  74.7 us
    scatter x1, local copies, waits for them, and re-layouts, shards(): jnp.zeros((all_map.shape[0], cases), jnp.bfloat16).at[all_map].set(all_rhs)  74.2 us
    ppermute x28, starting transfers between devices, from_partner(): lax.ppermute(value, axis, [(i, i ^ 1 << apart) for i in range(lax.axis_si...  45.8 us
    all_gather x1, waiting for transfers between devices, shards(): lax.all_gather(restricted, ('row', 'col'), axis=0, tiled=True)  36.5 us
    all_gather x1, blocking collectives, shards(): lax.all_gather(coarse_map, ('row', 'col'), axis=0, tiled=True)  29.7 us
    reduce_scatter x1, waiting for transfers between devices, shards(): lax.psum_scatter(partial_sum, 'col', scatter_dimension=0, tiled=True)  26.1 us
    select_n x28, other arithmetic, travel(): carried = jnp.where(chosen, other, carried)  15.8 us
  transfers between devices with their start and end apart: 31, of which 24 were waited for; matrix products, arithmetic and copies ran while one was open for 4% of the time, Pallas kernels for 0%

commit v1 on v0

v1 whole, which is shorter than its diff:
```python
import jax
import jax.numpy as jnp
from jax import lax
from jax.experimental import pallas as pl
from jax.experimental.pallas import tpu as pltpu
from jax.sharding import PartitionSpec as P

AXES = ("row", "col")
MODES = 32
HALF = 128
LANE = 128
GROUP = 8
VMEM_LIMIT = 40 * 1024 * 1024


def spread(value):
    return lax.all_to_all(value, AXES, 0, 0, tiled=True)


def call(kernel, out_shape, **kw):
    return pl.pallas_call(
        kernel,
        out_shape=out_shape,
        compiler_params=pltpu.CompilerParams(vmem_limit_bytes=VMEM_LIMIT),
        **kw,
    )


def smem():
    return pl.BlockSpec(memory_space=pltpu.SMEM)


def table_of(neighbours, block_sizes, block_offsets):
    count = neighbours.shape[0]
    own = lax.axis_index(AXES).astype(jnp.int32)
    device_mask = jnp.bitwise_xor(neighbours[0] // count, own)
    inner_mask = neighbours[0] % count
    second = (block_offsets // HALF) % 2
    both = block_sizes // HALF - 1
    return jnp.concatenate([device_mask, inner_mask, second.reshape(-1), both.reshape(-1)]).astype(
        jnp.int32
    )


def flags(table, sub, which):
    return table[4 + sub * 2 + which], table[12 + sub * 2 + which]


def pack_blocks(field, table):
    count, _, cases = field.shape
    second = table[4:12].reshape(count, 2)
    region = field[:, : 4 * HALF].reshape(count, 2, 2, HALF, cases)
    first = jnp.where((second == 1)[:, :, None, None], region[:, :, 1], region[:, :, 0])
    aligned = jnp.stack([first, region[:, :, 1]], 1)
    pieces = aligned.reshape(count, 2, 2, HALF // 8, 8, cases).transpose(0, 1, 3, 2, 4, 5)
    return pieces.reshape(-1, 2, 8, cases)


def reroute_kernel(table, chunks, out):
    def step(device, carry):
        for which in range(2):
            out[device, which] = chunks[jnp.bitwise_xor(device, table[which]), which]
        return carry

    lax.fori_loop(0, chunks.shape[0], step, 0, unroll=8)


def exchange(field, table):
    chunks = spread(pack_blocks(field, table))
    chunks = call(
        reroute_kernel,
        jax.ShapeDtypeStruct(chunks.shape, chunks.dtype),
        in_specs=[smem(), pl.BlockSpec(memory_space=pltpu.VMEM)],
        out_specs=pl.BlockSpec(memory_space=pltpu.VMEM),
    )(table, chunks)
    count, cases = field.shape[0], field.shape[2]
    return spread(chunks).reshape(count, 2, HALF // 8, 2, 8, cases)


def arrived_rows(table, sub, which, half, arrived):
    second, both = flags(table, sub, which)
    inside = jnp.maximum(both, (second == half).astype(jnp.int32)).astype(jnp.float32)
    other = jnp.bitwise_xor(sub, table[2 + which])
    rows = arrived[other, half * both, :, which].astype(jnp.float32)
    return rows.reshape(HALF, rows.shape[-1]), inside


def weigh_kernel(table, residual, modes, arrived, weighted, restricted):
    sub = pl.program_id(0)
    for which in range(2):
        for half in range(2):
            start = (which * 2 + half) * HALF
            rows, inside = arrived_rows(table, sub, which, half, arrived)
            own = residual[0, start : start + HALF].astype(jnp.float32)
            value = (own + rows * inside) * (1.0 - 0.5 * inside)
            weighted[0, start : start + HALF] = value.astype(jnp.bfloat16)
    weighted[0, 4 * HALF :] = residual[0, 4 * HALF :]
    restricted[0] = lax.dot_general(
        modes[0], weighted[0], (((0,), (0,)), ((), ())), preferred_element_type=jnp.float32
    ).astype(jnp.bfloat16)


def finish_kernel(table, corrected, arrived, out):
    sub = pl.program_id(0)
    for which in range(2):
        for half in range(2):
            start = (which * 2 + half) * HALF
            rows, inside = arrived_rows(table, sub, which, half, arrived)
            own = corrected[0, start : start + HALF].astype(jnp.float32)
            out[0, start : start + HALF] = (own + rows * inside).astype(jnp.bfloat16)
    out[0, 4 * HALF :] = corrected[0, 4 * HALF :]


def correct_kernel(table, local, modes, picked, corrected):
    sub = pl.program_id(0)
    added = lax.dot_general(
        modes[0], picked[0], (((1,), (0,)), ((), ())), preferred_element_type=jnp.float32
    )
    for which in range(2):
        for half in range(2):
            start = (which * 2 + half) * HALF
            second, both = flags(table, sub, which)
            inside = jnp.maximum(both, (second == half).astype(jnp.int32)).astype(jnp.float32)
            value = local[0, start : start + HALF] + added[start : start + HALF]
            corrected[0, start : start + HALF] = (value * (1.0 - 0.5 * inside)).astype(jnp.bfloat16)
    corrected[0, 4 * HALF :] = (local[0, 4 * HALF :] + added[4 * HALF :]).astype(jnp.bfloat16)


def scatter_kernel(received, out, total, staged):
    devices = received.shape[0]
    place = lax.broadcasted_iota(jnp.int32, (LANE, LANE), 0).astype(jnp.float32)
    total[...] = jnp.zeros_like(total)

    def step(block, carry):
        left, right = [], []
        for inner in range(GROUP):
            piece = received[block * GROUP + inner].astype(jnp.float32)
            high = place == piece[2:3]
            low = place == piece[3:4]
            left.append(
                jnp.concatenate(
                    [jnp.where(high, piece[0:1], 0.0), jnp.where(high, piece[1:2], 0.0)], 0
                ).astype(jnp.bfloat16)
            )
            right.append(jnp.where(low, 1.0, 0.0).astype(jnp.bfloat16))
        total[...] += lax.dot_general(
            jnp.concatenate(left, 1),
            jnp.concatenate(right, 1),
            (((1,), (1,)), ((), ())),
            preferred_element_type=jnp.float32,
        )
        return carry

    lax.fori_loop(0, devices // GROUP, step, 0)
    blocks, _, columns = staged.shape
    pieces = columns // LANE
    for block in range(blocks):
        for case in range(2):
            for piece in range(pieces):
                at = case * LANE + block * pieces + piece
                staged[block, case : case + 1, piece * LANE : (piece + 1) * LANE] = total[at : at + 1]

    def copies(row, carry):
        for block in range(blocks):
            out[row * blocks + block] = staged[block].astype(jnp.bfloat16)
        return carry

    lax.fori_loop(0, devices // blocks, copies, 0)


def gather_kernel(received, partial, out, solved):
    devices, _, rows = partial.shape
    pieces = rows // LANE
    row_blocks = LANE // pieces
    col_blocks = devices // row_blocks
    for block in range(row_blocks):
        value = partial[block * col_blocks].astype(jnp.float32)
        for col in range(1, col_blocks):
            value = value + partial[block * col_blocks + col].astype(jnp.float32)
        for piece in range(pieces):
            for case in range(2):
                at = case * LANE + block * pieces + piece
                solved[at : at + 1] = value[case : case + 1, piece * LANE : (piece + 1) * LANE]
    turned = jnp.concatenate([solved[:LANE].T, solved[LANE:].T], 0).astype(jnp.bfloat16)
    place = lax.broadcasted_iota(jnp.int32, (LANE, LANE), 0).astype(jnp.float32)

    def step(block, carry):
        highs, lows = [], []
        for inner in range(GROUP):
            piece = received[block * GROUP + inner].astype(jnp.float32)
            highs.append(jnp.where(place == piece[2:3], 1.0, 0.0).astype(jnp.bfloat16))
            lows.append(place == piece[3:4])
        chosen = lax.dot_general(
            turned,
            jnp.concatenate(highs, 1),
            (((1,), (0,)), ((), ())),
            preferred_element_type=jnp.float32,
        )
        for inner in range(GROUP):
            lanes = slice(inner * LANE, (inner + 1) * LANE)
            both = [
                jnp.sum(
                    jnp.where(lows[inner], chosen[case * LANE : (case + 1) * LANE, lanes], 0.0),
                    axis=0,
                    keepdims=True,
                )
                for case in range(2)
            ]
            out[block * GROUP + inner] = jnp.concatenate(both, 0).astype(jnp.bfloat16)
        return carry

    lax.fori_loop(0, devices // GROUP, step, 0)


def whole():
    return pl.BlockSpec(memory_space=pltpu.VMEM)


def per_sub(*shape):
    zeros = (0,) * len(shape)
    return pl.BlockSpec((1,) + shape, lambda sub: (sub,) + zeros)


def same(*shape):
    zeros = (0,) * len(shape)
    return pl.BlockSpec(shape, lambda sub: zeros)


def shards(
    residual,
    interface_inverse,
    modes,
    coarse_map,
    coarse_inverse,
    neighbours,
    block_sizes,
    block_offsets,
):
    count, trace_len, cases = residual.shape
    devices = cases // 2
    table = table_of(neighbours, block_sizes, block_offsets)
    field = jax.ShapeDtypeStruct(residual.shape, jnp.bfloat16)

    arrived = exchange(residual, table)
    weighted, restricted = call(
        weigh_kernel,
        (field, jax.ShapeDtypeStruct((count, MODES, cases), jnp.bfloat16)),
        grid=(count,),
        in_specs=[
            smem(),
            per_sub(trace_len, cases),
            per_sub(trace_len, MODES),
            same(*arrived.shape),
        ],
        out_specs=(per_sub(trace_len, cases), per_sub(MODES, cases)),
    )(table, residual, modes, arrived)
    local_part = jnp.einsum(
        "sij,sjr->sir", interface_inverse, weighted, preferred_element_type=jnp.float32
    )

    by_case = restricted.reshape(count * MODES, cases).T.reshape(devices, 2, count * MODES)
    digits = jnp.stack([coarse_map // LANE, coarse_map % LANE]).astype(jnp.bfloat16)
    received = spread(
        jnp.concatenate([by_case, jnp.broadcast_to(digits[None], (devices,) + digits.shape)], 1)
    )
    rows, columns = coarse_inverse.shape
    placed = call(
        scatter_kernel,
        jax.ShapeDtypeStruct((devices, 2, columns), jnp.bfloat16),
        in_specs=[whole()],
        out_specs=whole(),
        scratch_shapes=[
            pltpu.VMEM((2 * LANE, LANE), jnp.float32),
            pltpu.VMEM((LANE * LANE // columns, 2, columns), jnp.float32),
        ],
    )(received)
    coarse_rhs = spread(placed).reshape(cases, columns)
    partial_sum = lax.dot_general(
        coarse_rhs, coarse_inverse, (((1,), (1,)), ((), ())), preferred_element_type=jnp.float32
    ).astype(jnp.bfloat16)
    partial_sum = spread(partial_sum.reshape(devices, 2, rows))
    picked = call(
        gather_kernel,
        jax.ShapeDtypeStruct((devices, 2, LANE), jnp.bfloat16),
        in_specs=[whole(), whole()],
        out_specs=whole(),
        scratch_shapes=[pltpu.VMEM((2 * LANE, LANE), jnp.float32)],
    )(received, partial_sum)
    picked = spread(picked).reshape(cases, count * MODES).T.reshape(count, MODES, cases)

    corrected = call(
        correct_kernel,
        field,
        grid=(count,),
        in_specs=[
            smem(),
            per_sub(trace_len, cases),
            per_sub(trace_len, MODES),
            per_sub(MODES, cases),
        ],
        out_specs=per_sub(trace_len, cases),
    )(table, local_part, modes, picked)
    arrived = exchange(corrected, table)
    return call(
        finish_kernel,
        field,
        grid=(count,),
        in_specs=[smem(), per_sub(trace_len, cases), same(*arrived.shape)],
        out_specs=per_sub(trace_len, cases),
    )(table, corrected, arrived)


def solution(mesh):
    return jax.shard_map(
        shards,
        mesh=mesh,
        in_specs=(
            P(AXES, None, None),
            P(AXES, None, None),
            P(AXES, None, None),
            P(AXES),
            P("row", "col"),
            P(AXES, None),
            P(AXES, None),
            P(AXES, None),
        ),
        out_specs=P(AXES, None, None),
        check_vma=False,
    )
```

time: 569 us -> 209 us (0.37)
  waiting for transfers between devices: 325 us -> 37.8 us
  local copies, waits for them, and re-layouts: 104 us -> 10 us
  blocking collectives: 29.7 us -> 106 us
  starting transfers between devices: 46.1 us -> 21.8 us
  other arithmetic: 24.2 us -> 1.4 us
  Pallas kernels: 0 us -> 19.7 us
  between operations: 18.8 us -> 0.29 us
  matrix products: 18 us -> 11.7 us
    ppermute x28 -> x0, waiting for transfers between devices: 188 us -> none  [from_partner(): lax.ppermute(value, axis, [(i, i ^ 1 << apart) for i in range(lax.axis_si...]
    all_gather x2 -> x0, waiting for transfers between devices: 111 us -> none  [the longest x1 74.7 us: shards(): coarse_full = lax.all_gather(own_rows, ('row', 'col'), axis=0, tiled=True)]
    all_to_all x0 -> x5, blocking collectives: none -> 106 us  [spread(): return lax.all_to_all(value, AXES, 0, 0, tiled=True)]
    scatter x1 -> x0, local copies, waits for them, and re-layouts: 74.2 us -> none  [shards(): jnp.zeros((all_map.shape[0], cases), jnp.bfloat16).at[all_map].set(all_rhs)]
    ppermute x28 -> x0, starting transfers between devices: 45.8 us -> none  [from_partner(): lax.ppermute(value, axis, [(i, i ^ 1 << apart) for i in range(lax.axis_si...]
    all_to_all x0 -> x3, waiting for transfers between devices: none -> 37.8 us  [spread(): return lax.all_to_all(value, AXES, 0, 0, tiled=True)]
    all_gather x1 -> x0, blocking collectives: 29.7 us -> none  [shards(): lax.all_gather(coarse_map, ('row', 'col'), axis=0, tiled=True)]
    reduce_scatter x1 -> x0, waiting for transfers between devices: 26.1 us -> none  [shards(): lax.psum_scatter(partial_sum, 'col', scatter_dimension=0, tiled=True)]
  transfers between devices with their start and end apart: 31 -> 3, of which waited for: 24 -> 3; matrix products, arithmetic and copies ran while one was open for 4% -> 4% of each run, Pallas kernels for 0% -> 0%
where the time goes in v1:
time: 209 us
  blocking collectives  106 us (51%)
  waiting for transfers between devices  37.8 us (18%)
  starting transfers between devices  21.8 us (10%)
  Pallas kernels  19.7 us (9%)
  matrix products  11.7 us (6%)
  local copies, waits for them, and re-layouts  10 us (5%)
    all_to_all x5, blocking collectives, spread(): return lax.all_to_all(value, AXES, 0, 0, tiled=True)  106 us
    all_to_all x3, waiting for transfers between devices, spread(): return lax.all_to_all(value, AXES, 0, 0, tiled=True)  37.8 us
    all_to_all x3, starting transfers between devices, spread(): return lax.all_to_all(value, AXES, 0, 0, tiled=True)  21.8 us
    dot_general x1, matrix products, shards(): jnp.einsum('sij,sjr->sir', interface_inverse, weighted, preferred_element...  8.26 us
    pallas_call x1, Pallas kernels, shards(): call(scatter_kernel, jax.ShapeDtypeStruct((devices, 2, columns), jnp.bflo...  5.89 us
    pallas_call x1, Pallas kernels, shards(): call(gather_kernel, jax.ShapeDtypeStruct((devices, 2, LANE), jnp.bfloat16...  5.58 us
    unnamed x17, local copies, waits for them, and re-layouts  4.96 us
  transfers between devices with their start and end apart: 3, of which 3 were waited for; matrix products, arithmetic and copies ran while one was open for 4% of the time, Pallas kernels for 0%

profile of v1, /device:TPU:1, one launch (start us, length us, event | category | flops | bytes accessed | tf_op | source)
XLA Modules:
  0.0 208.7 jit_solution(4503570917674174649)
XLA Ops:
  0.0 0.7 broadcast_compare_fusion
  0.8 1.3 slice.25
  2.2 0.1 fusion.1
  2.4 1.1 copy.34
  3.5 11.5 %all-to-all-start = ((bf16[128,2,8,256]{3,2,1,0:T(8,128)(2,1)}), bf16[128,2,8,256]{3,2,1,0:T(8,128)(2,1)S(1)}, u32[]{:S(2)}, u32[]{:S(2)}) async-start(bf16[128,2,8,256]{3,2,1,0:T(8,128)(2,1)} %bitcast.55), calls=%async_computation | async-start | bytes 2097152 | tf_op jit(solution)/shard_map/all_to_all | solution.py:17
  15.6 18.3 %all-to-all-done.chunks = bf16[128,2,8,256]{3,2,1,0:T(8,128)(2,1)S(1)} async-done(((bf16[128,2,8,256]{3,2,1,0:T(8,128)(2,1)}), bf16[128,2,8,256]{3,2,1,0:T(8,128)(2,1)S(1)}, u32[]{:S(2)}, u32[]{:S(2)}) %all-to-all-start) | async-done | bytes 1048608 | tf_op jit(solution)/shard_map/all_to_all | solution.py:17
  33.9 0.9 shard_map.82
  34.8 1.0 copy-done.1
  35.7 5.7 %all-to-all-start.1 = ((bf16[128,2,8,256]{3,2,1,0:T(8,128)(2,1)}), bf16[128,2,8,256]{3,2,1,0:T(8,128)(2,1)}, u32[]{:S(2)}, u32[]{:S(2)}) async-start(bf16[128,2,8,256]{3,2,1,0:T(8,128)(2,1)} %copy-done.1), calls=%async_computation.1 | async-start | bytes 2097152 | tf_op jit(solution)/shard_map/all_to_all | solution.py:17
  41.5 0.5 copy.35.modes
  42.0 18.2 %all-to-all-done.1 = bf16[128,2,8,256]{3,2,1,0:T(8,128)(2,1)} async-done(((bf16[128,2,8,256]{3,2,1,0:T(8,128)(2,1)}), bf16[128,2,8,256]{3,2,1,0:T(8,128)(2,1)}, u32[]{:S(2)}, u32[]{:S(2)}) %all-to-all-start.1) | async-done | bytes 1048608 | tf_op jit(solution)/shard_map/all_to_all | solution.py:17
  60.2 2.3 %shard_map.83 = (bf16[4,1024,256]{2,1,0:T(8,128)(2,1)S(1)}, bf16[4,32,256]{2,1,0:T(8,128)(2,1)S(1)}) custom-call(s32[20]{0:T(128)S(1)} %pad_add_fusion.table, bf16[4,1024,256]{2,1,0:T(8,128)(2,1)S(1)} %copy-done, bf16[4,1024,32]{2,1,0:T(8,128)(2,1)S(1)} %copy.35.modes, bf16[4,2,16,2,8,256]{5,4,3,2,1,0:T(8,128)(2,1)} %bitcast.5.arrived), custom_call_target="tpu_custom_call" | custom-call | tf_op jit(solution)/shard_map/pallas_call | solution.py:245
  62.5 1.3 copy-done.3
  64.0 0.1 pad_maximum_fusion
  64.1 14.5 %all_to_all.40.received = bf16[128,4,128]{2,1,0:T(4,128)(2,1)S(1)} all-to-all(bf16[128,4,128]{2,1,0:T(4,128)(2,1)S(1)} %pad_maximum_fusion), channel_id=1, replica_groups=mesh['row'=16,'col'=8] {'row','col'}, dimensions={0} | all-to-all | bytes 262144 | tf_op jit(solution)/shard_map/all_to_all | solution.py:17
  78.7 5.9 %shard_map.84 = bf16[128,2,2048]{2,1,0:T(2,128)(2,1)S(1)} custom-call(bf16[128,4,128]{2,1,0:T(4,128)(2,1)S(1)} %all_to_all.40.received), custom_call_target="tpu_custom_call" | custom-call | tf_op jit(solution)/shard_map/pallas_call | solution.py:267
  84.5 23.1 %all_to_all.41 = bf16[128,2,2048]{2,1,0:T(2,128)(2,1)} all-to-all(bf16[128,2,2048]{2,1,0:T(2,128)(2,1)S(1)} %shard_map.84), channel_id=1, replica_groups=mesh['row'=16,'col'=8] {'row','col'}, dimensions={0} | all-to-all | bytes 2097152 | tf_op jit(solution)/shard_map/all_to_all | solution.py:17
  107.7 1.5 reshape.115
  109.1 3.5 %convolution_convert_fusion = bf16[256,1024]{1,0:T(8,128)(2,1)S(1)} fusion(bf16[256,2048]{1,0:T(8,128)(2,1)S(1)} %reshape.115, bf16[1024,2048]{1,0:T(8,128)(2,1)} %param.12), kind=kOutput, calls=%fused_computation.1 | convolution fusion | flops 1074003968 | bytes 5767168 | tf_op jit(solution)/shard_map/dot_general | solution.py:278
  112.6 0.2 reshape.116
  112.8 17.9 %all_to_all.42.partial = bf16[128,2,1024]{2,1,0:T(2,128)(2,1)S(1)} all-to-all(bf16[128,2,1024]{2,1,0:T(2,128)(2,1)S(1)} %reshape.116), channel_id=1, replica_groups=mesh['row'=16,'col'=8] {'row','col'}, dimensions={0} | all-to-all | bytes 1048576 | tf_op jit(solution)/shard_map/all_to_all | solution.py:17
  130.7 5.6 %shard_map.85 = bf16[128,2,128]{2,1,0:T(2,128)(2,1)} custom-call(bf16[128,4,128]{2,1,0:T(4,128)(2,1)S(1)} %all_to_all.40.received, bf16[128,2,1024]{2,1,0:T(2,128)(2,1)S(1)} %all_to_all.42.partial), custom_call_target="tpu_custom_call" | custom-call | tf_op jit(solution)/shard_map/pallas_call | solution.py:282
  136.3 4.6 %all-to-all-start.5 = ((bf16[128,2,128]{2,1,0:T(2,128)(2,1)}), bf16[128,2,128]{2,1,0:T(2,128)(2,1)S(1)}, u32[]{:S(2)}, u32[]{:S(2)}) async-start(bf16[128,2,128]{2,1,0:T(2,128)(2,1)} %shard_map.85), calls=%async_computation.5 | async-start | bytes 131072 | tf_op jit(solution)/shard_map/all_to_all | solution.py:17
  140.9 8.3 %convolution_bitcast_fusion.local = f32[4,1024,256]{2,1,0:T(8,128)} fusion(bf16[4,1024,1024]{2,1,0:T(8,128)(2,1)} %param.9, bf16[4,1024,256]{2,1,0:T(8,128)(2,1)} %copy-done.3), kind=kOutput, calls=%fused_computation | convolution fusion | flops 2147483648 | bytes 14680064 | tf_op jit(solution)/shard_map/sij,sjr->sir/dot_general | solution.py:257
  149.2 1.3 all-to-all-done.5
  150.6 2.2 %copy-done.2 = f32[4,1024,256]{2,1,0:T(8,128)S(1)} copy-done((f32[4,1024,256]{2,1,0:T(8,128)S(1)}, f32[4,1024,256]{2,1,0:T(8,128)}, u32[]{:S(2)}) %copy-start.2) | copy-done | bytes 4194328
  152.8 1.7 shard_map.86.corrected
  154.6 0.1 fusion
  154.9 27.1 %all_to_all.43.chunks = bf16[128,2,8,256]{3,2,1,0:T(8,128)(2,1)S(1)} all-to-all(bf16[128,2,8,256]{3,2,1,0:T(8,128)(2,1)S(1)} %bitcast.56), channel_id=1, replica_groups=mesh['row'=16,'col'=8] {'row','col'}, dimensions={0} | all-to-all | bytes 2097152 | tf_op jit(solution)/shard_map/all_to_all | solution.py:17
  182.1 0.9 shard_map.87
  182.9 23.3 %all_to_all.44 = bf16[128,2,8,256]{3,2,1,0:T(8,128)(2,1)S(1)} all-to-all(bf16[128,2,8,256]{3,2,1,0:T(8,128)(2,1)S(1)} %shard_map.87), channel_id=1, replica_groups=mesh['row'=16,'col'=8] {'row','col'}, dimensions={0} | all-to-all | bytes 2097152 | tf_op jit(solution)/shard_map/all_to_all | solution.py:17
  206.2 2.5 %shard_map.88 = bf16[4,1024,256]{2,1,0:T(8,128)(2,1)} custom-call(s32[20]{0:T(128)S(1)} %pad_add_fusion.table, bf16[4,1024,256]{2,1,0:T(8,128)(2,1)S(1)} %shard_map.86.corrected, bf16[4,2,16,2,8,256]{5,4,3,2,1,0:T(8,128)(2,1)S(1)} %bitcast.48), custom_call_target="tpu_custom_call" | custom-call | tf_op jit(solution)/shard_map/pallas_call | solution.py:304
  (33 shorter events, 1.4 us)
Async XLA Ops:
  2.1 12.8 %copy-start.5 = (s32[4,2]{0,1:T(2,128)S(1)}, s32[4,2]{0,1:T(2,128)}, u32[]{:S(2)}) copy-start(s32[4,2]{0,1:T(2,128)} %param.14) | copy-start | bytes 100
  2.2 13.2 %copy-start.6 = (s32[4,2]{0,1:T(2,128)S(1)}, s32[4,2]{0,1:T(2,128)}, u32[]{:S(2)}) copy-start(s32[4,2]{0,1:T(2,128)} %param.13) | copy-start | bytes 100
  2.4 39.1 %copy-start.4 = (bf16[4,1024,32]{1,2,0:T(8,128)(2,1)S(1)}, bf16[4,1024,32]{1,2,0:T(8,128)(2,1)}, u32[]{:S(2)}) copy-start(bf16[4,1024,32]{1,2,0:T(8,128)(2,1)} %param.10) | copy-start | bytes 786436
  3.5 38.5 %copy-start.7 = (s32[128]{0:T(128)S(1)}, s32[128]{0:T(128)}, u32[]{:S(2)}) copy-start(s32[128]{0:T(128)} %param.11) | copy-start | bytes 1540
  3.5 56.7 %copy-start = (bf16[4,1024,256]{2,1,0:T(8,128)(2,1)S(1)}, bf16[4,1024,256]{2,1,0:T(8,128)(2,1)}, u32[]{:S(2)}) copy-start(bf16[4,1024,256]{2,1,0:T(8,128)(2,1)} %residual.1) | copy-start | bytes 6291460
  3.5 30.4 %all-to-all-start = ((bf16[128,2,8,256]{3,2,1,0:T(8,128)(2,1)}), bf16[128,2,8,256]{3,2,1,0:T(8,128)(2,1)S(1)}, u32[]{:S(2)}, u32[]{:S(2)}) async-start(bf16[128,2,8,256]{3,2,1,0:T(8,128)(2,1)} %bitcast.55), calls=%async_computation | async-start | bytes 2097152 | tf_op jit(solution)/shard_map/all_to_all | solution.py:17
  34.8 1.0 copy-start.1
  35.7 24.4 %all-to-all-start.1 = ((bf16[128,2,8,256]{3,2,1,0:T(8,128)(2,1)}), bf16[128,2,8,256]{3,2,1,0:T(8,128)(2,1)}, u32[]{:S(2)}, u32[]{:S(2)}) async-start(bf16[128,2,8,256]{3,2,1,0:T(8,128)(2,1)} %copy-done.1), calls=%async_computation.1 | async-start | bytes 2097152 | tf_op jit(solution)/shard_map/all_to_all | solution.py:17
  62.5 1.3 copy-start.3
  136.3 14.2 %all-to-all-start.5 = ((bf16[128,2,128]{2,1,0:T(2,128)(2,1)}), bf16[128,2,128]{2,1,0:T(2,128)(2,1)S(1)}, u32[]{:S(2)}, u32[]{:S(2)}) async-start(bf16[128,2,128]{2,1,0:T(2,128)(2,1)} %shard_map.85), calls=%async_computation.5 | async-start | bytes 131072 | tf_op jit(solution)/shard_map/all_to_all | solution.py:17
  150.6 2.2 %copy-start.2 = (f32[4,1024,256]{2,1,0:T(8,128)S(1)}, f32[4,1024,256]{2,1,0:T(8,128)}, u32[]{:S(2)}) copy-start(f32[4,1024,256]{2,1,0:T(8,128)} %convolution_bitcast_fusion.local) | copy-start | bytes 12582916

commit v2 on v1

--- a/solution.py
+++ b/solution.py
@@ -46,14 +46,22 @@
     return table[4 + sub * 2 + which], table[12 + sub * 2 + which]
 
 
-def pack_blocks(field, table):
-    count, _, cases = field.shape
-    second = table[4:12].reshape(count, 2)
-    region = field[:, : 4 * HALF].reshape(count, 2, 2, HALF, cases)
-    first = jnp.where((second == 1)[:, :, None, None], region[:, :, 1], region[:, :, 0])
-    aligned = jnp.stack([first, region[:, :, 1]], 1)
-    pieces = aligned.reshape(count, 2, 2, HALF // 8, 8, cases).transpose(0, 1, 3, 2, 4, 5)
-    return pieces.reshape(-1, 2, 8, cases)
+def store_blocks(table, sub, load, packed):
+    for which in range(2):
+        second, _ = flags(table, sub, which)
+        for half in range(2):
+            start = which * 2 * HALF + (second * HALF if half == 0 else HALF)
+            rows = load(pl.multiple_of(start, HALF)).astype(jnp.float32)
+            packed[0, half, :, which] = rows.reshape(HALF // 8, 8, rows.shape[-1]).astype(jnp.bfloat16)
+
+
+def pack_kernel(table, field, packed):
+    store_blocks(table, pl.program_id(0), lambda start: field[0, pl.ds(start, HALF)], packed)
+
+
+def local_kernel(table, inverse, weighted, local, packed):
+    local[0] = jnp.dot(inverse[0], weighted[0], preferred_element_type=jnp.float32)
+    store_blocks(table, pl.program_id(0), lambda start: local[0, pl.ds(start, HALF)], packed)
 
 
 def reroute_kernel(table, chunks, out):
@@ -65,16 +73,16 @@
     lax.fori_loop(0, chunks.shape[0], step, 0, unroll=8)
 
 
-def exchange(field, table):
-    chunks = spread(pack_blocks(field, table))
+def exchange(packed, table):
+    count, cases = packed.shape[0], packed.shape[-1]
+    chunks = spread(packed.reshape(-1, 2, 8, cases))
     chunks = call(
         reroute_kernel,
         jax.ShapeDtypeStruct(chunks.shape, chunks.dtype),
-        in_specs=[smem(), pl.BlockSpec(memory_space=pltpu.VMEM)],
-        out_specs=pl.BlockSpec(memory_space=pltpu.VMEM),
+        in_specs=[smem(), whole()],
+        out_specs=whole(),
     )(table, chunks)
-    count, cases = field.shape[0], field.shape[2]
-    return spread(chunks).reshape(count, 2, HALF // 8, 2, 8, cases)
+    return spread(chunks).reshape(packed.shape)
 
 
 def arrived_rows(table, sub, which, half, arrived):
@@ -96,37 +104,34 @@
             weighted[0, start : start + HALF] = value.astype(jnp.bfloat16)
     weighted[0, 4 * HALF :] = residual[0, 4 * HALF :]
     restricted[0] = lax.dot_general(
-        modes[0], weighted[0], (((0,), (0,)), ((), ())), preferred_element_type=jnp.float32
+        modes[0], weighted[0], (((1,), (0,)), ((), ())), preferred_element_type=jnp.float32
     ).astype(jnp.bfloat16)
 
 
-def finish_kernel(table, corrected, arrived, out):
+def prolong(modes, picked):
+    return lax.dot_general(
+        modes, picked, (((0,), (0,)), ((), ())), preferred_element_type=jnp.float32
+    )
+
+
+def finish_kernel(table, local, modes, picked, arrived, arrived_modes, out):
     sub = pl.program_id(0)
+    added = prolong(modes[0], picked[0, sub])
     for which in range(2):
+        other = jnp.bitwise_xor(sub, table[2 + which])
         for half in range(2):
             start = (which * 2 + half) * HALF
             rows, inside = arrived_rows(table, sub, which, half, arrived)
-            own = corrected[0, start : start + HALF].astype(jnp.float32)
-            out[0, start : start + HALF] = (own + rows * inside).astype(jnp.bfloat16)
-    out[0, 4 * HALF :] = corrected[0, 4 * HALF :]
-
-
-def correct_kernel(table, local, modes, picked, corrected):
-    sub = pl.program_id(0)
-    added = lax.dot_general(
-        modes[0], picked[0], (((1,), (0,)), ((), ())), preferred_element_type=jnp.float32
-    )
-    for which in range(2):
-        for half in range(2):
-            start = (which * 2 + half) * HALF
-            second, both = flags(table, sub, which)
-            inside = jnp.maximum(both, (second == half).astype(jnp.int32)).astype(jnp.float32)
-            value = local[0, start : start + HALF] + added[start : start + HALF]
-            corrected[0, start : start + HALF] = (value * (1.0 - 0.5 * inside)).astype(jnp.bfloat16)
-    corrected[0, 4 * HALF :] = (local[0, 4 * HALF :] + added[4 * HALF :]).astype(jnp.bfloat16)
-
-
-def scatter_kernel(received, out, total, staged):
+            _, both = flags(table, sub, which)
+            theirs = prolong(arrived_modes[which, other, half * both], picked[1 + which, other])
+            theirs = (0.5 * (rows + theirs)).astype(jnp.bfloat16).astype(jnp.float32)
+            own = local[0, start : start + HALF] + added[start : start + HALF]
+            own = (own * (1.0 - 0.5 * inside)).astype(jnp.bfloat16).astype(jnp.float32)
+            out[0, start : start + HALF] = (own + theirs * inside).astype(jnp.bfloat16)
+    out[0, 4 * HALF :] = (local[0, 4 * HALF :] + added[4 * HALF :]).astype(jnp.bfloat16)
+
+
+def scatter_kernel(table, received, out, total, staged):
     devices = received.shape[0]
     place = lax.broadcasted_iota(jnp.int32, (LANE, LANE), 0).astype(jnp.float32)
     total[...] = jnp.zeros_like(total)
@@ -162,13 +167,20 @@
 
     def copies(row, carry):
         for block in range(blocks):
-            out[row * blocks + block] = staged[block].astype(jnp.bfloat16)
+            device = row * blocks + block
+            out[device, :, :columns] = staged[block].astype(jnp.bfloat16)
+            shared = []
+            for which in range(2):
+                piece = received[jnp.bitwise_xor(device, table[which])].astype(jnp.float32)
+                at = 4 + 2 * which
+                shared.append(jnp.concatenate([piece[at : at + 1], piece[at + 1 : at + 2]], 1))
+            out[device, :, columns:] = jnp.concatenate(shared, 0).astype(jnp.bfloat16)
         return carry
 
     lax.fori_loop(0, devices // blocks, copies, 0)
 
 
-def gather_kernel(received, partial, out, solved):
+def gather_kernel(table, received, partial, out, solved, chosen_rows):
     devices, _, rows = partial.shape
     pieces = rows // LANE
     row_blocks = LANE // pieces
@@ -206,10 +218,22 @@
                 )
                 for case in range(2)
             ]
-            out[block * GROUP + inner] = jnp.concatenate(both, 0).astype(jnp.bfloat16)
+            chosen_rows[block * GROUP + inner] = jnp.concatenate(both, 0)
         return carry
 
     lax.fori_loop(0, devices // GROUP, step, 0)
+
+    def share(device, carry):
+        rows = [
+            chosen_rows[device],
+            chosen_rows[jnp.bitwise_xor(device, table[0])],
+            chosen_rows[jnp.bitwise_xor(device, table[1])],
+        ]
+        rows.append(jnp.zeros_like(rows[0]))
+        out[device] = jnp.concatenate(rows, 0).astype(jnp.bfloat16)
+        return carry
+
+    lax.fori_loop(0, devices, share, 0, unroll=4)
 
 
 def whole():
@@ -241,7 +265,18 @@
     table = table_of(neighbours, block_sizes, block_offsets)
     field = jax.ShapeDtypeStruct(residual.shape, jnp.bfloat16)
 
-    arrived = exchange(residual, table)
+    turned_modes = modes.transpose(0, 2, 1)
+    packed_spec = per_sub(2, HALF // 8, 2, 8, cases)
+    packed_shape = jax.ShapeDtypeStruct((count, 2, HALF // 8, 2, 8, cases), jnp.bfloat16)
+
+    packed = call(
+        pack_kernel,
+        packed_shape,
+        grid=(count,),
+        in_specs=[smem(), per_sub(trace_len, cases)],
+        out_specs=packed_spec,
+    )(table, residual)
+    arrived = exchange(packed, table)
     weighted, restricted = call(
         weigh_kernel,
         (field, jax.ShapeDtypeStruct((count, MODES, cases), jnp.bfloat16)),
@@ -249,65 +284,77 @@
         in_specs=[
             smem(),
             per_sub(trace_len, cases),
-            per_sub(trace_len, MODES),
+            per_sub(MODES, trace_len),
             same(*arrived.shape),
         ],
         out_specs=(per_sub(trace_len, cases), per_sub(MODES, cases)),
-    )(table, residual, modes, arrived)
-    local_part = jnp.einsum(
-        "sij,sjr->sir", interface_inverse, weighted, preferred_element_type=jnp.float32
-    )
+    )(table, residual, turned_modes, arrived)
 
     by_case = restricted.reshape(count * MODES, cases).T.reshape(devices, 2, count * MODES)
     digits = jnp.stack([coarse_map // LANE, coarse_map % LANE]).astype(jnp.bfloat16)
+    shared = turned_modes[:, :, : 4 * HALF].reshape(count, MODES, 2, 2, HALF)
+    second = table[4:12].reshape(count, 1, 2, 1) == 1
+    shared = jnp.stack(
+        [jnp.where(second, shared[:, :, :, 1], shared[:, :, :, 0]), shared[:, :, :, 1]], 3
+    ).reshape(devices, 4, HALF)
     received = spread(
-        jnp.concatenate([by_case, jnp.broadcast_to(digits[None], (devices,) + digits.shape)], 1)
-    )
+        jnp.concatenate(
+            [by_case, jnp.broadcast_to(digits[None], (devices,) + digits.shape), shared], 1
+        )
+    )
+    local_part, packed = call(
+        local_kernel,
+        (jax.ShapeDtypeStruct(residual.shape, jnp.float32), packed_shape),
+        grid=(count,),
+        in_specs=[smem(), per_sub(trace_len, trace_len), per_sub(trace_len, cases)],
+        out_specs=(per_sub(trace_len, cases), packed_spec),
+    )(table, interface_inverse, weighted)
+    arrived_local = exchange(packed, table)
+
     rows, columns = coarse_inverse.shape
     placed = call(
         scatter_kernel,
-        jax.ShapeDtypeStruct((devices, 2, columns), jnp.bfloat16),
-        in_specs=[whole()],
+        jax.ShapeDtypeStruct((devices, 2, columns + 2 * HALF), jnp.bfloat16),
+        in_specs=[smem(), whole()],
         out_specs=whole(),
         scratch_shapes=[
             pltpu.VMEM((2 * LANE, LANE), jnp.float32),
             pltpu.VMEM((LANE * LANE // columns, 2, columns), jnp.float32),
         ],
-    )(received)
-    coarse_rhs = spread(placed).reshape(cases, columns)
+    )(table, received)
+    placed = spread(placed)
+    coarse_rhs = placed[:, :, :columns].reshape(cases, columns)
+    arrived_modes = placed[:, :, columns:].reshape(count, MODES, 2, 2, HALF).transpose(2, 0, 3, 1, 4)
     partial_sum = lax.dot_general(
         coarse_rhs, coarse_inverse, (((1,), (1,)), ((), ())), preferred_element_type=jnp.float32
     ).astype(jnp.bfloat16)
     partial_sum = spread(partial_sum.reshape(devices, 2, rows))
     picked = call(
         gather_kernel,
-        jax.ShapeDtypeStruct((devices, 2, LANE), jnp.bfloat16),
-        in_specs=[whole(), whole()],
+        jax.ShapeDtypeStruct((devices, 8, LANE), jnp.bfloat16),
+        in_specs=[smem(), whole(), whole()],
         out_specs=whole(),
-        scratch_shapes=[pltpu.VMEM((2 * LANE, LANE), jnp.float32)],
-    )(received, partial_sum)
-    picked = spread(picked).reshape(cases, count * MODES).T.reshape(count, MODES, cases)
-
-    corrected = call(
-        correct_kernel,
+        scratch_shapes=[
+            pltpu.VMEM((2 * LANE, LANE), jnp.float32),
+            pltpu.VMEM((devices, 2, LANE), jnp.float32),
+        ],
+    )(table, received, partial_sum)
+    picked = spread(picked)[:, :6].reshape(devices, 3, 2, count * MODES).transpose(1, 3, 0, 2)
+    picked = picked.reshape(3, count, MODES, cases)
+    return call(
+        finish_kernel,
         field,
         grid=(count,),
         in_specs=[
             smem(),
             per_sub(trace_len, cases),
-            per_sub(trace_len, MODES),
-            per_sub(MODES, cases),
+            per_sub(MODES, trace_len),
+            same(*picked.shape),
+            same(*arrived_local.shape),
+            same(*arrived_modes.shape),
         ],
         out_specs=per_sub(trace_len, cases),
-    )(table, local_part, modes, picked)
-    arrived = exchange(corrected, table)
-    return call(
-        finish_kernel,
-        field,
-        grid=(count,),
-        in_specs=[smem(), per_sub(trace_len, cases), same(*arrived.shape)],
-        out_specs=per_sub(trace_len, cases),
-    )(table, corrected, arrived)
+    )(table, local_part, turned_modes, picked, arrived_local, arrived_modes)
 
 
 def solution(mesh):

time: 209 us -> 207 us (level)
  blocking collectives: 106 us -> 70.1 us
  waiting for transfers between devices: 37.8 us -> 59 us
  Pallas kernels: 19.7 us -> 29.2 us
  matrix products: 11.7 us -> 3.79 us
  local copies, waits for them, and re-layouts: 10 us -> 15.8 us
  starting transfers between devices: 21.8 us -> 24.6 us
  other arithmetic: 1.4 us -> 3.83 us
    all_to_all x5 -> x3, blocking collectives: 106 us -> 70.1 us  [spread(): return lax.all_to_all(value, AXES, 0, 0, tiled=True)]
    all_to_all x3 -> x5, waiting for transfers between devices: 37.8 us -> 59 us  [spread(): return lax.all_to_all(value, AXES, 0, 0, tiled=True)]
    dot_general x1 -> x0, matrix products: 8.26 us -> none  [shards(): jnp.einsum('sij,sjr->sir', interface_inverse, weighted, preferred_element...]
    pallas_call x3 -> x4, Pallas kernels: 13.2 us -> 20.4 us  [the longest x1 6.68 us: shards(): call(gather_kernel, jax.ShapeDtypeStruct((devices, 8, LANE), jnp.bfloat16...]
    unnamed x17 -> x16, local copies, waits for them, and re-layouts: 4.96 us -> 8.64 us
    all_to_all x3 -> x5, starting transfers between devices: 21.8 us -> 24.6 us  [spread(): return lax.all_to_all(value, AXES, 0, 0, tiled=True)]
  transfers between devices with their start and end apart: 3 -> 5, of which waited for: 3 -> 5; matrix products, arithmetic and copies ran while one was open for 4% -> 2% of each run, Pallas kernels for 0% -> 7%
where the time goes in v2:
time: 207 us; the launch traced here: 206 us
  blocking collectives  70.1 us (34%)
  waiting for transfers between devices  59 us (29%)
  Pallas kernels  29.2 us (14%)
  starting transfers between devices  24.6 us (12%)
  local copies, waits for them, and re-layouts  15.8 us (8%)
  other arithmetic  3.83 us (2%)
  matrix products  3.79 us (2%)
    all_to_all x3, blocking collectives, spread(): return lax.all_to_all(value, AXES, 0, 0, tiled=True)  70.1 us
    all_to_all x5, waiting for transfers between devices, spread(): return lax.all_to_all(value, AXES, 0, 0, tiled=True)  59 us
    all_to_all x5, starting transfers between devices, spread(): return lax.all_to_all(value, AXES, 0, 0, tiled=True)  24.6 us
    unnamed x16, local copies, waits for them, and re-layouts  8.64 us
    pallas_call x1, Pallas kernels, shards(): call(gather_kernel, jax.ShapeDtypeStruct((devices, 8, LANE), jnp.bfloat16...  6.68 us
    pallas_call x1, Pallas kernels, shards(): call(scatter_kernel, jax.ShapeDtypeStruct((devices, 2, columns + 2 * HALF...  6.57 us
    pallas_call x1, Pallas kernels, shards(): call(local_kernel, (jax.ShapeDtypeStruct(residual.shape, jnp.float32), pa...  6.47 us
  transfers between devices with their start and end apart: 5, of which 5 were waited for; matrix products, arithmetic and copies ran while one was open for 2% of the time, Pallas kernels for 7%

profile of v2, /device:TPU:1, one launch (start us, length us, event | category | flops | bytes accessed | tf_op | source)
XLA Modules:
  0.0 206.4 jit_solution(10309700489084481696)
XLA Ops:
  0.0 0.8 slice_reduce_fusion
  2.6 1.6 copy-done
  5.0 30.2 %all_to_all.40.chunks = bf16[128,2,8,256]{3,2,1,0:T(8,128)(2,1)S(1)} all-to-all(bf16[128,2,8,256]{3,2,1,0:T(8,128)(2,1)S(1)} %bitcast.27), channel_id=1, replica_groups=mesh['row'=16,'col'=8] {'row','col'}, dimensions={0} | all-to-all | bytes 2097152 | tf_op jit(solution)/shard_map/all_to_all | solution.py:17
  35.2 1.9 shard_map.83
  37.0 4.7 %all-to-all-start.1 = ((bf16[128,2,8,256]{3,2,1,0:T(8,128)(2,1)}), bf16[128,2,8,256]{3,2,1,0:T(8,128)(2,1)S(1)}, u32[]{:S(2)}, u32[]{:S(2)}) async-start(bf16[128,2,8,256]{3,2,1,0:T(8,128)(2,1)} %shard_map.83), calls=%async_computation.1 | async-start | bytes 2097152 | tf_op jit(solution)/shard_map/all_to_all | solution.py:17
  42.5 0.9 reshape.72
  43.7 0.9 pad_maximum_fusion.1
  44.7 16.1 %all-to-all-done.1 = bf16[128,2,8,256]{3,2,1,0:T(8,128)(2,1)S(1)} async-done(((bf16[128,2,8,256]{3,2,1,0:T(8,128)(2,1)}), bf16[128,2,8,256]{3,2,1,0:T(8,128)(2,1)S(1)}, u32[]{:S(2)}, u32[]{:S(2)}) %all-to-all-start.1) | async-done | bytes 1048608 | tf_op jit(solution)/shard_map/all_to_all | solution.py:17
  60.7 1.5 shard_map.84
  62.3 1.3 copy-done.4
  63.8 1.1 pad_maximum_fusion
  64.9 15.5 %all_to_all.41.received = bf16[128,8,128]{2,1,0:T(8,128)(2,1)S(1)} all-to-all(bf16[128,8,128]{2,1,0:T(8,128)(2,1)S(1)} %pad_maximum_fusion), channel_id=1, replica_groups=mesh['row'=16,'col'=8] {'row','col'}, dimensions={0} | all-to-all | bytes 524288 | tf_op jit(solution)/shard_map/all_to_all | solution.py:17
  80.4 6.6 %shard_map.86 = bf16[128,2,2304]{2,1,0:T(2,128)(2,1)S(1)} custom-call(s32[20]{0:T(128)S(1)} %pad_add_fusion.table, bf16[128,8,128]{2,1,0:T(8,128)(2,1)S(1)} %all_to_all.41.received), custom_call_target="tpu_custom_call" | custom-call | tf_op jit(solution)/shard_map/pallas_call | solution.py:315
  87.0 24.4 %all_to_all.42 = bf16[128,2,2304]{2,1,0:T(2,128)(2,1)S(1)} all-to-all(bf16[128,2,2304]{2,1,0:T(2,128)(2,1)S(1)} %shard_map.86), channel_id=1, replica_groups=mesh['row'=16,'col'=8] {'row','col'}, dimensions={0} | all-to-all | bytes 2359296 | tf_op jit(solution)/shard_map/all_to_all | solution.py:17
  112.1 1.2 reshape.74
  113.3 3.8 %convolution_convert_fusion = bf16[256,1024]{1,0:T(8,128)(2,1)S(1)} fusion(bf16[256,2048]{1,0:T(8,128)(2,1)} %reshape.74, bf16[1024,2048]{1,0:T(8,128)(2,1)} %param.12), kind=kOutput, calls=%fused_computation | convolution fusion | flops 1074003968 | bytes 5767168 | tf_op jit(solution)/shard_map/dot_general | solution.py:328
  117.1 1.0 reshape.75
  118.1 4.7 %all-to-all-start.4 = ((bf16[128,2,1024]{2,1,0:T(2,128)(2,1)}), bf16[128,2,1024]{2,1,0:T(2,128)(2,1)S(1)}, u32[]{:S(2)}, u32[]{:S(2)}) async-start(bf16[128,2,1024]{2,1,0:T(2,128)(2,1)} %reshape.75), calls=%async_computation.4 | async-start | bytes 1048576 | tf_op jit(solution)/shard_map/all_to_all | solution.py:17
  122.8 1.6 copy-done.5
  124.4 6.5 %shard_map.85 = (f32[4,1024,256]{2,1,0:T(8,128)S(1)}, bf16[4,2,16,2,8,256]{5,4,3,2,1,0:T(8,128)(2,1)}) custom-call(s32[20]{0:T(128)S(1)} %pad_add_fusion.table, bf16[4,1024,1024]{2,1,0:T(8,128)(2,1)} %inverse.1, bf16[4,1024,256]{2,1,0:T(8,128)(2,1)S(1)} %copy-done.5), custom_call_target="tpu_custom_call" | custom-call | tf_op jit(solution)/shard_map/pallas_call | solution.py:305
  130.9 1.9 copy-done.2
  132.8 3.6 %all-to-all-done.4.partial = bf16[128,2,1024]{2,1,0:T(2,128)(2,1)S(1)} async-done(((bf16[128,2,1024]{2,1,0:T(2,128)(2,1)}), bf16[128,2,1024]{2,1,0:T(2,128)(2,1)S(1)}, u32[]{:S(2)}, u32[]{:S(2)}) %all-to-all-start.4) | async-done | bytes 524320 | tf_op jit(solution)/shard_map/all_to_all | solution.py:17
  136.4 6.3 %all-to-all-start.6 = ((bf16[128,2,8,256]{3,2,1,0:T(8,128)(2,1)}), bf16[128,2,8,256]{3,2,1,0:T(8,128)(2,1)S(1)}, u32[]{:S(2)}, u32[]{:S(2)}) async-start(bf16[128,2,8,256]{3,2,1,0:T(8,128)(2,1)} %bitcast.11), calls=%async_computation.6 | async-start | bytes 2097152 | tf_op jit(solution)/shard_map/all_to_all | solution.py:17
  142.7 6.7 %shard_map.87 = bf16[128,8,128]{2,1,0:T(8,128)(2,1)} custom-call(s32[20]{0:T(128)S(1)} %pad_add_fusion.table, bf16[128,8,128]{2,1,0:T(8,128)(2,1)S(1)} %all_to_all.41.received, bf16[128,2,1024]{2,1,0:T(2,128)(2,1)S(1)} %all-to-all-done.4.partial), custom_call_target="tpu_custom_call" | custom-call | tf_op jit(solution)/shard_map/pallas_call | solution.py:332
  149.4 12.2 %all-to-all-done.6.chunks = bf16[128,2,8,256]{3,2,1,0:T(8,128)(2,1)S(1)} async-done(((bf16[128,2,8,256]{3,2,1,0:T(8,128)(2,1)}), bf16[128,2,8,256]{3,2,1,0:T(8,128)(2,1)S(1)}, u32[]{:S(2)}, u32[]{:S(2)}) %all-to-all-start.6) | async-done | bytes 1048608 | tf_op jit(solution)/shard_map/all_to_all | solution.py:17
  161.6 4.7 %all-to-all-start.5 = ((bf16[128,8,128]{2,1,0:T(8,128)(2,1)}), bf16[128,8,128]{2,1,0:T(8,128)(2,1)S(1)}, u32[]{:S(2)}, u32[]{:S(2)}) async-start(bf16[128,8,128]{2,1,0:T(8,128)(2,1)} %shard_map.87), calls=%async_computation.5 | async-start | bytes 524288 | tf_op jit(solution)/shard_map/all_to_all | solution.py:17
  166.3 1.9 shard_map.88
  168.1 9.4 %all-to-all-done.5 = bf16[128,8,128]{2,1,0:T(8,128)(2,1)S(1)} async-done(((bf16[128,8,128]{2,1,0:T(8,128)(2,1)}), bf16[128,8,128]{2,1,0:T(8,128)(2,1)S(1)}, u32[]{:S(2)}, u32[]{:S(2)}) %all-to-all-start.5) | async-done | bytes 262176 | tf_op jit(solution)/shard_map/all_to_all | solution.py:17
  177.5 4.3 %all-to-all-start.7 = ((bf16[128,2,8,256]{3,2,1,0:T(8,128)(2,1)}), bf16[128,2,8,256]{3,2,1,0:T(8,128)(2,1)S(1)}, u32[]{:S(2)}, u32[]{:S(2)}) async-start(bf16[128,2,8,256]{3,2,1,0:T(8,128)(2,1)} %shard_map.88), calls=%async_computation.7 | async-start | bytes 2097152 | tf_op jit(solution)/shard_map/all_to_all | solution.py:17
  183.1 17.7 %all-to-all-done.7 = bf16[128,2,8,256]{3,2,1,0:T(8,128)(2,1)S(1)} async-done(((bf16[128,2,8,256]{3,2,1,0:T(8,128)(2,1)}), bf16[128,2,8,256]{3,2,1,0:T(8,128)(2,1)S(1)}, u32[]{:S(2)}, u32[]{:S(2)}) %all-to-all-start.7) | async-done | bytes 1048608 | tf_op jit(solution)/shard_map/all_to_all | solution.py:17
  200.7 2.2 %copy-done.3 = f32[4,1024,256]{2,1,0:T(8,128)S(1)} copy-done((f32[4,1024,256]{2,1,0:T(8,128)S(1)}, f32[4,1024,256]{2,1,0:T(8,128)}, u32[]{:S(2)}) %copy-start.3) | copy-done | bytes 4194328
  202.9 3.5 %shard_map.89 = bf16[4,1024,256]{2,1,0:T(8,128)(2,1)} custom-call(s32[20]{0:T(128)S(1)} %pad_add_fusion.table, f32[4,1024,256]{2,1,0:T(8,128)S(1)} %copy-done.3, bf16[4,32,1024]{2,1,0:T(8,128)(2,1)S(1)} %bitcast.30, bf16[3,4,32,256]{3,2,1,0:T(8,128)(2,1)S(1)} %copy.22.picked, bf16[4,2,16,2,8,256]{5,4,3,2,1,0:T(8,128)(2,1)S(1)} %bitcast.25, ...), custom_call_target="tpu_custom_call" | custom-call | tf_op jit(solution)/shard_map/pallas_call | solution.py:344
  (35 shorter events, 5.7 us)
Async XLA Ops:
  2.6 1.6 copy-start
  4.2 37.6 %copy-start.6 = (bf16[4,1024,32]{1,2,0:T(8,128)(2,1)S(1)}, bf16[4,1024,32]{1,2,0:T(8,128)(2,1)}, u32[]{:S(2)}) copy-start(bf16[4,1024,32]{1,2,0:T(8,128)(2,1)} %param.10) | copy-start | bytes 786436
  4.9 38.5 %copy-start.7 = (s32[128]{0:T(128)S(1)}, s32[128]{0:T(128)}, u32[]{:S(2)}) copy-start(s32[128]{0:T(128)} %param.11) | copy-start | bytes 1540
  4.9 55.8 %copy-start.1 = (bf16[4,1024,256]{2,1,0:T(8,128)(2,1)S(1)}, bf16[4,1024,256]{2,1,0:T(8,128)(2,1)}, u32[]{:S(2)}) copy-start(bf16[4,1024,256]{2,1,0:T(8,128)(2,1)} %residual.1) | copy-start | bytes 6291460
  37.0 23.7 %all-to-all-start.1 = ((bf16[128,2,8,256]{3,2,1,0:T(8,128)(2,1)}), bf16[128,2,8,256]{3,2,1,0:T(8,128)(2,1)S(1)}, u32[]{:S(2)}, u32[]{:S(2)}) async-start(bf16[128,2,8,256]{3,2,1,0:T(8,128)(2,1)} %shard_map.83), calls=%async_computation.1 | async-start | bytes 2097152 | tf_op jit(solution)/shard_map/all_to_all | solution.py:17
  62.3 1.3 copy-start.4
  118.1 18.3 %all-to-all-start.4 = ((bf16[128,2,1024]{2,1,0:T(2,128)(2,1)}), bf16[128,2,1024]{2,1,0:T(2,128)(2,1)S(1)}, u32[]{:S(2)}, u32[]{:S(2)}) async-start(bf16[128,2,1024]{2,1,0:T(2,128)(2,1)} %reshape.75), calls=%async_computation.4 | async-start | bytes 1048576 | tf_op jit(solution)/shard_map/all_to_all | solution.py:17
  122.8 1.6 copy-start.5
  130.9 1.9 copy-start.2
  136.4 25.2 %all-to-all-start.6 = ((bf16[128,2,8,256]{3,2,1,0:T(8,128)(2,1)}), bf16[128,2,8,256]{3,2,1,0:T(8,128)(2,1)S(1)}, u32[]{:S(2)}, u32[]{:S(2)}) async-start(bf16[128,2,8,256]{3,2,1,0:T(8,128)(2,1)} %bitcast.11), calls=%async_computation.6 | async-start | bytes 2097152 | tf_op jit(solution)/shard_map/all_to_all | solution.py:17
  161.6 15.9 %all-to-all-start.5 = ((bf16[128,8,128]{2,1,0:T(8,128)(2,1)}), bf16[128,8,128]{2,1,0:T(8,128)(2,1)S(1)}, u32[]{:S(2)}, u32[]{:S(2)}) async-start(bf16[128,8,128]{2,1,0:T(8,128)(2,1)} %shard_map.87), calls=%async_computation.5 | async-start | bytes 524288 | tf_op jit(solution)/shard_map/all_to_all | solution.py:17
  177.5 23.2 %all-to-all-start.7 = ((bf16[128,2,8,256]{3,2,1,0:T(8,128)(2,1)}), bf16[128,2,8,256]{3,2,1,0:T(8,128)(2,1)S(1)}, u32[]{:S(2)}, u32[]{:S(2)}) async-start(bf16[128,2,8,256]{3,2,1,0:T(8,128)(2,1)} %shard_map.88), calls=%async_computation.7 | async-start | bytes 2097152 | tf_op jit(solution)/shard_map/all_to_all | solution.py:17
  200.7 2.2 %copy-start.3 = (f32[4,1024,256]{2,1,0:T(8,128)S(1)}, f32[4,1024,256]{2,1,0:T(8,128)}, u32[]{:S(2)}) copy-start(f32[4,1024,256]{2,1,0:T(8,128)} %copy-done.2) | copy-start | bytes 12582916

commit v3 on v2

--- a/solution.py
+++ b/solution.py
@@ -1,3 +1,5 @@
+import functools
+
 import jax
 import jax.numpy as jnp
 from jax import lax
@@ -46,22 +48,22 @@
     return table[4 + sub * 2 + which], table[12 + sub * 2 + which]
 
 
-def store_blocks(table, sub, load, packed):
+def store_blocks(offsets, sub, load, packed):
     for which in range(2):
-        second, _ = flags(table, sub, which)
+        second = jnp.bitwise_and(jnp.right_shift(offsets[which, sub], 7), 1)
         for half in range(2):
             start = which * 2 * HALF + (second * HALF if half == 0 else HALF)
             rows = load(pl.multiple_of(start, HALF)).astype(jnp.float32)
             packed[0, half, :, which] = rows.reshape(HALF // 8, 8, rows.shape[-1]).astype(jnp.bfloat16)
 
 
-def pack_kernel(table, field, packed):
-    store_blocks(table, pl.program_id(0), lambda start: field[0, pl.ds(start, HALF)], packed)
-
-
-def local_kernel(table, inverse, weighted, local, packed):
+def pack_kernel(offsets, field, packed):
+    store_blocks(offsets, pl.program_id(0), lambda start: field[0, pl.ds(start, HALF)], packed)
+
+
+def local_kernel(offsets, inverse, weighted, local, packed):
     local[0] = jnp.dot(inverse[0], weighted[0], preferred_element_type=jnp.float32)
-    store_blocks(table, pl.program_id(0), lambda start: local[0, pl.ds(start, HALF)], packed)
+    store_blocks(offsets, pl.program_id(0), lambda start: local[0, pl.ds(start, HALF)], packed)
 
 
 def reroute_kernel(table, chunks, out):
@@ -131,7 +133,7 @@
     out[0, 4 * HALF :] = (local[0, 4 * HALF :] + added[4 * HALF :]).astype(jnp.bfloat16)
 
 
-def scatter_kernel(table, received, out, total, staged):
+def scatter_kernel(table, received, packed, out, total, staged):
     devices = received.shape[0]
     place = lax.broadcasted_iota(jnp.int32, (LANE, LANE), 0).astype(jnp.float32)
     total[...] = jnp.zeros_like(total)
@@ -165,30 +167,55 @@
                 at = case * LANE + block * pieces + piece
                 staged[block, case : case + 1, piece * LANE : (piece + 1) * LANE] = total[at : at + 1]
 
-    def copies(row, carry):
-        for block in range(blocks):
-            device = row * blocks + block
-            out[device, :, :columns] = staged[block].astype(jnp.bfloat16)
-            shared = []
-            for which in range(2):
-                piece = received[jnp.bitwise_xor(device, table[which])].astype(jnp.float32)
-                at = 4 + 2 * which
-                shared.append(jnp.concatenate([piece[at : at + 1], piece[at + 1 : at + 2]], 1))
-            out[device, :, columns:] = jnp.concatenate(shared, 0).astype(jnp.bfloat16)
-        return carry
-
-    lax.fori_loop(0, devices // blocks, copies, 0)
-
-
-def gather_kernel(table, received, partial, out, solved, chosen_rows):
-    devices, _, rows = partial.shape
-    pieces = rows // LANE
-    row_blocks = LANE // pieces
+    for block in range(blocks):
+        value = staged[block].astype(jnp.bfloat16)
+
+        def copies(row, carry, block=block, value=value):
+            out[row * blocks + block, :, :columns] = value
+            return carry
+
+        lax.fori_loop(0, devices // blocks, copies, 0, unroll=4)
+
+    local_at = columns + 2 * HALF
+
+    def forward(device, carry):
+        shared = []
+        for which in range(2):
+            piece = received[jnp.bitwise_xor(device, table[which])].astype(jnp.float32)
+            at = 4 + 2 * which
+            shared.append(jnp.concatenate([piece[at : at + 1], piece[at + 1 : at + 2]], 1))
+        out[device, :, columns:local_at] = jnp.concatenate(shared, 0).astype(jnp.bfloat16)
+        out[device, :, local_at:] = packed[device]
+        return carry
+
+    lax.fori_loop(0, devices, forward, 0, unroll=4)
+
+
+def join_kernel(table, partial, merged, out):
+    rows = partial.shape[-1]
+    size = (out.shape[-1] - rows) // 2
+    base = merged.shape[-1] - 2 * size
+
+    def step(device, carry):
+        out[device, :, :rows] = partial[device]
+        for which in range(2):
+            out[device, :, rows + which * size : rows + (which + 1) * size] = merged[
+                jnp.bitwise_xor(device, table[which]), :, base + which * size : base + (which + 1) * size
+            ]
+        return carry
+
+    lax.fori_loop(0, partial.shape[0], step, 0, unroll=4)
+
+
+def gather_kernel(table, received, partial, out, solved, chosen_rows, *, row_blocks):
+    devices, _, _ = partial.shape
+    pieces = LANE // row_blocks
+    rows = pieces * LANE
     col_blocks = devices // row_blocks
     for block in range(row_blocks):
-        value = partial[block * col_blocks].astype(jnp.float32)
+        value = partial[block * col_blocks, :, :rows].astype(jnp.float32)
         for col in range(1, col_blocks):
-            value = value + partial[block * col_blocks + col].astype(jnp.float32)
+            value = value + partial[block * col_blocks + col, :, :rows].astype(jnp.float32)
         for piece in range(pieces):
             for case in range(2):
                 at = case * LANE + block * pieces + piece
@@ -266,6 +293,7 @@
     field = jax.ShapeDtypeStruct(residual.shape, jnp.bfloat16)
 
     turned_modes = modes.transpose(0, 2, 1)
+    offsets = block_offsets.T
     packed_spec = per_sub(2, HALF // 8, 2, 8, cases)
     packed_shape = jax.ShapeDtypeStruct((count, 2, HALF // 8, 2, 8, cases), jnp.bfloat16)
 
@@ -275,7 +303,7 @@
         grid=(count,),
         in_specs=[smem(), per_sub(trace_len, cases)],
         out_specs=packed_spec,
-    )(table, residual)
+    )(offsets, residual)
     arrived = exchange(packed, table)
     weighted, restricted = call(
         weigh_kernel,
@@ -308,29 +336,38 @@
         grid=(count,),
         in_specs=[smem(), per_sub(trace_len, trace_len), per_sub(trace_len, cases)],
         out_specs=(per_sub(trace_len, cases), packed_spec),
-    )(table, interface_inverse, weighted)
-    arrived_local = exchange(packed, table)
+    )(offsets, interface_inverse, weighted)
+    lanes = 2 * 4 * cases
+    packed = packed.reshape(devices, 2, 4, 2, cases).transpose(0, 3, 1, 2, 4).reshape(devices, 2, lanes)
 
     rows, columns = coarse_inverse.shape
     placed = call(
         scatter_kernel,
-        jax.ShapeDtypeStruct((devices, 2, columns + 2 * HALF), jnp.bfloat16),
-        in_specs=[smem(), whole()],
+        jax.ShapeDtypeStruct((devices, 2, columns + 2 * HALF + lanes), jnp.bfloat16),
+        in_specs=[smem(), whole(), whole()],
         out_specs=whole(),
         scratch_shapes=[
             pltpu.VMEM((2 * LANE, LANE), jnp.float32),
             pltpu.VMEM((LANE * LANE // columns, 2, columns), jnp.float32),
         ],
-    )(table, received)
+    )(table, received, packed)
     placed = spread(placed)
     coarse_rhs = placed[:, :, :columns].reshape(cases, columns)
-    arrived_modes = placed[:, :, columns:].reshape(count, MODES, 2, 2, HALF).transpose(2, 0, 3, 1, 4)
+    arrived_modes = placed[:, :, columns : columns + 2 * HALF].reshape(count, MODES, 2, 2, HALF).transpose(2, 0, 3, 1, 4)
     partial_sum = lax.dot_general(
         coarse_rhs, coarse_inverse, (((1,), (1,)), ((), ())), preferred_element_type=jnp.float32
     ).astype(jnp.bfloat16)
-    partial_sum = spread(partial_sum.reshape(devices, 2, rows))
+    joined = call(
+        join_kernel,
+        jax.ShapeDtypeStruct((devices, 2, rows + lanes), jnp.bfloat16),
+        in_specs=[smem(), whole(), whole()],
+        out_specs=whole(),
+    )(table, partial_sum.reshape(devices, 2, rows), placed)
+    joined = spread(joined)
+    arrived_local = joined[:, :, rows:].reshape(devices, 2, 2, 4, cases).transpose(0, 2, 3, 1, 4)
+    arrived_local = arrived_local.reshape(packed_shape.shape)
     picked = call(
-        gather_kernel,
+        functools.partial(gather_kernel, row_blocks=lax.axis_size("row")),
         jax.ShapeDtypeStruct((devices, 8, LANE), jnp.bfloat16),
         in_specs=[smem(), whole(), whole()],
         out_specs=whole(),
@@ -338,7 +375,7 @@
             pltpu.VMEM((2 * LANE, LANE), jnp.float32),
             pltpu.VMEM((devices, 2, LANE), jnp.float32),
         ],
-    )(table, received, partial_sum)
+    )(table, received, joined)
     picked = spread(picked)[:, :6].reshape(devices, 3, 2, count * MODES).transpose(1, 3, 0, 2)
     picked = picked.reshape(3, count, MODES, cases)
     return call(

time: 207 us -> 202 us (0.976)
  waiting for transfers between devices: 59 us -> 41.3 us
  local copies, waits for them, and re-layouts: 15.8 us -> 26 us
    all_to_all x5 -> x4, waiting for transfers between devices: 59 us -> 41.3 us  [spread(): return lax.all_to_all(value, AXES, 0, 0, tiled=True)]
    reshape x3 -> x7, local copies, waits for them, and re-layouts: 1.11 us -> 5.97 us  [the longest x3 3.28 us: shards(): packed.reshape(devices, 2, 4, 2, cases).transpose(0, 3, 1, 2, 4)]
    all_to_all x5 -> x4, starting transfers between devices: 24.6 us -> 26.6 us  [spread(): return lax.all_to_all(value, AXES, 0, 0, tiled=True)]
    unnamed x16 -> x26, local copies, waits for them, and re-layouts: 8.64 us -> 10.4 us
    pallas_call x1 -> x2, Pallas kernels: 6.68 us -> 7.66 us  [the longest x1 6.66 us: shards(): call(functools.partial(gather_kernel, row_blocks=lax.axis_size('row')), j...]
    all_to_all x3 -> x2, blocking collectives: 70.1 us -> 70 us  [spread(): return lax.all_to_all(value, AXES, 0, 0, tiled=True)]
  transfers between devices with their start and end apart: 5 -> 4, of which waited for: 5 -> 3; matrix products, arithmetic and copies ran while one was open for 2% -> 5% of each run, Pallas kernels for 7% -> 3%
where the time goes in v3:
time: 202 us
  blocking collectives  70 us (35%)
  waiting for transfers between devices  41.3 us (20%)
  Pallas kernels  28.6 us (14%)
  starting transfers between devices  26.6 us (13%)
  local copies, waits for them, and re-layouts  26 us (13%)
  matrix products  4.59 us (2%)
  other arithmetic  4.18 us (2%)
    all_to_all x2, blocking collectives, spread(): return lax.all_to_all(value, AXES, 0, 0, tiled=True)  70 us
    all_to_all x4, waiting for transfers between devices, spread(): return lax.all_to_all(value, AXES, 0, 0, tiled=True)  41.3 us
    all_to_all x4, starting transfers between devices, spread(): return lax.all_to_all(value, AXES, 0, 0, tiled=True)  26.6 us
    unnamed x26, local copies, waits for them, and re-layouts  10.4 us
    pallas_call x1, Pallas kernels, shards(): call(functools.partial(gather_kernel, row_blocks=lax.axis_size('row')), j...  6.66 us
    pallas_call x1, Pallas kernels, shards(): call(scatter_kernel, jax.ShapeDtypeStruct((devices, 2, columns + 2 * HALF...  6.32 us
    pallas_call x1, Pallas kernels, shards(): call(local_kernel, (jax.ShapeDtypeStruct(residual.shape, jnp.float32), pa...  5.58 us
    dot_general x1, matrix products, shards(): lax.dot_general(coarse_rhs, coarse_inverse, (((1,), (1,)), ((), ())), pre...  4.59 us
  transfers between devices with their start and end apart: 4, of which 3 were waited for; matrix products, arithmetic and copies ran while one was open for 5% of the time, Pallas kernels for 3%

profile of v3, /device:TPU:1, one launch (start us, length us, event | category | flops | bytes accessed | tf_op | source)
XLA Modules:
  0.0 201.6 jit_solution(17386885933897570882)
XLA Ops:
  0.0 1.6 copy-done.1
  2.3 2.1 %shard_map.82 = bf16[4,2,16,2,8,256]{5,4,3,2,1,0:T(8,128)(2,1)} custom-call(s32[2,4]{1,0:T(2,128)S(1)} %bitcast.39, bf16[4,1024,256]{2,1,0:T(8,128)(2,1)S(1)} %copy-done.1), custom_call_target="tpu_custom_call" | custom-call | tf_op jit(solution)/shard_map/pallas_call | solution.py:300
  4.4 11.5 %all-to-all-start = ((bf16[128,2,8,256]{3,2,1,0:T(8,128)(2,1)}), bf16[128,2,8,256]{3,2,1,0:T(8,128)(2,1)S(1)}, u32[]{:S(2)}, u32[]{:S(2)}) async-start(bf16[128,2,8,256]{3,2,1,0:T(8,128)(2,1)} %bitcast.2), calls=%async_computation | async-start | bytes 2097152 | tf_op jit(solution)/shard_map/all_to_all | solution.py:19
  16.5 18.3 %all-to-all-done.chunks = bf16[128,2,8,256]{3,2,1,0:T(8,128)(2,1)S(1)} async-done(((bf16[128,2,8,256]{3,2,1,0:T(8,128)(2,1)}), bf16[128,2,8,256]{3,2,1,0:T(8,128)(2,1)S(1)}, u32[]{:S(2)}, u32[]{:S(2)}) %all-to-all-start) | async-done | bytes 1048608 | tf_op jit(solution)/shard_map/all_to_all | solution.py:19
  34.8 1.9 shard_map.83
  36.6 4.8 %all-to-all-start.1 = ((bf16[128,2,8,256]{3,2,1,0:T(8,128)(2,1)}), bf16[128,2,8,256]{3,2,1,0:T(8,128)(2,1)S(1)}, u32[]{:S(2)}, u32[]{:S(2)}) async-start(bf16[128,2,8,256]{3,2,1,0:T(8,128)(2,1)} %shard_map.83), calls=%async_computation.1 | async-start | bytes 2097152 | tf_op jit(solution)/shard_map/all_to_all | solution.py:19
  42.2 1.6 reshape.78
  43.9 1.3 broadcast_select_fusion
  46.1 14.5 %all-to-all-done.1 = bf16[128,2,8,256]{3,2,1,0:T(8,128)(2,1)S(1)} async-done(((bf16[128,2,8,256]{3,2,1,0:T(8,128)(2,1)}), bf16[128,2,8,256]{3,2,1,0:T(8,128)(2,1)S(1)}, u32[]{:S(2)}, u32[]{:S(2)}) %all-to-all-start.1) | async-done | bytes 1048608 | tf_op jit(solution)/shard_map/all_to_all | solution.py:19
  60.5 1.5 shard_map.84
  62.1 1.3 copy-done.5
  63.5 1.8 pad_maximum_fusion
  65.4 4.6 %all-to-all-start.2 = ((bf16[128,8,128]{2,1,0:T(8,128)(2,1)}), bf16[128,8,128]{2,1,0:T(8,128)(2,1)S(1)}, u32[]{:S(2)}, u32[]{:S(2)}) async-start(bf16[128,8,128]{2,1,0:T(8,128)(2,1)} %pad_maximum_fusion), calls=%async_computation.2 | async-start | bytes 524288 | tf_op jit(solution)/shard_map/all_to_all | solution.py:19
  70.0 1.6 copy-done.6
  71.6 5.6 %shard_map.85 = (f32[4,1024,256]{2,1,0:T(8,128)S(1)}, bf16[4,2,16,2,8,256]{5,4,3,2,1,0:T(8,128)(2,1)S(1)}) custom-call(s32[2,4]{1,0:T(2,128)S(1)} %bitcast.40, bf16[4,1024,1024]{2,1,0:T(8,128)(2,1)} %inverse.1, bf16[4,1024,256]{2,1,0:T(8,128)(2,1)S(1)} %copy-done.6), custom_call_target="tpu_custom_call" | custom-call | tf_op jit(solution)/shard_map/pallas_call | solution.py:333
  77.2 1.9 copy-done.3
  79.6 1.4 copy.31
  81.0 1.5 reshape.81.packed
  82.4 6.3 %shard_map.86 = bf16[128,2,4352]{2,1,0:T(2,128)(2,1)S(1)} custom-call(s32[20]{0:T(128)S(1)} %pad_add_fusion.table, bf16[128,8,128]{2,1,0:T(8,128)(2,1)S(1)} %all-to-all-done.2.received, bf16[128,2,2048]{2,1,0:T(2,128)(2,1)S(1)} %reshape.81.packed), custom_call_target="tpu_custom_call" | custom-call | tf_op jit(solution)/shard_map/pallas_call | solution.py:344
  88.8 41.6 %all_to_all.30.merged = bf16[128,2,4352]{2,1,0:T(2,128)(2,1)S(1)} all-to-all(bf16[128,2,4352]{2,1,0:T(2,128)(2,1)S(1)} %shard_map.86), channel_id=1, replica_groups=mesh['row'=16,'col'=8] {'row','col'}, dimensions={0} | all-to-all | bytes 4456448 | tf_op jit(solution)/shard_map/all_to_all | solution.py:19
  130.4 1.7 slice.37
  132.1 2.3 %reshape.82 = bf16[256,2048]{1,0:T(8,128)(2,1)} reshape(bf16[128,2,2048]{2,1,0:T(2,128)(2,1)} %slice.37) | data formatting | bytes 2097152 | tf_op jit(solution)/shard_map/reshape | solution.py:355
  134.3 4.6 %convolution_convert_fusion = bf16[256,1024]{1,0:T(8,128)(2,1)} fusion(bf16[256,2048]{1,0:T(8,128)(2,1)} %reshape.82, bf16[1024,2048]{1,0:T(8,128)(2,1)} %param.12), kind=kOutput, calls=%fused_computation | convolution fusion | flops 1074003968 | bytes 5767168 | tf_op jit(solution)/shard_map/dot_general | solution.py:357
  138.9 1.2 reshape.83.partial
  140.2 1.0 shard_map.87
  141.2 28.4 %all_to_all.31.partial = bf16[128,2,3072]{2,1,0:T(2,128)(2,1)S(1)} all-to-all(bf16[128,2,3072]{2,1,0:T(2,128)(2,1)S(1)} %shard_map.87), channel_id=1, replica_groups=mesh['row'=16,'col'=8] {'row','col'}, dimensions={0} | all-to-all | bytes 3145728 | tf_op jit(solution)/shard_map/all_to_all | solution.py:19
  169.6 6.7 %shard_map.88 = bf16[128,8,128]{2,1,0:T(8,128)(2,1)} custom-call(s32[20]{0:T(128)S(1)} %pad_add_fusion.table, bf16[128,8,128]{2,1,0:T(8,128)(2,1)S(1)} %all-to-all-done.2.received, bf16[128,2,3072]{2,1,0:T(2,128)(2,1)S(1)} %all_to_all.31.partial), custom_call_target="tpu_custom_call" | custom-call | tf_op jit(solution)/shard_map/pallas_call | solution.py:369
  176.2 1.1 copy-done
  177.4 5.7 %all-to-all-start.5 = ((bf16[128,8,128]{2,1,0:T(8,128)(2,1)}), bf16[128,8,128]{2,1,0:T(8,128)(2,1)}, u32[]{:S(2)}, u32[]{:S(2)}) async-start(bf16[128,8,128]{2,1,0:T(8,128)(2,1)} %shard_map.88), calls=%async_computation.5 | async-start | bytes 524288 | tf_op jit(solution)/shard_map/all_to_all | solution.py:19
  185.3 8.6 %all-to-all-done.5 = bf16[128,8,128]{2,1,0:T(8,128)(2,1)} async-done(((bf16[128,8,128]{2,1,0:T(8,128)(2,1)}), bf16[128,8,128]{2,1,0:T(8,128)(2,1)}, u32[]{:S(2)}, u32[]{:S(2)}) %all-to-all-start.5) | async-done | bytes 262176 | tf_op jit(solution)/shard_map/all_to_all | solution.py:19
  195.9 2.2 %copy-done.4 = f32[4,1024,256]{2,1,0:T(8,128)S(1)} copy-done((f32[4,1024,256]{2,1,0:T(8,128)S(1)}, f32[4,1024,256]{2,1,0:T(8,128)}, u32[]{:S(2)}) %copy-start.4) | copy-done | bytes 4194328
  198.1 3.5 %shard_map.89 = bf16[4,1024,256]{2,1,0:T(8,128)(2,1)} custom-call(s32[20]{0:T(128)S(1)} %pad_add_fusion.table, f32[4,1024,256]{2,1,0:T(8,128)S(1)} %copy-done.4, bf16[4,32,1024]{2,1,0:T(8,128)(2,1)S(1)} %bitcast.36, bf16[3,4,32,256]{3,2,1,0:T(8,128)(2,1)S(1)} %copy.26.picked, bf16[4,2,16,2,8,256]{5,4,3,2,1,0:T(8,128)(2,1)S(1)} %reshape.87.arrived, ...), custom_call_target="tpu_custom_call" | custom-call | tf_op jit(solution)/shard_map/pallas_call | solution.py:381
  (48 shorter events, 7.7 us)
Async XLA Ops:
  0.0 1.6 copy-start.1
  1.6 0.7 copy-start.8
  2.3 13.6 %copy-start.10 = (s32[4,2]{0,1:T(2,128)S(1)}, s32[4,2]{0,1:T(2,128)}, u32[]{:S(2)}) copy-start(s32[4,2]{0,1:T(2,128)} %param.14) | copy-start | bytes 100
  2.3 13.8 %copy-start.9 = (s32[4,2]{0,1:T(2,128)S(1)}, s32[4,2]{0,1:T(2,128)}, u32[]{:S(2)}) copy-start(s32[4,2]{0,1:T(2,128)} %param.15) | copy-start | bytes 100
  2.3 14.0 %copy-start.11 = (s32[4,2]{0,1:T(2,128)S(1)}, s32[4,2]{0,1:T(2,128)}, u32[]{:S(2)}) copy-start(s32[4,2]{0,1:T(2,128)} %param.13) | copy-start | bytes 100
  4.4 30.4 %all-to-all-start = ((bf16[128,2,8,256]{3,2,1,0:T(8,128)(2,1)}), bf16[128,2,8,256]{3,2,1,0:T(8,128)(2,1)S(1)}, u32[]{:S(2)}, u32[]{:S(2)}) async-start(bf16[128,2,8,256]{3,2,1,0:T(8,128)(2,1)} %bitcast.2), calls=%async_computation | async-start | bytes 2097152 | tf_op jit(solution)/shard_map/all_to_all | solution.py:19
  15.9 25.7 %copy-start.7 = (bf16[4,1024,32]{1,2,0:T(8,128)(2,1)S(1)}, bf16[4,1024,32]{1,2,0:T(8,128)(2,1)}, u32[]{:S(2)}) copy-start(bf16[4,1024,32]{1,2,0:T(8,128)(2,1)} %param.10) | copy-start | bytes 786436
  16.5 27.3 %copy-start.12 = (s32[128]{0:T(128)S(1)}, s32[128]{0:T(128)}, u32[]{:S(2)}) copy-start(s32[128]{0:T(128)} %param.11) | copy-start | bytes 1540
  36.6 23.9 %copy-start.2 = (bf16[4,1024,256]{2,1,0:T(8,128)(2,1)S(1)}, bf16[4,1024,256]{2,1,0:T(8,128)(2,1)}, u32[]{:S(2)}) copy-start(bf16[4,1024,256]{2,1,0:T(8,128)(2,1)} %residual.1) | copy-start | bytes 6291460
  36.6 23.9 %all-to-all-start.1 = ((bf16[128,2,8,256]{3,2,1,0:T(8,128)(2,1)}), bf16[128,2,8,256]{3,2,1,0:T(8,128)(2,1)S(1)}, u32[]{:S(2)}, u32[]{:S(2)}) async-start(bf16[128,2,8,256]{3,2,1,0:T(8,128)(2,1)} %shard_map.83), calls=%async_computation.1 | async-start | bytes 2097152 | tf_op jit(solution)/shard_map/all_to_all | solution.py:19
  62.1 1.3 copy-start.5
  65.4 17.1 %all-to-all-start.2 = ((bf16[128,8,128]{2,1,0:T(8,128)(2,1)}), bf16[128,8,128]{2,1,0:T(8,128)(2,1)S(1)}, u32[]{:S(2)}, u32[]{:S(2)}) async-start(bf16[128,8,128]{2,1,0:T(8,128)(2,1)} %pad_maximum_fusion), calls=%async_computation.2 | async-start | bytes 524288 | tf_op jit(solution)/shard_map/all_to_all | solution.py:19
  70.0 1.6 copy-start.6
  77.2 1.9 copy-start.3
  176.2 1.1 copy-start
  177.4 16.6 %all-to-all-start.5 = ((bf16[128,8,128]{2,1,0:T(8,128)(2,1)}), bf16[128,8,128]{2,1,0:T(8,128)(2,1)}, u32[]{:S(2)}, u32[]{:S(2)}) async-start(bf16[128,8,128]{2,1,0:T(8,128)(2,1)} %shard_map.88), calls=%async_computation.5 | async-start | bytes 524288 | tf_op jit(solution)/shard_map/all_to_all | solution.py:19
  183.1 1.8 slice-start
  195.9 2.2 %copy-start.4 = (f32[4,1024,256]{2,1,0:T(8,128)S(1)}, f32[4,1024,256]{2,1,0:T(8,128)}, u32[]{:S(2)}) copy-start(f32[4,1024,256]{2,1,0:T(8,128)} %copy-done.3) | copy-start | bytes 12582916

commit v4 on v3

--- a/solution.py
+++ b/solution.py
@@ -12,7 +12,7 @@
 HALF = 128
 LANE = 128
 GROUP = 8
-VMEM_LIMIT = 40 * 1024 * 1024
+VMEM_LIMIT = 12 * 1024 * 1024
 
 
 def spread(value):
@@ -91,23 +91,40 @@
     second, both = flags(table, sub, which)
     inside = jnp.maximum(both, (second == half).astype(jnp.int32)).astype(jnp.float32)
     other = jnp.bitwise_xor(sub, table[2 + which])
-    rows = arrived[other, half * both, :, which].astype(jnp.float32)
+    rows = arrived(other, half * both).astype(jnp.float32)
     return rows.reshape(HALF, rows.shape[-1]), inside
 
 
-def weigh_kernel(table, residual, modes, arrived, weighted, restricted):
+def weigh_kernel(table, residual, modes, arrived, base, weighted, payload, restricted, turned):
     sub = pl.program_id(0)
     for which in range(2):
         for half in range(2):
             start = (which * 2 + half) * HALF
-            rows, inside = arrived_rows(table, sub, which, half, arrived)
+            rows, inside = arrived_rows(
+                table, sub, which, half, lambda i, h, which=which: arrived[i, h, :, which]
+            )
             own = residual[0, start : start + HALF].astype(jnp.float32)
             value = (own + rows * inside) * (1.0 - 0.5 * inside)
             weighted[0, start : start + HALF] = value.astype(jnp.bfloat16)
     weighted[0, 4 * HALF :] = residual[0, 4 * HALF :]
-    restricted[0] = lax.dot_general(
+    restricted[pl.ds(pl.multiple_of(sub * MODES, MODES), MODES)] = lax.dot_general(
         modes[0], weighted[0], (((1,), (0,)), ((), ())), preferred_element_type=jnp.float32
-    ).astype(jnp.bfloat16)
+    )
+
+    @pl.when(sub == pl.num_programs(0) - 1)
+    def _():
+        devices, rows, _ = payload.shape
+        turned[: 2 * devices] = restricted[...].T
+        turned[2 * devices :] = jnp.zeros((turned.shape[0] - 2 * devices, LANE), jnp.float32)
+        own = lax.broadcasted_iota(jnp.int32, (rows, LANE), 0) < 2
+
+        def step(device, carry):
+            piece = turned[pl.ds(2 * device, rows)]
+            rest = base[device].astype(jnp.float32)
+            payload[device] = jnp.where(own, piece, rest).astype(jnp.bfloat16)
+            return carry
+
+        lax.fori_loop(0, devices, step, 0, unroll=8)
 
 
 def prolong(modes, picked):
@@ -116,14 +133,16 @@
     )
 
 
-def finish_kernel(table, local, modes, picked, arrived, arrived_modes, out):
+def finish_kernel(table, local, modes, picked, first, second, arrived_modes, out):
     sub = pl.program_id(0)
     added = prolong(modes[0], picked[0, sub])
     for which in range(2):
         other = jnp.bitwise_xor(sub, table[2 + which])
         for half in range(2):
             start = (which * 2 + half) * HALF
-            rows, inside = arrived_rows(table, sub, which, half, arrived)
+            rows, inside = arrived_rows(
+                table, sub, which, half, lambda *at, which=which: (first, second)[which][at]
+            )
             _, both = flags(table, sub, which)
             theirs = prolong(arrived_modes[which, other, half * both], picked[1 + which, other])
             theirs = (0.5 * (rows + theirs)).astype(jnp.bfloat16).astype(jnp.float32)
@@ -185,23 +204,20 @@
             at = 4 + 2 * which
             shared.append(jnp.concatenate([piece[at : at + 1], piece[at + 1 : at + 2]], 1))
         out[device, :, columns:local_at] = jnp.concatenate(shared, 0).astype(jnp.bfloat16)
-        out[device, :, local_at:] = packed[device]
+        out[device, :, local_at:] = packed[device, :, : out.shape[-1] - local_at]
         return carry
 
     lax.fori_loop(0, devices, forward, 0, unroll=4)
 
 
-def join_kernel(table, partial, merged, out):
-    rows = partial.shape[-1]
-    size = (out.shape[-1] - rows) // 2
-    base = merged.shape[-1] - 2 * size
+def join_kernel(table, partial, merged, packed, out):
+    rows, size = partial.shape[-1], packed.shape[-1] // 2
+    base = merged.shape[-1] - size
 
     def step(device, carry):
         out[device, :, :rows] = partial[device]
-        for which in range(2):
-            out[device, :, rows + which * size : rows + (which + 1) * size] = merged[
-                jnp.bitwise_xor(device, table[which]), :, base + which * size : base + (which + 1) * size
-            ]
+        out[device, :, rows : rows + size] = merged[jnp.bitwise_xor(device, table[0]), :, base:]
+        out[device, :, rows + size :] = packed[device, :, size:]
         return carry
 
     lax.fori_loop(0, partial.shape[0], step, 0, unroll=4)
@@ -250,14 +266,13 @@
 
     lax.fori_loop(0, devices // GROUP, step, 0)
 
+    size = out.shape[-1] - 3 * LANE
+
     def share(device, carry):
-        rows = [
-            chosen_rows[device],
-            chosen_rows[jnp.bitwise_xor(device, table[0])],
-            chosen_rows[jnp.bitwise_xor(device, table[1])],
-        ]
-        rows.append(jnp.zeros_like(rows[0]))
-        out[device] = jnp.concatenate(rows, 0).astype(jnp.bfloat16)
+        first, second = (jnp.bitwise_xor(device, table[which]) for which in range(2))
+        for at, source in enumerate((device, first, second)):
+            out[device, :, at * LANE : (at + 1) * LANE] = chosen_rows[source].astype(jnp.bfloat16)
+        out[device, :, 3 * LANE :] = partial[second, :, partial.shape[-1] - size :]
         return carry
 
     lax.fori_loop(0, devices, share, 0, unroll=4)
@@ -305,31 +320,33 @@
         out_specs=packed_spec,
     )(offsets, residual)
     arrived = exchange(packed, table)
-    weighted, restricted = call(
+    digits = jnp.stack([coarse_map // LANE, coarse_map % LANE]).astype(jnp.bfloat16)
+    digits = jnp.concatenate([jnp.zeros_like(digits), digits], 0)
+    shared = turned_modes[:, :, : 4 * HALF].reshape(count, MODES, 2, 2, HALF)
+    second = table[4:12].reshape(count, 1, 2, 1) == 1
+    shared = jnp.stack(
+        [jnp.where(second, shared[:, :, :, 1], shared[:, :, :, 0]), shared[:, :, :, 1]], 3
+    ).reshape(devices, 4, HALF)
+    base = jnp.concatenate([jnp.broadcast_to(digits[None], (devices,) + digits.shape), shared], 1)
+    weighted, payload = call(
         weigh_kernel,
-        (field, jax.ShapeDtypeStruct((count, MODES, cases), jnp.bfloat16)),
+        (field, jax.ShapeDtypeStruct(base.shape, jnp.bfloat16)),
         grid=(count,),
         in_specs=[
             smem(),
             per_sub(trace_len, cases),
             per_sub(MODES, trace_len),
             same(*arrived.shape),
+            same(*base.shape),
         ],
-        out_specs=(per_sub(trace_len, cases), per_sub(MODES, cases)),
-    )(table, residual, turned_modes, arrived)
-
-    by_case = restricted.reshape(count * MODES, cases).T.reshape(devices, 2, count * MODES)
-    digits = jnp.stack([coarse_map // LANE, coarse_map % LANE]).astype(jnp.bfloat16)
-    shared = turned_modes[:, :, : 4 * HALF].reshape(count, MODES, 2, 2, HALF)
-    second = table[4:12].reshape(count, 1, 2, 1) == 1
-    shared = jnp.stack(
-        [jnp.where(second, shared[:, :, :, 1], shared[:, :, :, 0]), shared[:, :, :, 1]], 3
-    ).reshape(devices, 4, HALF)
-    received = spread(
-        jnp.concatenate(
-            [by_case, jnp.broadcast_to(digits[None], (devices,) + digits.shape), shared], 1
-        )
-    )
+        out_specs=(per_sub(trace_len, cases), same(*base.shape)),
+        scratch_shapes=[
+            pltpu.VMEM((count * MODES, cases), jnp.float32),
+            pltpu.VMEM((cases + 8, LANE), jnp.float32),
+        ],
+    )(table, residual, turned_modes, arrived, base)
+    received = spread(payload)
+
     local_part, packed = call(
         local_kernel,
         (jax.ShapeDtypeStruct(residual.shape, jnp.float32), packed_shape),
@@ -343,7 +360,7 @@
     rows, columns = coarse_inverse.shape
     placed = call(
         scatter_kernel,
-        jax.ShapeDtypeStruct((devices, 2, columns + 2 * HALF + lanes), jnp.bfloat16),
+        jax.ShapeDtypeStruct((devices, 2, columns + 2 * HALF + lanes // 2), jnp.bfloat16),
         in_specs=[smem(), whole(), whole()],
         out_specs=whole(),
         scratch_shapes=[
@@ -360,15 +377,18 @@
     joined = call(
         join_kernel,
         jax.ShapeDtypeStruct((devices, 2, rows + lanes), jnp.bfloat16),
-        in_specs=[smem(), whole(), whole()],
+        in_specs=[smem(), whole(), whole(), whole()],
         out_specs=whole(),
-    )(table, partial_sum.reshape(devices, 2, rows), placed)
+    )(table, partial_sum.reshape(devices, 2, rows), placed, packed)
     joined = spread(joined)
-    arrived_local = joined[:, :, rows:].reshape(devices, 2, 2, 4, cases).transpose(0, 2, 3, 1, 4)
-    arrived_local = arrived_local.reshape(packed_shape.shape)
+
+    def unpack(value):
+        value = value.reshape(devices, 2, 4, cases).transpose(0, 2, 1, 3)
+        return value.reshape(count, 2, HALF // 8, 8, cases)
+
     picked = call(
         functools.partial(gather_kernel, row_blocks=lax.axis_size("row")),
-        jax.ShapeDtypeStruct((devices, 8, LANE), jnp.bfloat16),
+        jax.ShapeDtypeStruct((devices, 2, 3 * LANE + lanes // 2), jnp.bfloat16),
         in_specs=[smem(), whole(), whole()],
         out_specs=whole(),
         scratch_shapes=[
@@ -376,7 +396,10 @@
             pltpu.VMEM((devices, 2, LANE), jnp.float32),
         ],
     )(table, received, joined)
-    picked = spread(picked)[:, :6].reshape(devices, 3, 2, count * MODES).transpose(1, 3, 0, 2)
+    picked = spread(picked)
+    arrived_first = unpack(joined[:, :, rows : rows + lanes // 2])
+    arrived_second = unpack(picked[:, :, 3 * LANE :])
+    picked = picked[:, :, : 3 * LANE].reshape(devices, 2, 3, count * MODES).transpose(2, 3, 0, 1)
     picked = picked.reshape(3, count, MODES, cases)
     return call(
         finish_kernel,
@@ -387,11 +410,12 @@
             per_sub(trace_len, cases),
             per_sub(MODES, trace_len),
             same(*picked.shape),
-            same(*arrived_local.shape),
+            same(*arrived_first.shape),
+            same(*arrived_second.shape),
             same(*arrived_modes.shape),
         ],
         out_specs=per_sub(trace_len, cases),
-    )(table, local_part, turned_modes, picked, arrived_local, arrived_modes)
+    )(table, local_part, turned_modes, picked, arrived_first, arrived_second, arrived_modes)
 
 
 def solution(mesh):

time: 202 us -> 201 us (level)
  waiting for transfers between devices: 41.3 us -> 48.6 us
  blocking collectives: 70 us -> 64.4 us
  other arithmetic: 4.18 us -> 1.56 us
  Pallas kernels: 28.6 us -> 26 us
  local copies, waits for them, and re-layouts: 26 us -> 28.5 us
    all_to_all x4, waiting for transfers between devices: 41.3 us -> 48.6 us  [spread(): return lax.all_to_all(value, AXES, 0, 0, tiled=True)]
    all_to_all x2, blocking collectives: 70 us -> 64.4 us  [spread(): return lax.all_to_all(value, AXES, 0, 0, tiled=True)]
    unnamed x26 -> x34, local copies, waits for them, and re-layouts: 10.4 us -> 15.2 us
    pallas_call x1, Pallas kernels: 5.58 us -> 3.51 us  [shards(): call(local_kernel, (jax.ShapeDtypeStruct(residual.shape, jnp.float32), pa...]
    slice x3 -> x4, local copies, waits for them, and re-layouts: 0.98 us -> 3.05 us  [the longest x1 1.4 us: shards(): arrived_second = unpack(picked[:, :, 3 * LANE:])]
  transfers between devices with their start and end apart: 4 -> 4, of which waited for: 3 -> 3; matrix products, arithmetic and copies ran while one was open for 5% -> 3% of each run, Pallas kernels for 3% -> 2%
where the time goes in v4:
time: 201 us
  blocking collectives  64.4 us (32%)
  waiting for transfers between devices  48.6 us (24%)
  local copies, waits for them, and re-layouts  28.5 us (14%)
  starting transfers between devices  26.6 us (13%)
  Pallas kernels  26 us (13%)
  matrix products  4.59 us (2%)
    all_to_all x2, blocking collectives, spread(): return lax.all_to_all(value, AXES, 0, 0, tiled=True)  64.4 us
    all_to_all x4, waiting for transfers between devices, spread(): return lax.all_to_all(value, AXES, 0, 0, tiled=True)  48.6 us
    all_to_all x4, starting transfers between devices, spread(): return lax.all_to_all(value, AXES, 0, 0, tiled=True)  26.6 us
    unnamed x34, local copies, waits for them, and re-layouts  15.2 us
    pallas_call x1, Pallas kernels, shards(): call(scatter_kernel, jax.ShapeDtypeStruct((devices, 2, columns + 2 * HALF...  6.31 us
    pallas_call x1, Pallas kernels, shards(): call(functools.partial(gather_kernel, row_blocks=lax.axis_size('row')), j...  6 us
    dot_general x1, matrix products, shards(): lax.dot_general(coarse_rhs, coarse_inverse, (((1,), (1,)), ((), ())), pre...  4.59 us
  transfers between devices with their start and end apart: 4, of which 3 were waited for; matrix products, arithmetic and copies ran while one was open for 3% of the time, Pallas kernels for 2%

profile of v4, /device:TPU:1, one launch (start us, length us, event | category | flops | bytes accessed | tf_op | source)
XLA Modules:
  0.0 200.6 jit_solution(9200721441834876196)
XLA Ops:
  0.0 1.6 copy-done.1
  2.3 2.1 %shard_map.82 = bf16[4,2,16,2,8,256]{5,4,3,2,1,0:T(8,128)(2,1)} custom-call(s32[2,4]{1,0:T(2,128)S(1)} %bitcast.35, bf16[4,1024,256]{2,1,0:T(8,128)(2,1)S(1)} %copy-done.1), custom_call_target="tpu_custom_call" | custom-call | tf_op jit(solution)/shard_map/pallas_call | solution.py:315
  4.4 11.5 %all-to-all-start = ((bf16[128,2,8,256]{3,2,1,0:T(8,128)(2,1)}), bf16[128,2,8,256]{3,2,1,0:T(8,128)(2,1)S(1)}, u32[]{:S(2)}, u32[]{:S(2)}) async-start(bf16[128,2,8,256]{3,2,1,0:T(8,128)(2,1)} %bitcast.2), calls=%async_computation | async-start | bytes 2097152 | tf_op jit(solution)/shard_map/all_to_all | solution.py:19
  16.5 18.3 %all-to-all-done.chunks = bf16[128,2,8,256]{3,2,1,0:T(8,128)(2,1)S(1)} async-done(((bf16[128,2,8,256]{3,2,1,0:T(8,128)(2,1)}), bf16[128,2,8,256]{3,2,1,0:T(8,128)(2,1)S(1)}, u32[]{:S(2)}, u32[]{:S(2)}) %all-to-all-start) | async-done | bytes 1048608 | tf_op jit(solution)/shard_map/all_to_all | solution.py:19
  34.8 1.9 shard_map.83
  36.6 4.8 %all-to-all-start.1 = ((bf16[128,2,8,256]{3,2,1,0:T(8,128)(2,1)}), bf16[128,2,8,256]{3,2,1,0:T(8,128)(2,1)S(1)}, u32[]{:S(2)}, u32[]{:S(2)}) async-start(bf16[128,2,8,256]{3,2,1,0:T(8,128)(2,1)} %shard_map.83), calls=%async_computation.1 | async-start | bytes 2097152 | tf_op jit(solution)/shard_map/all_to_all | solution.py:19
  42.2 0.9 reshape.58
  43.8 0.9 pad_maximum_fusion.base
  44.7 15.8 %all-to-all-done.1 = bf16[128,2,8,256]{3,2,1,0:T(8,128)(2,1)S(1)} async-done(((bf16[128,2,8,256]{3,2,1,0:T(8,128)(2,1)}), bf16[128,2,8,256]{3,2,1,0:T(8,128)(2,1)S(1)}, u32[]{:S(2)}, u32[]{:S(2)}) %all-to-all-start.1) | async-done | bytes 1048608 | tf_op jit(solution)/shard_map/all_to_all | solution.py:19
  60.5 0.9 copy-done.10
  61.5 1.8 shard_map.84
  63.2 1.3 copy-done.6
  65.3 4.6 %all-to-all-start.2 = ((bf16[128,8,128]{2,1,0:T(8,128)(2,1)}), bf16[128,8,128]{2,1,0:T(8,128)(2,1)S(1)}, u32[]{:S(2)}, u32[]{:S(2)}) async-start(bf16[128,8,128]{2,1,0:T(8,128)(2,1)} %copy-done.11), calls=%async_computation.2 | async-start | bytes 524288 | tf_op jit(solution)/shard_map/all_to_all | solution.py:19
  69.9 3.4 %copy-done = bf16[4,1024,1024]{2,1,0:T(8,128)(2,1)S(1)} copy-done((bf16[4,1024,1024]{2,1,0:T(8,128)(2,1)S(1)}, bf16[4,1024,1024]{2,1,0:T(8,128)(2,1)}, u32[]{:S(2)}) %copy-start) | copy-done | bytes 8388632
  73.3 1.6 copy-done.7
  74.9 3.5 %shard_map.85 = (f32[4,1024,256]{2,1,0:T(8,128)S(1)}, bf16[4,2,16,2,8,256]{5,4,3,2,1,0:T(8,128)(2,1)S(1)}) custom-call(s32[2,4]{1,0:T(2,128)S(1)} %bitcast.36, bf16[4,1024,1024]{2,1,0:T(8,128)(2,1)S(1)} %copy-done, bf16[4,1024,256]{2,1,0:T(8,128)(2,1)S(1)} %copy-done.7), custom_call_target="tpu_custom_call" | custom-call | tf_op jit(solution)/shard_map/pallas_call | solution.py:350
  78.4 1.9 copy-done.3
  81.7 6.3 %shard_map.86 = bf16[128,2,3328]{2,1,0:T(2,128)(2,1)S(1)} custom-call(s32[20]{0:T(128)S(1)} %pad_add_fusion.table, bf16[128,8,128]{2,1,0:T(8,128)(2,1)S(1)} %all-to-all-done.2.received, bf16[128,2,2048]{2,1,0:T(2,128)(2,1)S(1)} %reshape.61.packed), custom_call_target="tpu_custom_call" | custom-call | tf_op jit(solution)/shard_map/pallas_call | solution.py:361
  88.0 35.7 %all_to_all.30.merged = bf16[128,2,3328]{2,1,0:T(2,128)(2,1)S(1)} all-to-all(bf16[128,2,3328]{2,1,0:T(2,128)(2,1)S(1)} %shard_map.86), channel_id=1, replica_groups=mesh['row'=16,'col'=8] {'row','col'}, dimensions={0} | all-to-all | bytes 3407872 | tf_op jit(solution)/shard_map/all_to_all | solution.py:19
  123.6 1.7 slice.41
  125.3 2.3 %reshape.62 = bf16[256,2048]{1,0:T(8,128)(2,1)} reshape(bf16[128,2,2048]{2,1,0:T(2,128)(2,1)} %slice.41) | data formatting | bytes 2097152 | tf_op jit(solution)/shard_map/reshape | solution.py:372
  127.6 4.6 %convolution_convert_fusion = bf16[256,1024]{1,0:T(8,128)(2,1)} fusion(bf16[256,2048]{1,0:T(8,128)(2,1)} %reshape.62, bf16[1024,2048]{1,0:T(8,128)(2,1)} %param.12), kind=kOutput, calls=%fused_computation | convolution fusion | flops 1074003968 | bytes 5767168 | tf_op jit(solution)/shard_map/dot_general | solution.py:374
  132.2 1.2 reshape.63.partial
  133.4 0.9 shard_map.87
  134.3 28.7 %all_to_all.31.partial = bf16[128,2,3072]{2,1,0:T(2,128)(2,1)S(1)} all-to-all(bf16[128,2,3072]{2,1,0:T(2,128)(2,1)S(1)} %shard_map.87), channel_id=1, replica_groups=mesh['row'=16,'col'=8] {'row','col'}, dimensions={0} | all-to-all | bytes 3145728 | tf_op jit(solution)/shard_map/all_to_all | solution.py:19
  163.1 6.0 %shard_map.88 = bf16[128,2,1408]{2,1,0:T(2,128)(2,1)S(1)} custom-call(s32[20]{0:T(128)S(1)} %pad_add_fusion.table, bf16[128,8,128]{2,1,0:T(8,128)(2,1)S(1)} %all-to-all-done.2.received, bf16[128,2,3072]{2,1,0:T(2,128)(2,1)S(1)} %all_to_all.31.partial), custom_call_target="tpu_custom_call" | custom-call | tf_op jit(solution)/shard_map/pallas_call | solution.py:389
  169.9 5.7 %all-to-all-start.5 = ((bf16[128,2,1408]{2,1,0:T(2,128)(2,1)}), bf16[128,2,1408]{2,1,0:T(2,128)(2,1)}, u32[]{:S(2)}, u32[]{:S(2)}) async-start(bf16[128,2,1408]{2,1,0:T(2,128)(2,1)} %copy-done.5), calls=%async_computation.5 | async-start | bytes 1441792 | tf_op jit(solution)/shard_map/all_to_all | solution.py:19
  176.4 14.5 %all-to-all-done.5 = bf16[128,2,1408]{2,1,0:T(2,128)(2,1)} async-done(((bf16[128,2,1408]{2,1,0:T(2,128)(2,1)}), bf16[128,2,1408]{2,1,0:T(2,128)(2,1)}, u32[]{:S(2)}, u32[]{:S(2)}) %all-to-all-start.5) | async-done | bytes 720928 | tf_op jit(solution)/shard_map/all_to_all | solution.py:19
  191.0 1.1 slice.42
  193.2 1.4 slice.44
  194.9 2.2 %copy-done.4 = f32[4,1024,256]{2,1,0:T(8,128)S(1)} copy-done((f32[4,1024,256]{2,1,0:T(8,128)S(1)}, f32[4,1024,256]{2,1,0:T(8,128)}, u32[]{:S(2)}) %copy-start.4) | copy-done | bytes 4194328
  197.0 3.5 %shard_map.89 = bf16[4,1024,256]{2,1,0:T(8,128)(2,1)} custom-call(s32[20]{0:T(128)S(1)} %pad_add_fusion.table, f32[4,1024,256]{2,1,0:T(8,128)S(1)} %copy-done.4, bf16[4,32,1024]{2,1,0:T(8,128)(2,1)S(1)} %bitcast.33, bf16[3,4,32,256]{3,2,1,0:T(8,128)(2,1)S(1)} %copy.26.picked, bf16[4,2,16,8,256]{4,3,2,1,0:T(8,128)(2,1)S(1)} %reshape.67.first, ...), custom_call_target="tpu_custom_call" | custom-call | tf_op jit(solution)/shard_map/pallas_call | solution.py:404
  (57 shorter events, 7.7 us)
Async XLA Ops:
  0.0 1.6 copy-start.1
  1.6 0.7 copy-start.12
  2.3 13.6 %copy-start.14 = (s32[4,2]{0,1:T(2,128)S(1)}, s32[4,2]{0,1:T(2,128)}, u32[]{:S(2)}) copy-start(s32[4,2]{0,1:T(2,128)} %param.14) | copy-start | bytes 100
  2.3 13.8 %copy-start.13 = (s32[4,2]{0,1:T(2,128)S(1)}, s32[4,2]{0,1:T(2,128)}, u32[]{:S(2)}) copy-start(s32[4,2]{0,1:T(2,128)} %param.15) | copy-start | bytes 100
  2.3 14.0 %copy-start.15 = (s32[4,2]{0,1:T(2,128)S(1)}, s32[4,2]{0,1:T(2,128)}, u32[]{:S(2)}) copy-start(s32[4,2]{0,1:T(2,128)} %param.13) | copy-start | bytes 100
  4.4 30.4 %all-to-all-start = ((bf16[128,2,8,256]{3,2,1,0:T(8,128)(2,1)}), bf16[128,2,8,256]{3,2,1,0:T(8,128)(2,1)S(1)}, u32[]{:S(2)}, u32[]{:S(2)}) async-start(bf16[128,2,8,256]{3,2,1,0:T(8,128)(2,1)} %bitcast.2), calls=%async_computation | async-start | bytes 2097152 | tf_op jit(solution)/shard_map/all_to_all | solution.py:19
  16.5 25.1 %copy-start.8 = (bf16[4,1024,32]{1,2,0:T(8,128)(2,1)S(1)}, bf16[4,1024,32]{1,2,0:T(8,128)(2,1)}, u32[]{:S(2)}) copy-start(bf16[4,1024,32]{1,2,0:T(8,128)(2,1)} %param.10) | copy-start | bytes 786436
  16.5 26.7 %copy-start.16 = (s32[128]{0:T(128)S(1)}, s32[128]{0:T(128)}, u32[]{:S(2)}) copy-start(s32[128]{0:T(128)} %param.11) | copy-start | bytes 1540
  36.6 23.9 %copy-start.2 = (bf16[4,1024,256]{2,1,0:T(8,128)(2,1)S(1)}, bf16[4,1024,256]{2,1,0:T(8,128)(2,1)}, u32[]{:S(2)}) copy-start(bf16[4,1024,256]{2,1,0:T(8,128)(2,1)} %residual.1) | copy-start | bytes 6291460
  36.6 23.9 %all-to-all-start.1 = ((bf16[128,2,8,256]{3,2,1,0:T(8,128)(2,1)}), bf16[128,2,8,256]{3,2,1,0:T(8,128)(2,1)S(1)}, u32[]{:S(2)}, u32[]{:S(2)}) async-start(bf16[128,2,8,256]{3,2,1,0:T(8,128)(2,1)} %shard_map.83), calls=%async_computation.1 | async-start | bytes 2097152 | tf_op jit(solution)/shard_map/all_to_all | solution.py:19
  60.5 1.0 copy-start.10
  63.2 1.3 copy-start.6
  64.6 0.7 copy-start.11
  65.3 16.4 %all-to-all-start.2 = ((bf16[128,8,128]{2,1,0:T(8,128)(2,1)}), bf16[128,8,128]{2,1,0:T(8,128)(2,1)S(1)}, u32[]{:S(2)}, u32[]{:S(2)}) async-start(bf16[128,8,128]{2,1,0:T(8,128)(2,1)} %copy-done.11), calls=%async_computation.2 | async-start | bytes 524288 | tf_op jit(solution)/shard_map/all_to_all | solution.py:19
  69.9 3.4 %copy-start = (bf16[4,1024,1024]{2,1,0:T(8,128)(2,1)S(1)}, bf16[4,1024,1024]{2,1,0:T(8,128)(2,1)}, u32[]{:S(2)}) copy-start(bf16[4,1024,1024]{2,1,0:T(8,128)(2,1)} %inverse.1) | copy-start | bytes 25165828
  73.3 1.6 copy-start.7
  78.4 1.9 copy-start.3
  169.1 0.9 copy-start.5
  169.9 21.0 %all-to-all-start.5 = ((bf16[128,2,1408]{2,1,0:T(2,128)(2,1)}), bf16[128,2,1408]{2,1,0:T(2,128)(2,1)}, u32[]{:S(2)}, u32[]{:S(2)}) async-start(bf16[128,2,1408]{2,1,0:T(2,128)(2,1)} %copy-done.5), calls=%async_computation.5 | async-start | bytes 1441792 | tf_op jit(solution)/shard_map/all_to_all | solution.py:19
  192.4 2.4 %copy-start.9 = (bf16[4,1024,32]{1,2,0:T(8,128)(2,1)S(1)}, bf16[4,1024,32]{1,2,0:T(8,128)(2,1)}, u32[]{:S(2)}) copy-start(bf16[4,1024,32]{1,2,0:T(8,128)(2,1)} %param.10) | copy-start | bytes 786436
  194.8 2.2 %copy-start.4 = (f32[4,1024,256]{2,1,0:T(8,128)S(1)}, f32[4,1024,256]{2,1,0:T(8,128)}, u32[]{:S(2)}) copy-start(f32[4,1024,256]{2,1,0:T(8,128)} %copy-done.3) | copy-start | bytes 12582916

commit v5 on v4

--- a/solution.py
+++ b/solution.py
@@ -12,7 +12,7 @@
 HALF = 128
 LANE = 128
 GROUP = 8
-VMEM_LIMIT = 12 * 1024 * 1024
+VMEM_LIMIT = 16 * 1024 * 1024
 
 
 def spread(value):
@@ -54,7 +54,9 @@
         for half in range(2):
             start = which * 2 * HALF + (second * HALF if half == 0 else HALF)
             rows = load(pl.multiple_of(start, HALF)).astype(jnp.float32)
-            packed[0, half, :, which] = rows.reshape(HALF // 8, 8, rows.shape[-1]).astype(jnp.bfloat16)
+            for lane in range(2):
+                tile = rows[:, lane * LANE : (lane + 1) * LANE].reshape(HALF // 8, 8, LANE)
+                packed[0, half, :, which * 2 + lane] = tile.astype(jnp.bfloat16)
 
 
 def pack_kernel(offsets, field, packed):
@@ -67,17 +69,19 @@
 
 
 def reroute_kernel(table, chunks, out):
+    size = chunks.shape[1] // 2
+
     def step(device, carry):
         for which in range(2):
-            out[device, which] = chunks[jnp.bitwise_xor(device, table[which]), which]
+            rows = slice(which * size, (which + 1) * size)
+            out[device, rows] = chunks[jnp.bitwise_xor(device, table[which]), rows]
         return carry
 
     lax.fori_loop(0, chunks.shape[0], step, 0, unroll=8)
 
 
 def exchange(packed, table):
-    count, cases = packed.shape[0], packed.shape[-1]
-    chunks = spread(packed.reshape(-1, 2, 8, cases))
+    chunks = spread(packed.reshape(-1, 32, LANE))
     chunks = call(
         reroute_kernel,
         jax.ShapeDtypeStruct(chunks.shape, chunks.dtype),
@@ -91,8 +95,11 @@
     second, both = flags(table, sub, which)
     inside = jnp.maximum(both, (second == half).astype(jnp.int32)).astype(jnp.float32)
     other = jnp.bitwise_xor(sub, table[2 + which])
-    rows = arrived(other, half * both).astype(jnp.float32)
-    return rows.reshape(HALF, rows.shape[-1]), inside
+    tiles = [
+        arrived[other, half * both, :, which * 2 + lane].astype(jnp.float32).reshape(HALF, LANE)
+        for lane in range(2)
+    ]
+    return jnp.concatenate(tiles, 1), inside
 
 
 def weigh_kernel(table, residual, modes, arrived, base, weighted, payload, restricted, turned):
@@ -100,9 +107,7 @@
     for which in range(2):
         for half in range(2):
             start = (which * 2 + half) * HALF
-            rows, inside = arrived_rows(
-                table, sub, which, half, lambda i, h, which=which: arrived[i, h, :, which]
-            )
+            rows, inside = arrived_rows(table, sub, which, half, arrived)
             own = residual[0, start : start + HALF].astype(jnp.float32)
             value = (own + rows * inside) * (1.0 - 0.5 * inside)
             weighted[0, start : start + HALF] = value.astype(jnp.bfloat16)
@@ -133,16 +138,32 @@
     )
 
 
-def finish_kernel(table, local, modes, picked, first, second, arrived_modes, out):
+def finish_kernel(table, local, modes, arrived, arrived_modes, out, pairs, picked):
     sub = pl.program_id(0)
+
+    @pl.when(sub == 0)
+    def _():
+        for first in range(4):
+            for half in range(2):
+
+                def step(piece, carry, first=first, half=half):
+                    for inner in range(4):
+                        tile = arrived[first, half, piece * 4 + inner, 4].astype(jnp.float32)
+                        at = (first * 2 + half) * 32 + pl.multiple_of(piece * 8, 8) + inner * 2
+                        for kind in range(3):
+                            pairs[kind, pl.ds(at, 2)] = tile[kind * 2 : kind * 2 + 2]
+                    return carry
+
+                lax.fori_loop(0, 4, step, 0)
+        for kind in range(3):
+            picked[kind] = pairs[kind].T.reshape(picked.shape[1:]).astype(jnp.bfloat16)
+
     added = prolong(modes[0], picked[0, sub])
     for which in range(2):
         other = jnp.bitwise_xor(sub, table[2 + which])
         for half in range(2):
             start = (which * 2 + half) * HALF
-            rows, inside = arrived_rows(
-                table, sub, which, half, lambda *at, which=which: (first, second)[which][at]
-            )
+            rows, inside = arrived_rows(table, sub, which, half, arrived)
             _, both = flags(table, sub, which)
             theirs = prolong(arrived_modes[which, other, half * both], picked[1 + which, other])
             theirs = (0.5 * (rows + theirs)).astype(jnp.bfloat16).astype(jnp.float32)
@@ -152,7 +173,7 @@
     out[0, 4 * HALF :] = (local[0, 4 * HALF :] + added[4 * HALF :]).astype(jnp.bfloat16)
 
 
-def scatter_kernel(table, received, packed, out, total, staged):
+def scatter_kernel(table, received, out, total, staged):
     devices = received.shape[0]
     place = lax.broadcasted_iota(jnp.int32, (LANE, LANE), 0).astype(jnp.float32)
     total[...] = jnp.zeros_like(total)
@@ -178,64 +199,88 @@
         return carry
 
     lax.fori_loop(0, devices // GROUP, step, 0)
-    blocks, _, columns = staged.shape
-    pieces = columns // LANE
+    blocks, size, _ = staged.shape
+    pieces = size // 2
     for block in range(blocks):
         for case in range(2):
             for piece in range(pieces):
                 at = case * LANE + block * pieces + piece
-                staged[block, case : case + 1, piece * LANE : (piece + 1) * LANE] = total[at : at + 1]
-
+                staged[block, piece * 2 + case : piece * 2 + case + 1] = total[at : at + 1]
     for block in range(blocks):
         value = staged[block].astype(jnp.bfloat16)
 
         def copies(row, carry, block=block, value=value):
-            out[row * blocks + block, :, :columns] = value
+            out[row * blocks + block, :size] = value
             return carry
 
         lax.fori_loop(0, devices // blocks, copies, 0, unroll=4)
-
-    local_at = columns + 2 * HALF
+    first = lax.broadcasted_iota(jnp.int32, (8, LANE), 0) < 6
 
     def forward(device, carry):
-        shared = []
-        for which in range(2):
-            piece = received[jnp.bitwise_xor(device, table[which])].astype(jnp.float32)
-            at = 4 + 2 * which
-            shared.append(jnp.concatenate([piece[at : at + 1], piece[at + 1 : at + 2]], 1))
-        out[device, :, columns:local_at] = jnp.concatenate(shared, 0).astype(jnp.bfloat16)
-        out[device, :, local_at:] = packed[device, :, : out.shape[-1] - local_at]
+        pieces = [
+            received[jnp.bitwise_xor(device, table[which])].astype(jnp.float32) for which in range(2)
+        ]
+        out[device, size:] = jnp.where(first, pieces[0], pieces[1]).astype(jnp.bfloat16)
         return carry
 
     lax.fori_loop(0, devices, forward, 0, unroll=4)
 
 
-def join_kernel(table, partial, merged, packed, out):
-    rows, size = partial.shape[-1], packed.shape[-1] // 2
-    base = merged.shape[-1] - size
-
-    def step(device, carry):
-        out[device, :, :rows] = partial[device]
-        out[device, :, rows : rows + size] = merged[jnp.bitwise_xor(device, table[0]), :, base:]
-        out[device, :, rows + size :] = packed[device, :, size:]
-        return carry
-
-    lax.fori_loop(0, partial.shape[0], step, 0, unroll=4)
+def product_kernel(placed, inverse, packed, out, pairs, left, parts):
+    at_step = pl.program_id(0)
+    groups = placed.shape[0] // 4
+    tiles, steps = pairs.shape[0], parts.shape[0]
+
+    @pl.when(at_step == 0)
+    def _():
+        def step(group, carry):
+            for inner in range(4):
+                rows = placed[group * 4 + inner, : 2 * tiles].astype(jnp.float32)
+                at = pl.multiple_of(group * 8, 8) + 2 * inner
+                for tile in range(tiles):
+                    pairs[tile, pl.ds(at, 2)] = rows[2 * tile : 2 * tile + 2]
+            return carry
+
+        lax.fori_loop(0, groups, step, 0)
+        for tile in range(tiles):
+            left[:, tile * LANE : (tile + 1) * LANE] = pairs[tile].astype(jnp.bfloat16)
+
+    parts[at_step] = lax.dot_general(
+        left[...], inverse[...], (((1,), (1,)), ((), ())), preferred_element_type=jnp.float32
+    )
+
+    @pl.when(at_step == steps - 1)
+    def _():
+        size = steps * parts.shape[2] // LANE * 2
+
+        def step(group, carry):
+            at = pl.multiple_of(group * 8, 8)
+            tall = [
+                parts[part, pl.ds(at, 8), lane * LANE : (lane + 1) * LANE]
+                for part in range(steps)
+                for lane in range(parts.shape[2] // LANE)
+            ]
+            for inner in range(4):
+                rows = jnp.concatenate([tile[2 * inner : 2 * inner + 2] for tile in tall], 0)
+                out[group * 4 + inner, :size] = rows.astype(jnp.bfloat16)
+                out[group * 4 + inner, size:] = packed[group * 4 + inner]
+            return carry
+
+        lax.fori_loop(0, groups, step, 0)
 
 
 def gather_kernel(table, received, partial, out, solved, chosen_rows, *, row_blocks):
-    devices, _, _ = partial.shape
+    devices = received.shape[0]
     pieces = LANE // row_blocks
-    rows = pieces * LANE
     col_blocks = devices // row_blocks
     for block in range(row_blocks):
-        value = partial[block * col_blocks, :, :rows].astype(jnp.float32)
+        value = partial[block * col_blocks, : 2 * pieces].astype(jnp.float32)
         for col in range(1, col_blocks):
-            value = value + partial[block * col_blocks + col, :, :rows].astype(jnp.float32)
+            value = value + partial[block * col_blocks + col, : 2 * pieces].astype(jnp.float32)
         for piece in range(pieces):
             for case in range(2):
                 at = case * LANE + block * pieces + piece
-                solved[at : at + 1] = value[case : case + 1, piece * LANE : (piece + 1) * LANE]
+                solved[at : at + 1] = value[2 * piece + case : 2 * piece + case + 1]
     turned = jnp.concatenate([solved[:LANE].T, solved[LANE:].T], 0).astype(jnp.bfloat16)
     place = lax.broadcasted_iota(jnp.int32, (LANE, LANE), 0).astype(jnp.float32)
 
@@ -266,13 +311,16 @@
 
     lax.fori_loop(0, devices // GROUP, step, 0)
 
-    size = out.shape[-1] - 3 * LANE
+    size = (partial.shape[1] - 2 * pieces) // 2
 
     def share(device, carry):
-        first, second = (jnp.bitwise_xor(device, table[which]) for which in range(2))
-        for at, source in enumerate((device, first, second)):
-            out[device, :, at * LANE : (at + 1) * LANE] = chosen_rows[source].astype(jnp.bfloat16)
-        out[device, :, 3 * LANE :] = partial[second, :, partial.shape[-1] - size :]
+        sources = [jnp.bitwise_xor(device, table[which]) for which in range(2)]
+        for which in range(2):
+            at = 2 * pieces + which * size
+            out[device, which * size : (which + 1) * size] = partial[sources[which], at : at + size]
+        rows = [chosen_rows[device], chosen_rows[sources[0]], chosen_rows[sources[1]]]
+        rows.append(jnp.zeros_like(rows[0]))
+        out[device, 2 * size :] = jnp.concatenate(rows, 0).astype(jnp.bfloat16)
         return carry
 
     lax.fori_loop(0, devices, share, 0, unroll=4)
@@ -309,8 +357,8 @@
 
     turned_modes = modes.transpose(0, 2, 1)
     offsets = block_offsets.T
-    packed_spec = per_sub(2, HALF // 8, 2, 8, cases)
-    packed_shape = jax.ShapeDtypeStruct((count, 2, HALF // 8, 2, 8, cases), jnp.bfloat16)
+    packed_spec = per_sub(2, HALF // 8, 4, 8, LANE)
+    packed_shape = jax.ShapeDtypeStruct((count, 2, HALF // 8, 4, 8, LANE), jnp.bfloat16)
 
     packed = call(
         pack_kernel,
@@ -346,6 +394,7 @@
         ],
     )(table, residual, turned_modes, arrived, base)
     received = spread(payload)
+    weighted, received = lax.optimization_barrier((weighted, received))
 
     local_part, packed = call(
         local_kernel,
@@ -354,41 +403,44 @@
         in_specs=[smem(), per_sub(trace_len, trace_len), per_sub(trace_len, cases)],
         out_specs=(per_sub(trace_len, cases), packed_spec),
     )(offsets, interface_inverse, weighted)
-    lanes = 2 * 4 * cases
-    packed = packed.reshape(devices, 2, 4, 2, cases).transpose(0, 3, 1, 2, 4).reshape(devices, 2, lanes)
+    packed = packed.reshape(devices, 32, LANE)
 
     rows, columns = coarse_inverse.shape
     placed = call(
         scatter_kernel,
-        jax.ShapeDtypeStruct((devices, 2, columns + 2 * HALF + lanes // 2), jnp.bfloat16),
-        in_specs=[smem(), whole(), whole()],
+        jax.ShapeDtypeStruct((devices, 2 * columns // LANE + 8, LANE), jnp.bfloat16),
+        in_specs=[smem(), whole()],
         out_specs=whole(),
         scratch_shapes=[
             pltpu.VMEM((2 * LANE, LANE), jnp.float32),
-            pltpu.VMEM((LANE * LANE // columns, 2, columns), jnp.float32),
-        ],
-    )(table, received, packed)
+            pltpu.VMEM((LANE * LANE // columns, 2 * columns // LANE, LANE), jnp.float32),
+        ],
+    )(table, received)
     placed = spread(placed)
-    coarse_rhs = placed[:, :, :columns].reshape(cases, columns)
-    arrived_modes = placed[:, :, columns : columns + 2 * HALF].reshape(count, MODES, 2, 2, HALF).transpose(2, 0, 3, 1, 4)
-    partial_sum = lax.dot_general(
-        coarse_rhs, coarse_inverse, (((1,), (1,)), ((), ())), preferred_element_type=jnp.float32
-    ).astype(jnp.bfloat16)
+    arrived_modes = placed[:, 2 * columns // LANE + 4 :].reshape(count, MODES, 2, 2, HALF)
+    arrived_modes = arrived_modes.transpose(2, 0, 3, 1, 4)
+    steps = 4
+    joined_shape = (devices, 2 * rows // LANE + 32, LANE)
     joined = call(
-        join_kernel,
-        jax.ShapeDtypeStruct((devices, 2, rows + lanes), jnp.bfloat16),
-        in_specs=[smem(), whole(), whole(), whole()],
-        out_specs=whole(),
-    )(table, partial_sum.reshape(devices, 2, rows), placed, packed)
+        product_kernel,
+        jax.ShapeDtypeStruct(joined_shape, jnp.bfloat16),
+        grid=(steps,),
+        in_specs=[
+            same(*placed.shape),
+            pl.BlockSpec((rows // steps, columns), lambda step: (step, 0)),
+            same(*packed.shape),
+        ],
+        out_specs=same(*joined_shape),
+        scratch_shapes=[
+            pltpu.VMEM((columns // LANE, cases, LANE), jnp.float32),
+            pltpu.VMEM((cases, columns), jnp.bfloat16),
+            pltpu.VMEM((steps, cases, rows // steps), jnp.float32),
+        ],
+    )(placed, coarse_inverse, packed)
     joined = spread(joined)
-
-    def unpack(value):
-        value = value.reshape(devices, 2, 4, cases).transpose(0, 2, 1, 3)
-        return value.reshape(count, 2, HALF // 8, 8, cases)
-
-    picked = call(
+    last = call(
         functools.partial(gather_kernel, row_blocks=lax.axis_size("row")),
-        jax.ShapeDtypeStruct((devices, 2, 3 * LANE + lanes // 2), jnp.bfloat16),
+        jax.ShapeDtypeStruct((devices, 40, LANE), jnp.bfloat16),
         in_specs=[smem(), whole(), whole()],
         out_specs=whole(),
         scratch_shapes=[
@@ -396,11 +448,7 @@
             pltpu.VMEM((devices, 2, LANE), jnp.float32),
         ],
     )(table, received, joined)
-    picked = spread(picked)
-    arrived_first = unpack(joined[:, :, rows : rows + lanes // 2])
-    arrived_second = unpack(picked[:, :, 3 * LANE :])
-    picked = picked[:, :, : 3 * LANE].reshape(devices, 2, 3, count * MODES).transpose(2, 3, 0, 1)
-    picked = picked.reshape(3, count, MODES, cases)
+    last = spread(last).reshape(count, 2, HALF // 8, 5, 8, LANE)
     return call(
         finish_kernel,
         field,
@@ -409,13 +457,15 @@
             smem(),
             per_sub(trace_len, cases),
             per_sub(MODES, trace_len),
-            same(*picked.shape),
-            same(*arrived_first.shape),
-            same(*arrived_second.shape),
+            same(*last.shape),
             same(*arrived_modes.shape),
         ],
         out_specs=per_sub(trace_len, cases),
-    )(table, local_part, turned_modes, picked, arrived_first, arrived_second, arrived_modes)
+        scratch_shapes=[
+            pltpu.VMEM((3, cases, LANE), jnp.float32),
+            pltpu.VMEM((3, count, MODES, cases), jnp.bfloat16),
+        ],
+    )(table, local_part, turned_modes, last, arrived_modes)
 
 
 def solution(mesh):

time: 201 us -> 188 us (0.935)
  blocking collectives: 64.4 us -> 44.3 us
  waiting for transfers between devices: 48.6 us -> 67 us
  local copies, waits for them, and re-layouts: 28.5 us -> 19.2 us
  matrix products: 4.59 us -> 0 us
  Pallas kernels: 26 us -> 30 us
    all_to_all x2, blocking collectives: 64.4 us -> 44.3 us  [spread(): return lax.all_to_all(value, AXES, 0, 0, tiled=True)]
    all_to_all x4, waiting for transfers between devices: 48.6 us -> 67 us  [spread(): return lax.all_to_all(value, AXES, 0, 0, tiled=True)]
    reshape x11 -> x1, local copies, waits for them, and re-layouts: 6.03 us -> 0.02 us  [shards(): placed[:, 2 * columns // LANE + 4:].reshape(count, MODES, 2, 2, HALF)]
    slice x6 -> x1, local copies, waits for them, and re-layouts: 4.83 us -> 0.07 us  [shards(): placed[:, 2 * columns // LANE + 4:].reshape(count, MODES, 2, 2, HALF)]
    dot_general x1 -> x0, matrix products: 4.59 us -> none  [shards(): lax.dot_general(coarse_rhs, coarse_inverse, (((1,), (1,)), ((), ())), pre...]
    pallas_call x2, Pallas kernels: 7.21 us -> 10.7 us  [the longest x1 7.28 us: shards(): call(scatter_kernel, jax.ShapeDtypeStruct((devices, 2 * columns // LANE +...]
    unnamed x34 -> x32, local copies, waits for them, and re-layouts: 15.2 us -> 16.9 us
  transfers between devices with their start and end apart: 4 -> 4, of which waited for: 3 -> 4; matrix products, arithmetic and copies ran while one was open for 3% -> 2% of each run, Pallas kernels for 2% -> 2%
where the time goes in v5:
time: 188 us; the launch traced here: 187 us
  waiting for transfers between devices  67 us (36%)
  blocking collectives  44.3 us (24%)
  Pallas kernels  30 us (16%)
  starting transfers between devices  25.3 us (13%)
  local copies, waits for them, and re-layouts  19.2 us (10%)
    all_to_all x4, waiting for transfers between devices, spread(): return lax.all_to_all(value, AXES, 0, 0, tiled=True)  67 us
    all_to_all x2, blocking collectives, spread(): return lax.all_to_all(value, AXES, 0, 0, tiled=True)  44.3 us
    all_to_all x4, starting transfers between devices, spread(): return lax.all_to_all(value, AXES, 0, 0, tiled=True)  25.3 us
    unnamed x32, local copies, waits for them, and re-layouts  16.9 us
    pallas_call x1, Pallas kernels, shards(): call(scatter_kernel, jax.ShapeDtypeStruct((devices, 2 * columns // LANE +...  7.28 us
    pallas_call x1, Pallas kernels, shards(): call(functools.partial(gather_kernel, row_blocks=lax.axis_size('row')), j...  6.03 us
    pallas_call x1, Pallas kernels, shards(): call(finish_kernel, field, grid=(count,), in_specs=[smem(), per_sub(trace...  3.9 us
  transfers between devices with their start and end apart: 4, of which 4 were waited for; matrix products, arithmetic and copies ran while one was open for 2% of the time, Pallas kernels for 2%

profile of v5, /device:TPU:1, one launch (start us, length us, event | category | flops | bytes accessed | tf_op | source)
XLA Modules:
  0.0 187.5 jit_solution(14121539351397074618)
XLA Ops:
  0.0 1.6 copy-done.1
  1.6 0.7 copy-done.11
  2.3 2.1 %shard_map.82 = bf16[4,2,16,4,8,128]{5,4,3,2,1,0:T(8,128)(2,1)} custom-call(s32[2,4]{1,0:T(2,128)S(1)} %bitcast.22, bf16[4,1024,256]{2,1,0:T(8,128)(2,1)S(1)} %copy-done.1), custom_call_target="tpu_custom_call" | custom-call | tf_op jit(solution)/shard_map/pallas_call | solution.py:363
  4.4 11.5 %all-to-all-start = ((bf16[128,32,128]{2,1,0:T(8,128)(2,1)}), bf16[128,32,128]{2,1,0:T(8,128)(2,1)S(1)}, u32[]{:S(2)}, u32[]{:S(2)}) async-start(bf16[128,32,128]{2,1,0:T(8,128)(2,1)} %bitcast.2), calls=%async_computation | async-start | bytes 2097152 | tf_op jit(solution)/shard_map/all_to_all | solution.py:19
  16.6 18.3 %all-to-all-done.chunks = bf16[128,32,128]{2,1,0:T(8,128)(2,1)S(1)} async-done(((bf16[128,32,128]{2,1,0:T(8,128)(2,1)}), bf16[128,32,128]{2,1,0:T(8,128)(2,1)S(1)}, u32[]{:S(2)}, u32[]{:S(2)}) %all-to-all-start) | async-done | bytes 1048608 | tf_op jit(solution)/shard_map/all_to_all | solution.py:19
  34.8 1.9 shard_map.83
  36.7 4.8 %all-to-all-start.1 = ((bf16[128,32,128]{2,1,0:T(8,128)(2,1)}), bf16[128,32,128]{2,1,0:T(8,128)(2,1)S(1)}, u32[]{:S(2)}, u32[]{:S(2)}) async-start(bf16[128,32,128]{2,1,0:T(8,128)(2,1)} %shard_map.83), calls=%async_computation.1 | async-start | bytes 2097152 | tf_op jit(solution)/shard_map/all_to_all | solution.py:19
  41.6 0.7 slice.22
  42.3 0.9 reshape.34
  43.5 0.3 pad_maximum_fusion.1
  43.9 0.8 pad_maximum_fusion.base
  44.7 15.8 %all-to-all-done.1 = bf16[128,32,128]{2,1,0:T(8,128)(2,1)S(1)} async-done(((bf16[128,32,128]{2,1,0:T(8,128)(2,1)}), bf16[128,32,128]{2,1,0:T(8,128)(2,1)S(1)}, u32[]{:S(2)}, u32[]{:S(2)}) %all-to-all-start.1) | async-done | bytes 1048608 | tf_op jit(solution)/shard_map/all_to_all | solution.py:19
  60.5 0.9 copy-done.10
  61.5 1.8 shard_map.84
  63.3 1.3 copy-done.7
  64.6 15.5 %all_to_all.30.received = bf16[128,8,128]{2,1,0:T(8,128)(2,1)S(1)} all-to-all(bf16[128,8,128]{2,1,0:T(8,128)(2,1)S(1)} %get-tuple-element.12), channel_id=1, replica_groups=mesh['row'=16,'col'=8] {'row','col'}, dimensions={0} | all-to-all | bytes 524288 | tf_op jit(solution)/shard_map/all_to_all | solution.py:19
  80.1 7.3 %shard_map.86 = bf16[128,40,128]{2,1,0:T(8,128)(2,1)} custom-call(s32[20]{0:T(128)S(1)} %pad_add_fusion.table, bf16[128,8,128]{2,1,0:T(8,128)(2,1)S(1)} %all_to_all.30.received), custom_call_target="tpu_custom_call" | custom-call | tf_op jit(solution)/shard_map/pallas_call | solution.py:409
  87.3 4.3 %all-to-all-start.3 = ((bf16[128,40,128]{2,1,0:T(8,128)(2,1)}), bf16[128,40,128]{2,1,0:T(8,128)(2,1)S(1)}, u32[]{:S(2)}, u32[]{:S(2)}) async-start(bf16[128,40,128]{2,1,0:T(8,128)(2,1)} %shard_map.86), calls=%async_computation.3 | async-start | bytes 2621440 | tf_op jit(solution)/shard_map/all_to_all | solution.py:19
  91.7 3.4 %copy-done = bf16[4,1024,1024]{2,1,0:T(8,128)(2,1)S(1)} copy-done((bf16[4,1024,1024]{2,1,0:T(8,128)(2,1)S(1)}, bf16[4,1024,1024]{2,1,0:T(8,128)(2,1)}, u32[]{:S(2)}) %copy-start) | copy-done | bytes 8388632
  95.1 1.6 copy-done.8
  96.6 3.5 %shard_map.85 = (f32[4,1024,256]{2,1,0:T(8,128)S(1)}, bf16[4,2,16,4,8,128]{5,4,3,2,1,0:T(8,128)(2,1)S(1)}) custom-call(s32[2,4]{1,0:T(2,128)S(1)} %bitcast.23, bf16[4,1024,1024]{2,1,0:T(8,128)(2,1)S(1)} %copy-done, bf16[4,1024,256]{2,1,0:T(8,128)(2,1)S(1)} %copy-done.8), custom_call_target="tpu_custom_call" | custom-call | tf_op jit(solution)/shard_map/pallas_call | solution.py:399
  100.2 1.9 %copy-done.5 = f32[4,1024,256]{2,1,0:T(8,128)} copy-done((f32[4,1024,256]{2,1,0:T(8,128)}, f32[4,1024,256]{2,1,0:T(8,128)S(1)}, u32[]{:S(2)}) %copy-start.5) | copy-done | bytes 4194328
  102.1 11.2 %all-to-all-done.3.placed = bf16[128,40,128]{2,1,0:T(8,128)(2,1)S(1)} async-done(((bf16[128,40,128]{2,1,0:T(8,128)(2,1)}), bf16[128,40,128]{2,1,0:T(8,128)(2,1)S(1)}, u32[]{:S(2)}, u32[]{:S(2)}) %all-to-all-start.3) | async-done | bytes 1310752 | tf_op jit(solution)/shard_map/all_to_all | solution.py:19
  113.3 2.2 %copy-done.4 = bf16[1024,2048]{1,0:T(8,128)(2,1)S(1)} copy-done((bf16[1024,2048]{1,0:T(8,128)(2,1)S(1)}, bf16[1024,2048]{1,0:T(8,128)(2,1)}, u32[]{:S(2)}) %copy-start.4) | copy-done | bytes 4194328
  115.5 3.5 %shard_map.87 = bf16[128,48,128]{2,1,0:T(8,128)(2,1)S(1)} custom-call(bf16[128,40,128]{2,1,0:T(8,128)(2,1)S(1)} %all-to-all-done.3.placed, bf16[1024,2048]{1,0:T(8,128)(2,1)S(1)} %copy-done.4, bf16[128,32,128]{2,1,0:T(8,128)(2,1)S(1)} %bitcast.20), custom_call_target="tpu_custom_call" | custom-call | tf_op jit(solution)/shard_map/pallas_call | solution.py:424
  119.0 28.8 %all_to_all.31.partial = bf16[128,48,128]{2,1,0:T(8,128)(2,1)S(1)} all-to-all(bf16[128,48,128]{2,1,0:T(8,128)(2,1)S(1)} %shard_map.87), channel_id=1, replica_groups=mesh['row'=16,'col'=8] {'row','col'}, dimensions={0} | all-to-all | bytes 3145728 | tf_op jit(solution)/shard_map/all_to_all | solution.py:19
  147.8 6.0 %shard_map.88 = bf16[128,40,128]{2,1,0:T(8,128)(2,1)S(1)} custom-call(s32[20]{0:T(128)S(1)} %pad_add_fusion.table, bf16[128,8,128]{2,1,0:T(8,128)(2,1)S(1)} %all_to_all.30.received, bf16[128,48,128]{2,1,0:T(8,128)(2,1)S(1)} %all_to_all.31.partial), custom_call_target="tpu_custom_call" | custom-call | tf_op jit(solution)/shard_map/pallas_call | solution.py:441
  153.9 1.0 copy-done.3
  154.9 4.7 %all-to-all-start.5 = ((bf16[128,40,128]{2,1,0:T(8,128)(2,1)}), bf16[128,40,128]{2,1,0:T(8,128)(2,1)S(1)}, u32[]{:S(2)}, u32[]{:S(2)}) async-start(bf16[128,40,128]{2,1,0:T(8,128)(2,1)} %copy-done.3), calls=%async_computation.5 | async-start | bytes 2621440 | tf_op jit(solution)/shard_map/all_to_all | solution.py:19
  159.7 21.7 %all-to-all-done.5 = bf16[128,40,128]{2,1,0:T(8,128)(2,1)S(1)} async-done(((bf16[128,40,128]{2,1,0:T(8,128)(2,1)}), bf16[128,40,128]{2,1,0:T(8,128)(2,1)S(1)}, u32[]{:S(2)}, u32[]{:S(2)}) %all-to-all-start.5) | async-done | bytes 1310752 | tf_op jit(solution)/shard_map/all_to_all | solution.py:19
  181.4 2.2 %copy-done.6 = f32[4,1024,256]{2,1,0:T(8,128)S(1)} copy-done((f32[4,1024,256]{2,1,0:T(8,128)S(1)}, f32[4,1024,256]{2,1,0:T(8,128)}, u32[]{:S(2)}) %copy-start.6) | copy-done | bytes 4194328
  183.6 3.9 %shard_map.89 = bf16[4,1024,256]{2,1,0:T(8,128)(2,1)} custom-call(s32[20]{0:T(128)S(1)} %pad_add_fusion.table, f32[4,1024,256]{2,1,0:T(8,128)S(1)} %copy-done.6, bf16[4,32,1024]{2,1,0:T(8,128)(2,1)S(1)} %bitcast.19, bf16[4,2,16,5,8,128]{5,4,3,2,1,0:T(8,128)(2,1)S(1)} %bitcast.15, bf16[2,4,2,32,128]{4,3,2,1,0:T(8,128)(2,1)S(1)} %bitcast.21), custom_call_target="tpu_custom_call" | custom-call | tf_op jit(solution)/shard_map/pallas_call | solution.py:452
  (38 shorter events, 1.2 us)
Async XLA Ops:
  0.0 1.6 copy-start.1
  1.6 0.7 copy-start.11
  2.3 13.7 %copy-start.13 = (s32[4,2]{0,1:T(2,128)S(1)}, s32[4,2]{0,1:T(2,128)}, u32[]{:S(2)}) copy-start(s32[4,2]{0,1:T(2,128)} %param.14) | copy-start | bytes 100
  2.3 13.9 %copy-start.12 = (s32[4,2]{0,1:T(2,128)S(1)}, s32[4,2]{0,1:T(2,128)}, u32[]{:S(2)}) copy-start(s32[4,2]{0,1:T(2,128)} %param.15) | copy-start | bytes 100
  2.3 14.1 %copy-start.14 = (s32[4,2]{0,1:T(2,128)S(1)}, s32[4,2]{0,1:T(2,128)}, u32[]{:S(2)}) copy-start(s32[4,2]{0,1:T(2,128)} %param.13) | copy-start | bytes 100
  4.4 30.4 %all-to-all-start = ((bf16[128,32,128]{2,1,0:T(8,128)(2,1)}), bf16[128,32,128]{2,1,0:T(8,128)(2,1)S(1)}, u32[]{:S(2)}, u32[]{:S(2)}) async-start(bf16[128,32,128]{2,1,0:T(8,128)(2,1)} %bitcast.2), calls=%async_computation | async-start | bytes 2097152 | tf_op jit(solution)/shard_map/all_to_all | solution.py:19
  16.6 25.1 %copy-start.9 = (bf16[4,1024,32]{1,2,0:T(8,128)(2,1)S(1)}, bf16[4,1024,32]{1,2,0:T(8,128)(2,1)}, u32[]{:S(2)}) copy-start(bf16[4,1024,32]{1,2,0:T(8,128)(2,1)} %param.10) | copy-start | bytes 786436
  16.6 26.7 %copy-start.15 = (s32[128]{0:T(128)S(1)}, s32[128]{0:T(128)}, u32[]{:S(2)}) copy-start(s32[128]{0:T(128)} %param.11) | copy-start | bytes 1540
  36.7 23.9 %copy-start.2 = (bf16[4,1024,256]{2,1,0:T(8,128)(2,1)S(1)}, bf16[4,1024,256]{2,1,0:T(8,128)(2,1)}, u32[]{:S(2)}) copy-start(bf16[4,1024,256]{2,1,0:T(8,128)(2,1)} %residual.1) | copy-start | bytes 6291460
  36.7 23.9 %all-to-all-start.1 = ((bf16[128,32,128]{2,1,0:T(8,128)(2,1)}), bf16[128,32,128]{2,1,0:T(8,128)(2,1)S(1)}, u32[]{:S(2)}, u32[]{:S(2)}) async-start(bf16[128,32,128]{2,1,0:T(8,128)(2,1)} %shard_map.83), calls=%async_computation.1 | async-start | bytes 2097152 | tf_op jit(solution)/shard_map/all_to_all | solution.py:19
  60.5 1.0 copy-start.10
  63.3 1.3 copy-start.7
  87.3 26.0 %all-to-all-start.3 = ((bf16[128,40,128]{2,1,0:T(8,128)(2,1)}), bf16[128,40,128]{2,1,0:T(8,128)(2,1)S(1)}, u32[]{:S(2)}, u32[]{:S(2)}) async-start(bf16[128,40,128]{2,1,0:T(8,128)(2,1)} %shard_map.86), calls=%async_computation.3 | async-start | bytes 2621440 | tf_op jit(solution)/shard_map/all_to_all | solution.py:19
  91.7 3.4 %copy-start = (bf16[4,1024,1024]{2,1,0:T(8,128)(2,1)S(1)}, bf16[4,1024,1024]{2,1,0:T(8,128)(2,1)}, u32[]{:S(2)}) copy-start(bf16[4,1024,1024]{2,1,0:T(8,128)(2,1)} %inverse.2) | copy-start | bytes 25165828
  95.1 1.6 copy-start.8
  100.2 2.0 %copy-start.5 = (f32[4,1024,256]{2,1,0:T(8,128)}, f32[4,1024,256]{2,1,0:T(8,128)S(1)}, u32[]{:S(2)}) copy-start(f32[4,1024,256]{2,1,0:T(8,128)S(1)} %get-tuple-element.14.local) | copy-start | bytes 12582916
  113.3 2.2 %copy-start.4 = (bf16[1024,2048]{1,0:T(8,128)(2,1)S(1)}, bf16[1024,2048]{1,0:T(8,128)(2,1)}, u32[]{:S(2)}) copy-start(bf16[1024,2048]{1,0:T(8,128)(2,1)} %inverse.3) | copy-start | bytes 12582916
  153.8 1.1 copy-start.3
  154.9 26.5 %all-to-all-start.5 = ((bf16[128,40,128]{2,1,0:T(8,128)(2,1)}), bf16[128,40,128]{2,1,0:T(8,128)(2,1)S(1)}, u32[]{:S(2)}, u32[]{:S(2)}) async-start(bf16[128,40,128]{2,1,0:T(8,128)(2,1)} %copy-done.3), calls=%async_computation.5 | async-start | bytes 2621440 | tf_op jit(solution)/shard_map/all_to_all | solution.py:19
  181.4 2.2 %copy-start.6 = (f32[4,1024,256]{2,1,0:T(8,128)S(1)}, f32[4,1024,256]{2,1,0:T(8,128)}, u32[]{:S(2)}) copy-start(f32[4,1024,256]{2,1,0:T(8,128)} %copy-done.5) | copy-start | bytes 12582916

commit v6 on v5

--- a/solution.py
+++ b/solution.py
@@ -26,6 +26,10 @@
         compiler_params=pltpu.CompilerParams(vmem_limit_bytes=VMEM_LIMIT),
         **kw,
     )
+
+
+def in_hbm(value):
+    return pltpu.with_memory_space_constraint(value, pltpu.HBM)
 
 
 def smem():
@@ -165,7 +169,7 @@
             start = (which * 2 + half) * HALF
             rows, inside = arrived_rows(table, sub, which, half, arrived)
             _, both = flags(table, sub, which)
-            theirs = prolong(arrived_modes[which, other, half * both], picked[1 + which, other])
+            theirs = prolong(arrived_modes[which * 2 + half * both, other], picked[1 + which, other])
             theirs = (0.5 * (rows + theirs)).astype(jnp.bfloat16).astype(jnp.float32)
             own = local[0, start : start + HALF] + added[start : start + HALF]
             own = (own * (1.0 - 0.5 * inside)).astype(jnp.bfloat16).astype(jnp.float32)
@@ -226,7 +230,7 @@
     lax.fori_loop(0, devices, forward, 0, unroll=4)
 
 
-def product_kernel(placed, inverse, packed, out, pairs, left, parts):
+def product_kernel(placed, inverse, packed, out, their_modes, pairs, left, parts):
     at_step = pl.program_id(0)
     groups = placed.shape[0] // 4
     tiles, steps = pairs.shape[0], parts.shape[0]
@@ -244,6 +248,21 @@
         lax.fori_loop(0, groups, step, 0)
         for tile in range(tiles):
             left[:, tile * LANE : (tile + 1) * LANE] = pairs[tile].astype(jnp.bfloat16)
+
+    @pl.when(at_step == 1)
+    def _():
+        def step(group, carry):
+            for inner in range(8):
+                row = pl.multiple_of(group * 8, 8) + inner
+                tile = placed[row, 2 * tiles :].astype(jnp.float32)
+                for kind in range(4):
+                    pairs[kind, pl.ds(row, 1)] = tile[4 + kind : 5 + kind]
+            return carry
+
+        lax.fori_loop(0, placed.shape[0] // 8, step, 0)
+        for kind in range(4):
+            value = pairs[kind, : placed.shape[0]].astype(jnp.bfloat16)
+            their_modes[kind] = value.reshape(their_modes.shape[1:])
 
     parts[at_step] = lax.dot_general(
         left[...], inverse[...], (((1,), (1,)), ((), ())), preferred_element_type=jnp.float32
@@ -356,6 +375,7 @@
     field = jax.ShapeDtypeStruct(residual.shape, jnp.bfloat16)
 
     turned_modes = modes.transpose(0, 2, 1)
+    residual = in_hbm(residual)
     offsets = block_offsets.T
     packed_spec = per_sub(2, HALF // 8, 4, 8, LANE)
     packed_shape = jax.ShapeDtypeStruct((count, 2, HALF // 8, 4, 8, LANE), jnp.bfloat16)
@@ -364,7 +384,7 @@
         pack_kernel,
         packed_shape,
         grid=(count,),
-        in_specs=[smem(), per_sub(trace_len, cases)],
+        in_specs=[smem(), per_sub(4 * HALF, cases)],
         out_specs=packed_spec,
     )(offsets, residual)
     arrived = exchange(packed, table)
@@ -378,7 +398,7 @@
     base = jnp.concatenate([jnp.broadcast_to(digits[None], (devices,) + digits.shape), shared], 1)
     weighted, payload = call(
         weigh_kernel,
-        (field, jax.ShapeDtypeStruct(base.shape, jnp.bfloat16)),
+        (pltpu.HBM(residual.shape, jnp.bfloat16), jax.ShapeDtypeStruct(base.shape, jnp.bfloat16)),
         grid=(count,),
         in_specs=[
             smem(),
@@ -392,17 +412,17 @@
             pltpu.VMEM((count * MODES, cases), jnp.float32),
             pltpu.VMEM((cases + 8, LANE), jnp.float32),
         ],
-    )(table, residual, turned_modes, arrived, base)
+    )(table, residual, turned_modes, arrived, in_hbm(base))
     received = spread(payload)
     weighted, received = lax.optimization_barrier((weighted, received))
 
     local_part, packed = call(
         local_kernel,
-        (jax.ShapeDtypeStruct(residual.shape, jnp.float32), packed_shape),
+        (pltpu.HBM(residual.shape, jnp.float32), packed_shape),
         grid=(count,),
         in_specs=[smem(), per_sub(trace_len, trace_len), per_sub(trace_len, cases)],
         out_specs=(per_sub(trace_len, cases), packed_spec),
-    )(offsets, interface_inverse, weighted)
+    )(offsets, in_hbm(interface_inverse), in_hbm(weighted))
     packed = packed.reshape(devices, 32, LANE)
 
     rows, columns = coarse_inverse.shape
@@ -417,26 +437,28 @@
         ],
     )(table, received)
     placed = spread(placed)
-    arrived_modes = placed[:, 2 * columns // LANE + 4 :].reshape(count, MODES, 2, 2, HALF)
-    arrived_modes = arrived_modes.transpose(2, 0, 3, 1, 4)
     steps = 4
     joined_shape = (devices, 2 * rows // LANE + 32, LANE)
-    joined = call(
+    modes_shape = (4, count, MODES, HALF)
+    joined, their_modes = call(
         product_kernel,
-        jax.ShapeDtypeStruct(joined_shape, jnp.bfloat16),
+        (
+            jax.ShapeDtypeStruct(joined_shape, jnp.bfloat16),
+            jax.ShapeDtypeStruct(modes_shape, jnp.bfloat16),
+        ),
         grid=(steps,),
         in_specs=[
             same(*placed.shape),
             pl.BlockSpec((rows // steps, columns), lambda step: (step, 0)),
             same(*packed.shape),
         ],
-        out_specs=same(*joined_shape),
+        out_specs=(same(*joined_shape), same(*modes_shape)),
         scratch_shapes=[
             pltpu.VMEM((columns // LANE, cases, LANE), jnp.float32),
             pltpu.VMEM((cases, columns), jnp.bfloat16),
             pltpu.VMEM((steps, cases, rows // steps), jnp.float32),
         ],
-    )(placed, coarse_inverse, packed)
+    )(placed, in_hbm(coarse_inverse), packed)
     joined = spread(joined)
     last = call(
         functools.partial(gather_kernel, row_blocks=lax.axis_size("row")),
@@ -458,14 +480,14 @@
             per_sub(trace_len, cases),
             per_sub(MODES, trace_len),
             same(*last.shape),
-            same(*arrived_modes.shape),
+            same(*modes_shape),
         ],
         out_specs=per_sub(trace_len, cases),
         scratch_shapes=[
             pltpu.VMEM((3, cases, LANE), jnp.float32),
             pltpu.VMEM((3, count, MODES, cases), jnp.bfloat16),
         ],
-    )(table, local_part, turned_modes, last, arrived_modes)
+    )(table, in_hbm(local_part), turned_modes, last, their_modes)
 
 
 def solution(mesh):

time: 188 us -> 186 us (0.989)
  blocking collectives: 44.3 us -> 70.1 us
  local copies, waits for them, and re-layouts: 19.2 us -> 1.36 us
  waiting for transfers between devices: 67 us -> 49.8 us
  Pallas kernels: 30 us -> 41.8 us
  starting transfers between devices: 25.3 us -> 20.5 us
    all_to_all x2 -> x3, blocking collectives: 44.3 us -> 70.1 us  [spread(): return lax.all_to_all(value, AXES, 0, 0, tiled=True)]
    all_to_all x4 -> x3, waiting for transfers between devices: 67 us -> 49.8 us  [spread(): return lax.all_to_all(value, AXES, 0, 0, tiled=True)]
    unnamed x32 -> x12, local copies, waits for them, and re-layouts: 16.9 us -> 0.7 us
    pallas_call x3, Pallas kernels: 8.75 us -> 17.8 us  [the longest x1 7.56 us: shards(): call(local_kernel, (pltpu.HBM(residual.shape, jnp.float32), packed_shape)...]
    all_to_all x4 -> x3, starting transfers between devices: 25.3 us -> 20.5 us  [spread(): return lax.all_to_all(value, AXES, 0, 0, tiled=True)]
  transfers between devices with their start and end apart: 4 -> 3, of which waited for: 4 -> 3; matrix products, arithmetic and copies ran while one was open for 2% -> 1% of each run, Pallas kernels for 2% -> 4%
where the time goes in v6:
time: 186 us; the launch traced here: 185 us
  blocking collectives  70.1 us (38%)
  waiting for transfers between devices  49.8 us (27%)
  Pallas kernels  41.8 us (22%)
  starting transfers between devices  20.5 us (11%)
    all_to_all x3, blocking collectives, spread(): return lax.all_to_all(value, AXES, 0, 0, tiled=True)  70.1 us
    all_to_all x3, waiting for transfers between devices, spread(): return lax.all_to_all(value, AXES, 0, 0, tiled=True)  49.8 us
    all_to_all x3, starting transfers between devices, spread(): return lax.all_to_all(value, AXES, 0, 0, tiled=True)  20.5 us
    pallas_call x1, Pallas kernels, shards(): call(local_kernel, (pltpu.HBM(residual.shape, jnp.float32), packed_shape)...  7.56 us
    pallas_call x1, Pallas kernels, shards(): call(scatter_kernel, jax.ShapeDtypeStruct((devices, 2 * columns // LANE +...  7.29 us
    pallas_call x1, Pallas kernels, shards(): call(functools.partial(gather_kernel, row_blocks=lax.axis_size('row')), j...  6.03 us
    pallas_call x1, Pallas kernels, shards(): call(product_kernel, (jax.ShapeDtypeStruct(joined_shape, jnp.bfloat16), j...  5.72 us
    pallas_call x1, Pallas kernels, shards(): call(finish_kernel, field, grid=(count,), in_specs=[smem(), per_sub(trace...  5.4 us
  transfers between devices with their start and end apart: 3, of which 3 were waited for; matrix products, arithmetic and copies ran while one was open for 1% of the time, Pallas kernels for 4%

profile of v6, /device:TPU:1, one launch (start us, length us, event | category | flops | bytes accessed | tf_op | source)
XLA Modules:
  0.0 185.2 jit_solution(342903958225987901)
XLA Ops:
  0.0 0.7 copy-done.1
  0.7 3.4 %shard_map.82 = bf16[4,2,16,4,8,128]{5,4,3,2,1,0:T(8,128)(2,1)} custom-call(s32[2,4]{1,0:T(2,128)S(1)} %bitcast.17, bf16[4,1024,256]{2,1,0:T(8,128)(2,1)} %residual.1), custom_call_target="tpu_custom_call" | custom-call | tf_op jit(solution)/shard_map/pallas_call | solution.py:383
  4.1 11.5 %all-to-all-start = ((bf16[128,32,128]{2,1,0:T(8,128)(2,1)}), bf16[128,32,128]{2,1,0:T(8,128)(2,1)S(1)}, u32[]{:S(2)}, u32[]{:S(2)}) async-start(bf16[128,32,128]{2,1,0:T(8,128)(2,1)} %bitcast.2), calls=%async_computation | async-start | bytes 2097152 | tf_op jit(solution)/shard_map/all_to_all | solution.py:19
  15.6 0.0 copy-done.3
  15.7 0.1 copy.13
  15.8 0.1 reshape.28
  15.8 0.0 copy-done.2
  15.9 0.1 copy.12
  16.0 0.1 reshape.27
  16.0 0.0 copy-done.4
  16.1 0.1 slice_reduce_fusion
  16.2 0.1 pad_add_fusion.table
  16.3 18.3 %all-to-all-done.chunks = bf16[128,32,128]{2,1,0:T(8,128)(2,1)S(1)} async-done(((bf16[128,32,128]{2,1,0:T(8,128)(2,1)}), bf16[128,32,128]{2,1,0:T(8,128)(2,1)S(1)}, u32[]{:S(2)}, u32[]{:S(2)}) %all-to-all-start) | async-done | bytes 1048608 | tf_op jit(solution)/shard_map/all_to_all | solution.py:19
  34.5 1.9 %shard_map.83 = bf16[128,32,128]{2,1,0:T(8,128)(2,1)} custom-call(s32[20]{0:T(128)S(1)} %pad_add_fusion.table, bf16[128,32,128]{2,1,0:T(8,128)(2,1)S(1)} %all-to-all-done.chunks), custom_call_target="tpu_custom_call" | custom-call | tf_op jit(solution)/shard_map/pallas_call | solution.py:89
  36.4 4.7 %all-to-all-start.1 = ((bf16[128,32,128]{2,1,0:T(8,128)(2,1)}), bf16[128,32,128]{2,1,0:T(8,128)(2,1)S(1)}, u32[]{:S(2)}, u32[]{:S(2)}) async-start(bf16[128,32,128]{2,1,0:T(8,128)(2,1)} %shard_map.83), calls=%async_computation.1 | async-start | bytes 2097152 | tf_op jit(solution)/shard_map/all_to_all | solution.py:19
  41.1 0.1 copy.14
  41.2 0.0 copy-done
  41.3 0.3 broadcast_select_fusion
  41.6 0.3 pad_maximum_fusion.1
  41.9 0.8 pad_maximum_fusion.base
  42.7 17.4 %all-to-all-done.1 = bf16[128,32,128]{2,1,0:T(8,128)(2,1)S(1)} async-done(((bf16[128,32,128]{2,1,0:T(8,128)(2,1)}), bf16[128,32,128]{2,1,0:T(8,128)(2,1)S(1)}, u32[]{:S(2)}, u32[]{:S(2)}) %all-to-all-start.1) | async-done | bytes 1048608 | tf_op jit(solution)/shard_map/all_to_all | solution.py:19
  60.1 4.5 %shard_map.84 = (bf16[4,1024,256]{2,1,0:T(8,128)(2,1)}, bf16[128,8,128]{2,1,0:T(8,128)(2,1)S(1)}) custom-call(s32[20]{0:T(128)S(1)} %pad_add_fusion.table, bf16[4,1024,256]{2,1,0:T(8,128)(2,1)} %residual.1, bf16[4,32,1024]{2,1,0:T(8,128)(2,1)S(1)} %bitcast.14, bf16[4,2,16,4,8,128]{5,4,3,2,1,0:T(8,128)(2,1)S(1)} %bitcast.12, ...), custom_call_target="tpu_custom_call" | custom-call | tf_op jit(solution)/shard_map/pallas_call | solution.py:399
  64.6 15.5 %all_to_all.30.received = bf16[128,8,128]{2,1,0:T(8,128)(2,1)S(1)} all-to-all(bf16[128,8,128]{2,1,0:T(8,128)(2,1)S(1)} %get-tuple-element.14), channel_id=1, replica_groups=mesh['row'=16,'col'=8] {'row','col'}, dimensions={0} | all-to-all | bytes 524288 | tf_op jit(solution)/shard_map/all_to_all | solution.py:19
  80.1 7.3 %shard_map.86 = bf16[128,40,128]{2,1,0:T(8,128)(2,1)} custom-call(s32[20]{0:T(128)S(1)} %pad_add_fusion.table, bf16[128,8,128]{2,1,0:T(8,128)(2,1)S(1)} %all_to_all.30.received), custom_call_target="tpu_custom_call" | custom-call | tf_op jit(solution)/shard_map/pallas_call | solution.py:429
  87.4 4.3 %all-to-all-start.3 = ((bf16[128,40,128]{2,1,0:T(8,128)(2,1)}), bf16[128,40,128]{2,1,0:T(8,128)(2,1)S(1)}, u32[]{:S(2)}, u32[]{:S(2)}) async-start(bf16[128,40,128]{2,1,0:T(8,128)(2,1)} %shard_map.86), calls=%async_computation.3 | async-start | bytes 2621440 | tf_op jit(solution)/shard_map/all_to_all | solution.py:19
  91.7 7.6 %shard_map.85 = (f32[4,1024,256]{2,1,0:T(8,128)}, bf16[4,2,16,4,8,128]{5,4,3,2,1,0:T(8,128)(2,1)S(1)}) custom-call(s32[2,4]{1,0:T(2,128)S(1)} %bitcast.18, bf16[4,1024,1024]{2,1,0:T(8,128)(2,1)} %inverse.2, bf16[4,1024,256]{2,1,0:T(8,128)(2,1)} %get-tuple-element.15.weighted), custom_call_target="tpu_custom_call" | custom-call | tf_op jit(solution)/shard_map/pallas_call | solution.py:419
  99.2 14.1 %all-to-all-done.3.placed = bf16[128,40,128]{2,1,0:T(8,128)(2,1)S(1)} async-done(((bf16[128,40,128]{2,1,0:T(8,128)(2,1)}), bf16[128,40,128]{2,1,0:T(8,128)(2,1)S(1)}, u32[]{:S(2)}, u32[]{:S(2)}) %all-to-all-start.3) | async-done | bytes 1310752 | tf_op jit(solution)/shard_map/all_to_all | solution.py:19
  113.4 5.7 %shard_map.87 = (bf16[128,48,128]{2,1,0:T(8,128)(2,1)S(1)}, bf16[4,4,32,128]{3,2,1,0:T(8,128)(2,1)S(1)}) custom-call(bf16[128,40,128]{2,1,0:T(8,128)(2,1)S(1)} %all-to-all-done.3.placed, bf16[1024,2048]{1,0:T(8,128)(2,1)} %inverse.3, bf16[128,32,128]{2,1,0:T(8,128)(2,1)S(1)} %bitcast.16), custom_call_target="tpu_custom_call" | custom-call | tf_op jit(solution)/shard_map/pallas_call | solution.py:443
  119.1 28.8 %all_to_all.31.partial = bf16[128,48,128]{2,1,0:T(8,128)(2,1)S(1)} all-to-all(bf16[128,48,128]{2,1,0:T(8,128)(2,1)S(1)} %get-tuple-element.19), channel_id=1, replica_groups=mesh['row'=16,'col'=8] {'row','col'}, dimensions={0} | all-to-all | bytes 3145728 | tf_op jit(solution)/shard_map/all_to_all | solution.py:19
  147.9 6.0 %shard_map.88 = bf16[128,40,128]{2,1,0:T(8,128)(2,1)S(1)} custom-call(s32[20]{0:T(128)S(1)} %pad_add_fusion.table, bf16[128,8,128]{2,1,0:T(8,128)(2,1)S(1)} %all_to_all.30.received, bf16[128,48,128]{2,1,0:T(8,128)(2,1)S(1)} %all_to_all.31.partial), custom_call_target="tpu_custom_call" | custom-call | tf_op jit(solution)/shard_map/pallas_call | solution.py:463
  153.9 25.9 %all_to_all.32 = bf16[128,40,128]{2,1,0:T(8,128)(2,1)S(1)} all-to-all(bf16[128,40,128]{2,1,0:T(8,128)(2,1)S(1)} %shard_map.88), channel_id=1, replica_groups=mesh['row'=16,'col'=8] {'row','col'}, dimensions={0} | all-to-all | bytes 2621440 | tf_op jit(solution)/shard_map/all_to_all | solution.py:19
  179.8 5.4 %shard_map.89 = bf16[4,1024,256]{2,1,0:T(8,128)(2,1)} custom-call(s32[20]{0:T(128)S(1)} %pad_add_fusion.table, f32[4,1024,256]{2,1,0:T(8,128)} %get-tuple-element.16.local, bf16[4,32,1024]{2,1,0:T(8,128)(2,1)S(1)} %bitcast.15, bf16[4,2,16,5,8,128]{5,4,3,2,1,0:T(8,128)(2,1)S(1)} %bitcast.11, bf16[4,4,32,128]{3,2,1,0:T(8,128)(2,1)S(1)} %get-tuple-element.20.arrived_modes), custom_call_target="tpu_custom_call" | custom-call | tf_op jit(solution)/shard_map/pallas_call | solution.py:474
  (15 shorter events, 0.2 us)
Async XLA Ops:
  0.0 0.7 copy-start.1
  0.7 15.0 %copy-start.3 = (s32[4,2]{0,1:T(2,128)S(1)}, s32[4,2]{0,1:T(2,128)}, u32[]{:S(2)}) copy-start(s32[4,2]{0,1:T(2,128)} %param.14) | copy-start | bytes 100
  0.7 15.2 %copy-start.2 = (s32[4,2]{0,1:T(2,128)S(1)}, s32[4,2]{0,1:T(2,128)}, u32[]{:S(2)}) copy-start(s32[4,2]{0,1:T(2,128)} %param.15) | copy-start | bytes 100
  0.7 15.4 %copy-start.4 = (s32[4,2]{0,1:T(2,128)S(1)}, s32[4,2]{0,1:T(2,128)}, u32[]{:S(2)}) copy-start(s32[4,2]{0,1:T(2,128)} %param.13) | copy-start | bytes 100
  4.1 30.4 %all-to-all-start = ((bf16[128,32,128]{2,1,0:T(8,128)(2,1)}), bf16[128,32,128]{2,1,0:T(8,128)(2,1)S(1)}, u32[]{:S(2)}, u32[]{:S(2)}) async-start(bf16[128,32,128]{2,1,0:T(8,128)(2,1)} %bitcast.2), calls=%async_computation | async-start | bytes 2097152 | tf_op jit(solution)/shard_map/all_to_all | solution.py:19
  16.3 24.9 %copy-start = (bf16[4,1024,32]{1,2,0:T(8,128)(2,1)S(1)}, bf16[4,1024,32]{1,2,0:T(8,128)(2,1)}, u32[]{:S(2)}) copy-start(bf16[4,1024,32]{1,2,0:T(8,128)(2,1)} %param.10) | copy-start | bytes 786436
  16.3 25.0 %copy-start.5 = (s32[128]{0:T(128)S(1)}, s32[128]{0:T(128)}, u32[]{:S(2)}) copy-start(s32[128]{0:T(128)} %param.11) | copy-start | bytes 1540
  36.4 23.7 %all-to-all-start.1 = ((bf16[128,32,128]{2,1,0:T(8,128)(2,1)}), bf16[128,32,128]{2,1,0:T(8,128)(2,1)S(1)}, u32[]{:S(2)}, u32[]{:S(2)}) async-start(bf16[128,32,128]{2,1,0:T(8,128)(2,1)} %shard_map.83), calls=%async_computation.1 | async-start | bytes 2097152 | tf_op jit(solution)/shard_map/all_to_all | solution.py:19
  87.4 26.0 %all-to-all-start.3 = ((bf16[128,40,128]{2,1,0:T(8,128)(2,1)}), bf16[128,40,128]{2,1,0:T(8,128)(2,1)S(1)}, u32[]{:S(2)}, u32[]{:S(2)}) async-start(bf16[128,40,128]{2,1,0:T(8,128)(2,1)} %shard_map.86), calls=%async_computation.3 | async-start | bytes 2621440 | tf_op jit(solution)/shard_map/all_to_all | solution.py:19

commit v7 on v6

--- a/solution.py
+++ b/solution.py
@@ -11,7 +11,7 @@
 MODES = 32
 HALF = 128
 LANE = 128
-GROUP = 8
+GROUP = 64
 VMEM_LIMIT = 16 * 1024 * 1024
 
 
@@ -63,8 +63,24 @@
                 packed[0, half, :, which * 2 + lane] = tile.astype(jnp.bfloat16)
 
 
-def pack_kernel(offsets, field, packed):
-    store_blocks(offsets, pl.program_id(0), lambda start: field[0, pl.ds(start, HALF)], packed)
+def pack_kernel(offsets, tiles, packed, done):
+    size = HALF // 8
+    copies = []
+    for sub in range(tiles.shape[0]):
+        for which in range(2):
+            second = jnp.bitwise_and(jnp.right_shift(offsets[which, sub], 7), 1)
+            for half in range(2):
+                start = which * 2 * size + (second * size if half == 0 else size)
+                copies.append(
+                    pltpu.make_async_copy(
+                        tiles.at[sub, pl.ds(start, size)],
+                        packed.at[sub, half, :, pl.ds(which * 2, 2)],
+                        done.at[sub, which, half],
+                    )
+                )
+                copies[-1].start()
+    for copy in copies:
+        copy.wait()
 
 
 def local_kernel(offsets, inverse, weighted, local, packed):
@@ -375,18 +391,19 @@
     field = jax.ShapeDtypeStruct(residual.shape, jnp.bfloat16)
 
     turned_modes = modes.transpose(0, 2, 1)
-    residual = in_hbm(residual)
     offsets = block_offsets.T
     packed_spec = per_sub(2, HALF // 8, 4, 8, LANE)
     packed_shape = jax.ShapeDtypeStruct((count, 2, HALF // 8, 4, 8, LANE), jnp.bfloat16)
 
+    tiles = residual.reshape(count, trace_len // 8, 8, 2, LANE).transpose(0, 1, 3, 2, 4)
+    hbm = pl.BlockSpec(memory_space=pltpu.HBM)
     packed = call(
         pack_kernel,
-        packed_shape,
-        grid=(count,),
-        in_specs=[smem(), per_sub(4 * HALF, cases)],
-        out_specs=packed_spec,
-    )(offsets, residual)
+        pltpu.HBM(packed_shape.shape, jnp.bfloat16),
+        in_specs=[smem(), hbm],
+        out_specs=hbm,
+        scratch_shapes=[pltpu.SemaphoreType.DMA((count, 2, 2))],
+    )(offsets, in_hbm(tiles))
     arrived = exchange(packed, table)
     digits = jnp.stack([coarse_map // LANE, coarse_map % LANE]).astype(jnp.bfloat16)
     digits = jnp.concatenate([jnp.zeros_like(digits), digits], 0)
@@ -418,7 +435,10 @@
 
     local_part, packed = call(
         local_kernel,
-        (pltpu.HBM(residual.shape, jnp.float32), packed_shape),
+        (
+            pltpu.HBM(residual.shape, jnp.float32),
+            pltpu.HBM(packed_shape.shape, jnp.bfloat16),
+        ),
         grid=(count,),
         in_specs=[smem(), per_sub(trace_len, trace_len), per_sub(trace_len, cases)],
         out_specs=(per_sub(trace_len, cases), packed_spec),
@@ -458,7 +478,7 @@
             pltpu.VMEM((cases, columns), jnp.bfloat16),
             pltpu.VMEM((steps, cases, rows // steps), jnp.float32),
         ],
-    )(placed, in_hbm(coarse_inverse), packed)
+    )(placed, in_hbm(coarse_inverse), in_hbm(packed))
     joined = spread(joined)
     last = call(
         functools.partial(gather_kernel, row_blocks=lax.axis_size("row")),

time: 186 us -> 211 us (1.13)
  Pallas kernels: 41.8 us -> 66.8 us
    pallas_call x2, Pallas kernels: 11 us -> 41.2 us  [the longest x1 33.6 us: shards(): call(pack_kernel, pltpu.HBM(packed_shape.shape, jnp.bfloat16), in_specs=[...]
    pallas_call x1, Pallas kernels: 7.29 us -> 4.92 us  [shards(): call(scatter_kernel, jax.ShapeDtypeStruct((devices, 2 * columns // LANE +...]
    pallas_call x1, Pallas kernels: 6.03 us -> 3.85 us  [shards(): call(functools.partial(gather_kernel, row_blocks=lax.axis_size('row')), j...]
  transfers between devices with their start and end apart: 3 -> 3, of which waited for: 3 -> 3; matrix products, arithmetic and copies ran while one was open for 1% -> 2% of each run, Pallas kernels for 4% -> 4%
where the time goes in v7:
time: 211 us; the launch traced here: 210 us
  blocking collectives  70.1 us (33%)
  Pallas kernels  66.8 us (32%)
  waiting for transfers between devices  48.1 us (23%)
  starting transfers between devices  20.6 us (10%)
  local copies, waits for them, and re-layouts  2.92 us (1%)
    all_to_all x3, blocking collectives, spread(): return lax.all_to_all(value, AXES, 0, 0, tiled=True)  70.1 us
    all_to_all x3, waiting for transfers between devices, spread(): return lax.all_to_all(value, AXES, 0, 0, tiled=True)  48.1 us
    pallas_call x1, Pallas kernels, shards(): call(pack_kernel, pltpu.HBM(packed_shape.shape, jnp.bfloat16), in_specs=[...  33.6 us
    all_to_all x3, starting transfers between devices, spread(): return lax.all_to_all(value, AXES, 0, 0, tiled=True)  20.6 us
    pallas_call x1, Pallas kernels, shards(): call(local_kernel, (pltpu.HBM(residual.shape, jnp.float32), pltpu.HBM(pac...  7.66 us
    pallas_call x1, Pallas kernels, shards(): call(product_kernel, (jax.ShapeDtypeStruct(joined_shape, jnp.bfloat16), j...  6.04 us
    pallas_call x1, Pallas kernels, shards(): call(finish_kernel, field, grid=(count,), in_specs=[smem(), per_sub(trace...  5.41 us
    pallas_call x1, Pallas kernels, shards(): call(scatter_kernel, jax.ShapeDtypeStruct((devices, 2 * columns // LANE +...  4.92 us
  transfers between devices with their start and end apart: 3, of which 3 were waited for; matrix products, arithmetic and copies ran while one was open for 2% of the time, Pallas kernels for 4%

profile of v7, /device:TPU:1, one launch (start us, length us, event | category | flops | bytes accessed | tf_op | source)
XLA Modules:
  0.0 210.2 jit_solution(18233102666547729865)
XLA Ops:
  0.0 0.7 copy-done.2
  0.7 33.6 %shard_map.82 = bf16[4,2,16,4,8,128]{5,4,3,2,1,0:T(8,128)(2,1)} custom-call(s32[2,4]{1,0:T(2,128)S(1)} %bitcast.20, bf16[4,128,2,8,128]{4,3,2,1,0:T(8,128)(2,1)} %bitcast.14), custom_call_target="tpu_custom_call" | custom-call | tf_op jit(solution)/shard_map/pallas_call | solution.py:400
  34.3 11.5 %all-to-all-start = ((bf16[128,32,128]{2,1,0:T(8,128)(2,1)}), bf16[128,32,128]{2,1,0:T(8,128)(2,1)S(1)}, u32[]{:S(2)}, u32[]{:S(2)}) async-start(bf16[128,32,128]{2,1,0:T(8,128)(2,1)} %bitcast.22), calls=%async_computation | async-start | bytes 2097152 | tf_op jit(solution)/shard_map/all_to_all | solution.py:19
  45.8 0.0 copy-done.4
  45.8 0.1 copy.13
  45.9 0.1 reshape.31
  46.0 0.0 copy-done.3
  46.0 0.1 copy.12
  46.1 0.1 reshape.30
  46.2 0.1 slice_reduce_fusion
  46.3 0.1 pad_add_fusion.table
  46.4 18.3 %all-to-all-done.chunks = bf16[128,32,128]{2,1,0:T(8,128)(2,1)S(1)} async-done(((bf16[128,32,128]{2,1,0:T(8,128)(2,1)}), bf16[128,32,128]{2,1,0:T(8,128)(2,1)S(1)}, u32[]{:S(2)}, u32[]{:S(2)}) %all-to-all-start) | async-done | bytes 1048608 | tf_op jit(solution)/shard_map/all_to_all | solution.py:19
  64.7 1.9 shard_map.83
  66.5 4.8 %all-to-all-start.1 = ((bf16[128,32,128]{2,1,0:T(8,128)(2,1)}), bf16[128,32,128]{2,1,0:T(8,128)(2,1)S(1)}, u32[]{:S(2)}, u32[]{:S(2)}) async-start(bf16[128,32,128]{2,1,0:T(8,128)(2,1)} %shard_map.83), calls=%async_computation.1 | async-start | bytes 2097152 | tf_op jit(solution)/shard_map/all_to_all | solution.py:19
  71.3 0.1 copy.14
  71.4 0.7 slice.18
  72.1 0.9 reshape.35
  73.1 0.3 broadcast_select_fusion
  73.4 0.3 pad_maximum_fusion.1
  73.7 0.8 pad_maximum_fusion.base
  74.5 15.8 %all-to-all-done.1 = bf16[128,32,128]{2,1,0:T(8,128)(2,1)S(1)} async-done(((bf16[128,32,128]{2,1,0:T(8,128)(2,1)}), bf16[128,32,128]{2,1,0:T(8,128)(2,1)S(1)}, u32[]{:S(2)}, u32[]{:S(2)}) %all-to-all-start.1) | async-done | bytes 1048608 | tf_op jit(solution)/shard_map/all_to_all | solution.py:19
  90.4 3.5 %shard_map.84 = (bf16[4,1024,256]{2,1,0:T(8,128)(2,1)}, bf16[128,8,128]{2,1,0:T(8,128)(2,1)S(1)}) custom-call(s32[20]{0:T(128)S(1)} %pad_add_fusion.table, bf16[4,1024,256]{2,1,0:T(8,128)(2,1)S(1)} %copy-done, bf16[4,32,1024]{2,1,0:T(8,128)(2,1)S(1)} %bitcast.18, bf16[4,2,16,4,8,128]{5,4,3,2,1,0:T(8,128)(2,1)S(1)} %bitcast.16, ...), custom_call_target="tpu_custom_call" | custom-call | tf_op jit(solution)/shard_map/pallas_call | solution.py:416
  93.9 15.5 %all_to_all.30.received = bf16[128,8,128]{2,1,0:T(8,128)(2,1)S(1)} all-to-all(bf16[128,8,128]{2,1,0:T(8,128)(2,1)S(1)} %get-tuple-element.14), channel_id=1, replica_groups=mesh['row'=16,'col'=8] {'row','col'}, dimensions={0} | all-to-all | bytes 524288 | tf_op jit(solution)/shard_map/all_to_all | solution.py:19
  109.4 4.9 %shard_map.86 = bf16[128,40,128]{2,1,0:T(8,128)(2,1)} custom-call(s32[20]{0:T(128)S(1)} %pad_add_fusion.table, bf16[128,8,128]{2,1,0:T(8,128)(2,1)S(1)} %all_to_all.30.received), custom_call_target="tpu_custom_call" | custom-call | tf_op jit(solution)/shard_map/pallas_call | solution.py:449
  114.3 4.3 %all-to-all-start.3 = ((bf16[128,40,128]{2,1,0:T(8,128)(2,1)}), bf16[128,40,128]{2,1,0:T(8,128)(2,1)S(1)}, u32[]{:S(2)}, u32[]{:S(2)}) async-start(bf16[128,40,128]{2,1,0:T(8,128)(2,1)} %shard_map.86), calls=%async_computation.3 | async-start | bytes 2621440 | tf_op jit(solution)/shard_map/all_to_all | solution.py:19
  118.6 7.7 %shard_map.85 = (f32[4,1024,256]{2,1,0:T(8,128)}, bf16[4,2,16,4,8,128]{5,4,3,2,1,0:T(8,128)(2,1)}) custom-call(s32[2,4]{1,0:T(2,128)S(1)} %bitcast.21, bf16[4,1024,1024]{2,1,0:T(8,128)(2,1)} %inverse.2, bf16[4,1024,256]{2,1,0:T(8,128)(2,1)} %get-tuple-element.15.weighted), custom_call_target="tpu_custom_call" | custom-call | tf_op jit(solution)/shard_map/pallas_call | solution.py:436
  126.3 14.0 %all-to-all-done.3.placed = bf16[128,40,128]{2,1,0:T(8,128)(2,1)S(1)} async-done(((bf16[128,40,128]{2,1,0:T(8,128)(2,1)}), bf16[128,40,128]{2,1,0:T(8,128)(2,1)S(1)}, u32[]{:S(2)}, u32[]{:S(2)}) %all-to-all-start.3) | async-done | bytes 1310752 | tf_op jit(solution)/shard_map/all_to_all | solution.py:19
  140.3 6.0 %shard_map.87 = (bf16[128,48,128]{2,1,0:T(8,128)(2,1)S(1)}, bf16[4,4,32,128]{3,2,1,0:T(8,128)(2,1)S(1)}) custom-call(bf16[128,40,128]{2,1,0:T(8,128)(2,1)S(1)} %all-to-all-done.3.placed, bf16[1024,2048]{1,0:T(8,128)(2,1)} %inverse.3, bf16[128,32,128]{2,1,0:T(8,128)(2,1)} %bitcast.23), custom_call_target="tpu_custom_call" | custom-call | tf_op jit(solution)/shard_map/pallas_call | solution.py:463
  146.3 28.8 %all_to_all.31.partial = bf16[128,48,128]{2,1,0:T(8,128)(2,1)S(1)} all-to-all(bf16[128,48,128]{2,1,0:T(8,128)(2,1)S(1)} %get-tuple-element.19), channel_id=1, replica_groups=mesh['row'=16,'col'=8] {'row','col'}, dimensions={0} | all-to-all | bytes 3145728 | tf_op jit(solution)/shard_map/all_to_all | solution.py:19
  175.1 3.8 %shard_map.88 = bf16[128,40,128]{2,1,0:T(8,128)(2,1)S(1)} custom-call(s32[20]{0:T(128)S(1)} %pad_add_fusion.table, bf16[128,8,128]{2,1,0:T(8,128)(2,1)S(1)} %all_to_all.30.received, bf16[128,48,128]{2,1,0:T(8,128)(2,1)S(1)} %all_to_all.31.partial), custom_call_target="tpu_custom_call" | custom-call | tf_op jit(solution)/shard_map/pallas_call | solution.py:483
  179.0 25.9 %all_to_all.32 = bf16[128,40,128]{2,1,0:T(8,128)(2,1)S(1)} all-to-all(bf16[128,40,128]{2,1,0:T(8,128)(2,1)S(1)} %shard_map.88), channel_id=1, replica_groups=mesh['row'=16,'col'=8] {'row','col'}, dimensions={0} | all-to-all | bytes 2621440 | tf_op jit(solution)/shard_map/all_to_all | solution.py:19
  204.8 5.4 %shard_map.89 = bf16[4,1024,256]{2,1,0:T(8,128)(2,1)} custom-call(s32[20]{0:T(128)S(1)} %pad_add_fusion.table, f32[4,1024,256]{2,1,0:T(8,128)} %get-tuple-element.16.local, bf16[4,32,1024]{2,1,0:T(8,128)(2,1)S(1)} %bitcast.19, bf16[4,2,16,5,8,128]{5,4,3,2,1,0:T(8,128)(2,1)S(1)} %bitcast.15, bf16[4,4,32,128]{3,2,1,0:T(8,128)(2,1)S(1)} %get-tuple-element.20.arrived_modes), custom_call_target="tpu_custom_call" | custom-call | tf_op jit(solution)/shard_map/pallas_call | solution.py:494
  (17 shorter events, 0.1 us)
Async XLA Ops:
  0.0 0.7 copy-start.2
  0.7 45.1 %copy-start.4 = (s32[4,2]{0,1:T(2,128)S(1)}, s32[4,2]{0,1:T(2,128)}, u32[]{:S(2)}) copy-start(s32[4,2]{0,1:T(2,128)} %param.14) | copy-start | bytes 100
  0.7 45.3 %copy-start.3 = (s32[4,2]{0,1:T(2,128)S(1)}, s32[4,2]{0,1:T(2,128)}, u32[]{:S(2)}) copy-start(s32[4,2]{0,1:T(2,128)} %param.15) | copy-start | bytes 100
  0.7 45.5 %copy-start.5 = (s32[4,2]{0,1:T(2,128)S(1)}, s32[4,2]{0,1:T(2,128)}, u32[]{:S(2)}) copy-start(s32[4,2]{0,1:T(2,128)} %param.13) | copy-start | bytes 100
  34.3 30.4 %all-to-all-start = ((bf16[128,32,128]{2,1,0:T(8,128)(2,1)}), bf16[128,32,128]{2,1,0:T(8,128)(2,1)S(1)}, u32[]{:S(2)}, u32[]{:S(2)}) async-start(bf16[128,32,128]{2,1,0:T(8,128)(2,1)} %bitcast.22), calls=%async_computation | async-start | bytes 2097152 | tf_op jit(solution)/shard_map/all_to_all | solution.py:19
  46.4 25.1 %copy-start.1 = (bf16[4,1024,32]{1,2,0:T(8,128)(2,1)S(1)}, bf16[4,1024,32]{1,2,0:T(8,128)(2,1)}, u32[]{:S(2)}) copy-start(bf16[4,1024,32]{1,2,0:T(8,128)(2,1)} %param.10) | copy-start | bytes 786436
  46.4 26.7 %copy-start.6 = (s32[128]{0:T(128)S(1)}, s32[128]{0:T(128)}, u32[]{:S(2)}) copy-start(s32[128]{0:T(128)} %param.11) | copy-start | bytes 1540
  66.5 23.9 %copy-start = (bf16[4,1024,256]{2,1,0:T(8,128)(2,1)S(1)}, bf16[4,1024,256]{2,1,0:T(8,128)(2,1)}, u32[]{:S(2)}) copy-start(bf16[4,1024,256]{2,1,0:T(8,128)(2,1)} %residual.1) | copy-start | bytes 6291460
  66.5 23.9 %all-to-all-start.1 = ((bf16[128,32,128]{2,1,0:T(8,128)(2,1)}), bf16[128,32,128]{2,1,0:T(8,128)(2,1)S(1)}, u32[]{:S(2)}, u32[]{:S(2)}) async-start(bf16[128,32,128]{2,1,0:T(8,128)(2,1)} %shard_map.83), calls=%async_computation.1 | async-start | bytes 2097152 | tf_op jit(solution)/shard_map/all_to_all | solution.py:19
  114.3 26.0 %all-to-all-start.3 = ((bf16[128,40,128]{2,1,0:T(8,128)(2,1)}), bf16[128,40,128]{2,1,0:T(8,128)(2,1)S(1)}, u32[]{:S(2)}, u32[]{:S(2)}) async-start(bf16[128,40,128]{2,1,0:T(8,128)(2,1)} %shard_map.86), calls=%async_computation.3 | async-start | bytes 2621440 | tf_op jit(solution)/shard_map/all_to_all | solution.py:19

commit v8 on v7

--- a/solution.py
+++ b/solution.py
@@ -53,6 +53,7 @@
 
 
 def store_blocks(offsets, sub, load, packed):
+    before = packed.shape[3] - 4
     for which in range(2):
         second = jnp.bitwise_and(jnp.right_shift(offsets[which, sub], 7), 1)
         for half in range(2):
@@ -60,26 +61,35 @@
             rows = load(pl.multiple_of(start, HALF)).astype(jnp.float32)
             for lane in range(2):
                 tile = rows[:, lane * LANE : (lane + 1) * LANE].reshape(HALF // 8, 8, LANE)
-                packed[0, half, :, which * 2 + lane] = tile.astype(jnp.bfloat16)
-
-
-def pack_kernel(offsets, tiles, packed, done):
+                packed[0, half, :, before + which * 2 + lane] = tile.astype(jnp.bfloat16)
+
+
+def pack_kernel(offsets, tiles, packed, staged, read, written):
     size = HALF // 8
-    copies = []
+    reads, writes = [], []
     for sub in range(tiles.shape[0]):
         for which in range(2):
             second = jnp.bitwise_and(jnp.right_shift(offsets[which, sub], 7), 1)
             for half in range(2):
                 start = which * 2 * size + (second * size if half == 0 else size)
-                copies.append(
+                at = (sub * 2 + which) * 2 + half
+                reads.append(
                     pltpu.make_async_copy(
-                        tiles.at[sub, pl.ds(start, size)],
-                        packed.at[sub, half, :, pl.ds(which * 2, 2)],
-                        done.at[sub, which, half],
+                        tiles.at[sub, pl.ds(start, size)], staged.at[at], read.at[at]
                     )
                 )
-                copies[-1].start()
-    for copy in copies:
+                reads[-1].start()
+                writes.append(
+                    pltpu.make_async_copy(
+                        staged.at[at],
+                        packed.at[sub, half, :, pl.ds(which * 2, 2)],
+                        written.at[at],
+                    )
+                )
+    for first, second in zip(reads, writes):
+        first.wait()
+        second.start()
+    for copy in writes:
         copy.wait()
 
 
@@ -246,7 +256,9 @@
     lax.fori_loop(0, devices, forward, 0, unroll=4)
 
 
-def product_kernel(placed, inverse, packed, out, their_modes, pairs, left, parts):
+def product_kernel(
+    placed, inverse, packed, out, their_modes, pairs, left, parts, own, written
+):
     at_step = pl.program_id(0)
     groups = placed.shape[0] // 4
     tiles, steps = pairs.shape[0], parts.shape[0]
@@ -286,7 +298,7 @@
 
     @pl.when(at_step == steps - 1)
     def _():
-        size = steps * parts.shape[2] // LANE * 2
+        size = own.shape[1]
 
         def step(group, carry):
             at = pl.multiple_of(group * 8, 8)
@@ -297,11 +309,13 @@
             ]
             for inner in range(4):
                 rows = jnp.concatenate([tile[2 * inner : 2 * inner + 2] for tile in tall], 0)
-                out[group * 4 + inner, :size] = rows.astype(jnp.bfloat16)
-                out[group * 4 + inner, size:] = packed[group * 4 + inner]
+                own[group * 4 + inner] = rows.astype(jnp.bfloat16)
             return carry
 
         lax.fori_loop(0, groups, step, 0)
+        copy = pltpu.make_async_copy(own, out.at[:, :size], written)
+        copy.start()
+        copy.wait()
 
 
 def gather_kernel(table, received, partial, out, solved, chosen_rows, *, row_blocks):
@@ -392,7 +406,6 @@
 
     turned_modes = modes.transpose(0, 2, 1)
     offsets = block_offsets.T
-    packed_spec = per_sub(2, HALF // 8, 4, 8, LANE)
     packed_shape = jax.ShapeDtypeStruct((count, 2, HALF // 8, 4, 8, LANE), jnp.bfloat16)
 
     tiles = residual.reshape(count, trace_len // 8, 8, 2, LANE).transpose(0, 1, 3, 2, 4)
@@ -402,7 +415,11 @@
         pltpu.HBM(packed_shape.shape, jnp.bfloat16),
         in_specs=[smem(), hbm],
         out_specs=hbm,
-        scratch_shapes=[pltpu.SemaphoreType.DMA((count, 2, 2))],
+        scratch_shapes=[
+            pltpu.VMEM((count * 4, HALF // 8, 2, 8, LANE), jnp.bfloat16),
+            pltpu.SemaphoreType.DMA((count * 4,)),
+            pltpu.SemaphoreType.DMA((count * 4,)),
+        ],
     )(offsets, in_hbm(tiles))
     arrived = exchange(packed, table)
     digits = jnp.stack([coarse_map // LANE, coarse_map % LANE]).astype(jnp.bfloat16)
@@ -433,19 +450,24 @@
     received = spread(payload)
     weighted, received = lax.optimization_barrier((weighted, received))
 
+    rows, columns = coarse_inverse.shape
+    own_tiles = 2 * rows // LANE // 8
     local_part, packed = call(
         local_kernel,
         (
             pltpu.HBM(residual.shape, jnp.float32),
-            pltpu.HBM(packed_shape.shape, jnp.bfloat16),
+            pltpu.HBM((count, 2, HALF // 8, own_tiles + 4, 8, LANE), jnp.bfloat16),
         ),
         grid=(count,),
         in_specs=[smem(), per_sub(trace_len, trace_len), per_sub(trace_len, cases)],
-        out_specs=(per_sub(trace_len, cases), packed_spec),
+        out_specs=(
+            per_sub(trace_len, cases),
+            per_sub(2, HALF // 8, own_tiles + 4, 8, LANE),
+        ),
     )(offsets, in_hbm(interface_inverse), in_hbm(weighted))
-    packed = packed.reshape(devices, 32, LANE)
-
-    rows, columns = coarse_inverse.shape
+    joined_shape = (devices, 8 * own_tiles + 32, LANE)
+    packed = packed.reshape(joined_shape)
+
     placed = call(
         scatter_kernel,
         jax.ShapeDtypeStruct((devices, 2 * columns // LANE + 8, LANE), jnp.bfloat16),
@@ -458,25 +480,27 @@
     )(table, received)
     placed = spread(placed)
     steps = 4
-    joined_shape = (devices, 2 * rows // LANE + 32, LANE)
     modes_shape = (4, count, MODES, HALF)
     joined, their_modes = call(
         product_kernel,
         (
-            jax.ShapeDtypeStruct(joined_shape, jnp.bfloat16),
+            pltpu.HBM(joined_shape, jnp.bfloat16),
             jax.ShapeDtypeStruct(modes_shape, jnp.bfloat16),
         ),
         grid=(steps,),
         in_specs=[
             same(*placed.shape),
             pl.BlockSpec((rows // steps, columns), lambda step: (step, 0)),
-            same(*packed.shape),
-        ],
-        out_specs=(same(*joined_shape), same(*modes_shape)),
+            hbm,
+        ],
+        out_specs=(hbm, same(*modes_shape)),
+        input_output_aliases={2: 0},
         scratch_shapes=[
             pltpu.VMEM((columns // LANE, cases, LANE), jnp.float32),
             pltpu.VMEM((cases, columns), jnp.bfloat16),
             pltpu.VMEM((steps, cases, rows // steps), jnp.float32),
+            pltpu.VMEM((devices, 8 * own_tiles, LANE), jnp.bfloat16),
+            pltpu.SemaphoreType.DMA(()),
         ],
     )(placed, in_hbm(coarse_inverse), in_hbm(packed))
     joined = spread(joined)

time: 211 us -> 182 us (0.86)
  Pallas kernels: 66.8 us -> 36.6 us
    pallas_call x1, Pallas kernels: 33.6 us -> 2.71 us  [shards(): call(pack_kernel, pltpu.HBM(packed_shape.shape, jnp.bfloat16), in_specs=[...]
where the time goes in v8:
time: 182 us; the launch traced here: 181 us
  blocking collectives  71 us (39%)
  waiting for transfers between devices  48 us (26%)
  Pallas kernels  36.6 us (20%)
  starting transfers between devices  20.6 us (11%)
  local copies, waits for them, and re-layouts  2.93 us (2%)
    all_to_all x3, blocking collectives, spread(): return lax.all_to_all(value, AXES, 0, 0, tiled=True)  71 us
    all_to_all x3, waiting for transfers between devices, spread(): return lax.all_to_all(value, AXES, 0, 0, tiled=True)  48 us
    all_to_all x3, starting transfers between devices, spread(): return lax.all_to_all(value, AXES, 0, 0, tiled=True)  20.6 us
    pallas_call x1, Pallas kernels, shards(): call(local_kernel, (pltpu.HBM(residual.shape, jnp.float32), pltpu.HBM((co...  7.81 us
    pallas_call x1, Pallas kernels, shards(): call(product_kernel, (pltpu.HBM(joined_shape, jnp.bfloat16), jax.ShapeDty...  6.56 us
    pallas_call x1, Pallas kernels, shards(): call(finish_kernel, field, grid=(count,), in_specs=[smem(), per_sub(trace...  5.41 us
    pallas_call x1, Pallas kernels, shards(): call(scatter_kernel, jax.ShapeDtypeStruct((devices, 2 * columns // LANE +...  4.92 us
    pallas_call x1, Pallas kernels, shards(): call(functools.partial(gather_kernel, row_blocks=lax.axis_size('row')), j...  3.85 us
  transfers between devices with their start and end apart: 3, of which 3 were waited for; matrix products, arithmetic and copies ran while one was open for 2% of the time, Pallas kernels for 4%

profile of v8, /device:TPU:1, one launch (start us, length us, event | category | flops | bytes accessed | tf_op | source)
XLA Modules:
  0.0 180.8 jit_solution(15537058205233258828)
XLA Ops:
  0.0 0.7 copy-done.2
  0.7 2.7 %shard_map.82 = bf16[4,2,16,4,8,128]{5,4,3,2,1,0:T(8,128)(2,1)} custom-call(s32[2,4]{1,0:T(2,128)S(1)} %bitcast.20, bf16[4,128,2,8,128]{4,3,2,1,0:T(8,128)(2,1)} %bitcast.14), custom_call_target="tpu_custom_call" | custom-call | tf_op jit(solution)/shard_map/pallas_call | solution.py:413
  3.4 0.0 copy-start.3
  3.4 0.0 copy-start.5
  3.4 11.5 %all-to-all-start = ((bf16[128,32,128]{2,1,0:T(8,128)(2,1)}), bf16[128,32,128]{2,1,0:T(8,128)(2,1)S(1)}, u32[]{:S(2)}, u32[]{:S(2)}) async-start(bf16[128,32,128]{2,1,0:T(8,128)(2,1)} %bitcast.23), calls=%async_computation | async-start | bytes 2097152 | tf_op jit(solution)/shard_map/all_to_all | solution.py:19
  15.0 0.1 copy.14
  15.1 0.1 reshape.31
  15.2 0.1 copy.13
  15.3 0.1 reshape.30
  15.4 0.1 slice_reduce_fusion
  15.5 0.1 pad_add_fusion.table
  15.6 18.3 %all-to-all-done.chunks = bf16[128,32,128]{2,1,0:T(8,128)(2,1)S(1)} async-done(((bf16[128,32,128]{2,1,0:T(8,128)(2,1)}), bf16[128,32,128]{2,1,0:T(8,128)(2,1)S(1)}, u32[]{:S(2)}, u32[]{:S(2)}) %all-to-all-start) | async-done | bytes 1048608 | tf_op jit(solution)/shard_map/all_to_all | solution.py:19
  33.8 1.9 %shard_map.83 = bf16[128,32,128]{2,1,0:T(8,128)(2,1)} custom-call(s32[20]{0:T(128)S(1)} %pad_add_fusion.table, bf16[128,32,128]{2,1,0:T(8,128)(2,1)S(1)} %all-to-all-done.chunks), custom_call_target="tpu_custom_call" | custom-call | tf_op jit(solution)/shard_map/pallas_call | solution.py:115
  35.7 4.8 %all-to-all-start.1 = ((bf16[128,32,128]{2,1,0:T(8,128)(2,1)}), bf16[128,32,128]{2,1,0:T(8,128)(2,1)S(1)}, u32[]{:S(2)}, u32[]{:S(2)}) async-start(bf16[128,32,128]{2,1,0:T(8,128)(2,1)} %shard_map.83), calls=%async_computation.1 | async-start | bytes 2097152 | tf_op jit(solution)/shard_map/all_to_all | solution.py:19
  40.5 0.1 copy.15
  40.6 0.7 slice.18
  41.3 0.9 reshape.35
  42.3 0.3 broadcast_select_fusion
  42.6 0.3 pad_maximum_fusion.1
  42.9 0.8 pad_maximum_fusion.base
  43.7 15.8 %all-to-all-done.1 = bf16[128,32,128]{2,1,0:T(8,128)(2,1)S(1)} async-done(((bf16[128,32,128]{2,1,0:T(8,128)(2,1)}), bf16[128,32,128]{2,1,0:T(8,128)(2,1)S(1)}, u32[]{:S(2)}, u32[]{:S(2)}) %all-to-all-start.1) | async-done | bytes 1048608 | tf_op jit(solution)/shard_map/all_to_all | solution.py:19
  59.6 3.5 %shard_map.84 = (bf16[4,1024,256]{2,1,0:T(8,128)(2,1)}, bf16[128,8,128]{2,1,0:T(8,128)(2,1)S(1)}) custom-call(s32[20]{0:T(128)S(1)} %pad_add_fusion.table, bf16[4,1024,256]{2,1,0:T(8,128)(2,1)S(1)} %copy-done, bf16[4,32,1024]{2,1,0:T(8,128)(2,1)S(1)} %bitcast.18, bf16[4,2,16,4,8,128]{5,4,3,2,1,0:T(8,128)(2,1)S(1)} %bitcast.16, ...), custom_call_target="tpu_custom_call" | custom-call | tf_op jit(solution)/shard_map/pallas_call | solution.py:433
  63.1 15.5 %all_to_all.30.received = bf16[128,8,128]{2,1,0:T(8,128)(2,1)S(1)} all-to-all(bf16[128,8,128]{2,1,0:T(8,128)(2,1)S(1)} %get-tuple-element.14), channel_id=1, replica_groups=mesh['row'=16,'col'=8] {'row','col'}, dimensions={0} | all-to-all | bytes 524288 | tf_op jit(solution)/shard_map/all_to_all | solution.py:19
  78.5 4.9 %shard_map.86 = bf16[128,40,128]{2,1,0:T(8,128)(2,1)} custom-call(s32[20]{0:T(128)S(1)} %pad_add_fusion.table, bf16[128,8,128]{2,1,0:T(8,128)(2,1)S(1)} %all_to_all.30.received), custom_call_target="tpu_custom_call" | custom-call | tf_op jit(solution)/shard_map/pallas_call | solution.py:471
  83.5 4.3 %all-to-all-start.3 = ((bf16[128,40,128]{2,1,0:T(8,128)(2,1)}), bf16[128,40,128]{2,1,0:T(8,128)(2,1)S(1)}, u32[]{:S(2)}, u32[]{:S(2)}) async-start(bf16[128,40,128]{2,1,0:T(8,128)(2,1)} %shard_map.86), calls=%async_computation.3 | async-start | bytes 2621440 | tf_op jit(solution)/shard_map/all_to_all | solution.py:19
  87.8 7.8 %shard_map.85 = (f32[4,1024,256]{2,1,0:T(8,128)}, bf16[4,2,16,6,8,128]{5,4,3,2,1,0:T(8,128)(2,1)}) custom-call(s32[2,4]{1,0:T(2,128)S(1)} %bitcast.21, bf16[4,1024,1024]{2,1,0:T(8,128)(2,1)} %inverse.2, bf16[4,1024,256]{2,1,0:T(8,128)(2,1)} %get-tuple-element.15.weighted), custom_call_target="tpu_custom_call" | custom-call | tf_op jit(solution)/shard_map/pallas_call | solution.py:455
  95.6 13.9 %all-to-all-done.3.placed = bf16[128,40,128]{2,1,0:T(8,128)(2,1)S(1)} async-done(((bf16[128,40,128]{2,1,0:T(8,128)(2,1)}), bf16[128,40,128]{2,1,0:T(8,128)(2,1)S(1)}, u32[]{:S(2)}, u32[]{:S(2)}) %all-to-all-start.3) | async-done | bytes 1310752 | tf_op jit(solution)/shard_map/all_to_all | solution.py:19
  109.4 6.6 %shard_map.87 = (bf16[128,48,128]{2,1,0:T(8,128)(2,1)}, bf16[4,4,32,128]{3,2,1,0:T(8,128)(2,1)S(1)}) custom-call(bf16[128,40,128]{2,1,0:T(8,128)(2,1)S(1)} %all-to-all-done.3.placed, bf16[1024,2048]{1,0:T(8,128)(2,1)} %inverse.3, bf16[128,48,128]{2,1,0:T(8,128)(2,1)} %bitcast.22), custom_call_target="tpu_custom_call", output_to_operand_aliasing={{0}: (2, {})} | custom-call | tf_op jit(solution)/shard_map/pallas_call | solution.py:484
  116.0 29.7 %all_to_all.31.partial = bf16[128,48,128]{2,1,0:T(8,128)(2,1)S(1)} all-to-all(bf16[128,48,128]{2,1,0:T(8,128)(2,1)} %get-tuple-element.19), channel_id=1, replica_groups=mesh['row'=16,'col'=8] {'row','col'}, dimensions={0} | all-to-all | bytes 3145728 | tf_op jit(solution)/shard_map/all_to_all | solution.py:19
  145.7 3.9 %shard_map.88 = bf16[128,40,128]{2,1,0:T(8,128)(2,1)S(1)} custom-call(s32[20]{0:T(128)S(1)} %pad_add_fusion.table, bf16[128,8,128]{2,1,0:T(8,128)(2,1)S(1)} %all_to_all.30.received, bf16[128,48,128]{2,1,0:T(8,128)(2,1)S(1)} %all_to_all.31.partial), custom_call_target="tpu_custom_call" | custom-call | tf_op jit(solution)/shard_map/pallas_call | solution.py:507
  149.6 25.9 %all_to_all.32 = bf16[128,40,128]{2,1,0:T(8,128)(2,1)S(1)} all-to-all(bf16[128,40,128]{2,1,0:T(8,128)(2,1)S(1)} %shard_map.88), channel_id=1, replica_groups=mesh['row'=16,'col'=8] {'row','col'}, dimensions={0} | all-to-all | bytes 2621440 | tf_op jit(solution)/shard_map/all_to_all | solution.py:19
  175.4 5.4 %shard_map.89 = bf16[4,1024,256]{2,1,0:T(8,128)(2,1)} custom-call(s32[20]{0:T(128)S(1)} %pad_add_fusion.table, f32[4,1024,256]{2,1,0:T(8,128)} %get-tuple-element.16.local, bf16[4,32,1024]{2,1,0:T(8,128)(2,1)S(1)} %bitcast.19, bf16[4,2,16,5,8,128]{5,4,3,2,1,0:T(8,128)(2,1)S(1)} %bitcast.15, bf16[4,4,32,128]{3,2,1,0:T(8,128)(2,1)S(1)} %get-tuple-element.20.arrived_modes), custom_call_target="tpu_custom_call" | custom-call | tf_op jit(solution)/shard_map/pallas_call | solution.py:518
  (17 shorter events, 0.1 us)
Async XLA Ops:
  0.0 0.7 copy-start.2
  3.4 11.6 %copy-start.4 = (s32[4,2]{0,1:T(2,128)S(1)}, s32[4,2]{0,1:T(2,128)}, u32[]{:S(2)}) copy-start(s32[4,2]{0,1:T(2,128)} %param.14) | copy-start | bytes 100
  3.4 11.7 %copy-start.3 = (s32[4,2]{0,1:T(2,128)S(1)}, s32[4,2]{0,1:T(2,128)}, u32[]{:S(2)}) copy-start(s32[4,2]{0,1:T(2,128)} %param.15) | copy-start | bytes 100
  3.4 11.9 %copy-start.5 = (s32[4,2]{0,1:T(2,128)S(1)}, s32[4,2]{0,1:T(2,128)}, u32[]{:S(2)}) copy-start(s32[4,2]{0,1:T(2,128)} %param.13) | copy-start | bytes 100
  3.4 30.4 %all-to-all-start = ((bf16[128,32,128]{2,1,0:T(8,128)(2,1)}), bf16[128,32,128]{2,1,0:T(8,128)(2,1)S(1)}, u32[]{:S(2)}, u32[]{:S(2)}) async-start(bf16[128,32,128]{2,1,0:T(8,128)(2,1)} %bitcast.23), calls=%async_computation | async-start | bytes 2097152 | tf_op jit(solution)/shard_map/all_to_all | solution.py:19
  35.7 4.9 %copy-start.1 = (bf16[4,1024,32]{1,2,0:T(8,128)(2,1)S(1)}, bf16[4,1024,32]{1,2,0:T(8,128)(2,1)}, u32[]{:S(2)}) copy-start(bf16[4,1024,32]{1,2,0:T(8,128)(2,1)} %param.10) | copy-start | bytes 786436
  35.7 6.5 %copy-start.6 = (s32[128]{0:T(128)S(1)}, s32[128]{0:T(128)}, u32[]{:S(2)}) copy-start(s32[128]{0:T(128)} %param.11) | copy-start | bytes 1540
  35.7 23.9 %all-to-all-start.1 = ((bf16[128,32,128]{2,1,0:T(8,128)(2,1)}), bf16[128,32,128]{2,1,0:T(8,128)(2,1)S(1)}, u32[]{:S(2)}, u32[]{:S(2)}) async-start(bf16[128,32,128]{2,1,0:T(8,128)(2,1)} %shard_map.83), calls=%async_computation.1 | async-start | bytes 2097152 | tf_op jit(solution)/shard_map/all_to_all | solution.py:19
  40.5 19.0 %copy-start = (bf16[4,1024,256]{2,1,0:T(8,128)(2,1)S(1)}, bf16[4,1024,256]{2,1,0:T(8,128)(2,1)}, u32[]{:S(2)}) copy-start(bf16[4,1024,256]{2,1,0:T(8,128)(2,1)} %residual.1) | copy-start | bytes 6291460
  83.5 26.0 %all-to-all-start.3 = ((bf16[128,40,128]{2,1,0:T(8,128)(2,1)}), bf16[128,40,128]{2,1,0:T(8,128)(2,1)S(1)}, u32[]{:S(2)}, u32[]{:S(2)}) async-start(bf16[128,40,128]{2,1,0:T(8,128)(2,1)} %shard_map.86), calls=%async_computation.3 | async-start | bytes 2621440 | tf_op jit(solution)/shard_map/all_to_all | solution.py:19

commit v9 on v7

--- a/solution.py
+++ b/solution.py
@@ -11,7 +11,8 @@
 MODES = 32
 HALF = 128
 LANE = 128
-GROUP = 64
+GROUP = 128
+SUBS = 2
 VMEM_LIMIT = 16 * 1024 * 1024
 
 
@@ -63,23 +64,32 @@
                 packed[0, half, :, which * 2 + lane] = tile.astype(jnp.bfloat16)
 
 
-def pack_kernel(offsets, tiles, packed, done):
+def pack_kernel(offsets, tiles, packed, staged, read, written):
     size = HALF // 8
-    copies = []
+    reads, writes = [], []
     for sub in range(tiles.shape[0]):
         for which in range(2):
             second = jnp.bitwise_and(jnp.right_shift(offsets[which, sub], 7), 1)
             for half in range(2):
                 start = which * 2 * size + (second * size if half == 0 else size)
-                copies.append(
+                at = (sub * 2 + which) * 2 + half
+                reads.append(
                     pltpu.make_async_copy(
-                        tiles.at[sub, pl.ds(start, size)],
-                        packed.at[sub, half, :, pl.ds(which * 2, 2)],
-                        done.at[sub, which, half],
+                        tiles.at[sub, pl.ds(start, size)], staged.at[at], read.at[at]
                     )
                 )
-                copies[-1].start()
-    for copy in copies:
+                reads[-1].start()
+                writes.append(
+                    pltpu.make_async_copy(
+                        staged.at[at],
+                        packed.at[sub, half, :, pl.ds(which * 2, 2)],
+                        written.at[at],
+                    )
+                )
+    for first, second in zip(reads, writes):
+        first.wait()
+        second.start()
+    for copy in writes:
         copy.wait()
 
 
@@ -100,15 +110,16 @@
     lax.fori_loop(0, chunks.shape[0], step, 0, unroll=8)
 
 
-def exchange(packed, table):
+def exchange(packed, table, early):
     chunks = spread(packed.reshape(-1, 32, LANE))
+    chunks, early = lax.optimization_barrier((chunks, early))
     chunks = call(
         reroute_kernel,
         jax.ShapeDtypeStruct(chunks.shape, chunks.dtype),
         in_specs=[smem(), whole()],
         out_specs=whole(),
     )(table, chunks)
-    return spread(chunks).reshape(packed.shape)
+    return spread(chunks).reshape(packed.shape), early
 
 
 def arrived_rows(table, sub, which, half, arrived):
@@ -123,20 +134,23 @@
 
 
 def weigh_kernel(table, residual, modes, arrived, base, weighted, payload, restricted, turned):
-    sub = pl.program_id(0)
-    for which in range(2):
-        for half in range(2):
-            start = (which * 2 + half) * HALF
-            rows, inside = arrived_rows(table, sub, which, half, arrived)
-            own = residual[0, start : start + HALF].astype(jnp.float32)
-            value = (own + rows * inside) * (1.0 - 0.5 * inside)
-            weighted[0, start : start + HALF] = value.astype(jnp.bfloat16)
-    weighted[0, 4 * HALF :] = residual[0, 4 * HALF :]
-    restricted[pl.ds(pl.multiple_of(sub * MODES, MODES), MODES)] = lax.dot_general(
-        modes[0], weighted[0], (((1,), (0,)), ((), ())), preferred_element_type=jnp.float32
-    )
-
-    @pl.when(sub == pl.num_programs(0) - 1)
+    step_at = pl.program_id(0)
+    subs = residual.shape[0]
+    for at in range(subs):
+        sub = step_at * subs + at
+        for which in range(2):
+            for half in range(2):
+                start = (which * 2 + half) * HALF
+                rows, inside = arrived_rows(table, sub, which, half, arrived)
+                own = residual[at, start : start + HALF].astype(jnp.float32)
+                value = (own + rows * inside) * (1.0 - 0.5 * inside)
+                weighted[at, start : start + HALF] = value.astype(jnp.bfloat16)
+        weighted[at, 4 * HALF :] = residual[at, 4 * HALF :]
+        restricted[pl.ds(pl.multiple_of(sub * MODES, MODES), MODES)] = lax.dot_general(
+            modes[at], weighted[at], (((1,), (0,)), ((), ())), preferred_element_type=jnp.float32
+        )
+
+    @pl.when(step_at == pl.num_programs(0) - 1)
     def _():
         devices, rows, _ = payload.shape
         turned[: 2 * devices] = restricted[...].T
@@ -158,10 +172,11 @@
     )
 
 
-def finish_kernel(table, local, modes, arrived, arrived_modes, out, pairs, picked):
-    sub = pl.program_id(0)
-
-    @pl.when(sub == 0)
+def finish_kernel(table, local, modes, arrived, their_modes, out, pairs, picked):
+    step_at = pl.program_id(0)
+    subs = local.shape[0]
+
+    @pl.when(step_at == 0)
     def _():
         for first in range(4):
             for half in range(2):
@@ -178,19 +193,21 @@
         for kind in range(3):
             picked[kind] = pairs[kind].T.reshape(picked.shape[1:]).astype(jnp.bfloat16)
 
-    added = prolong(modes[0], picked[0, sub])
-    for which in range(2):
-        other = jnp.bitwise_xor(sub, table[2 + which])
-        for half in range(2):
-            start = (which * 2 + half) * HALF
-            rows, inside = arrived_rows(table, sub, which, half, arrived)
-            _, both = flags(table, sub, which)
-            theirs = prolong(arrived_modes[which * 2 + half * both, other], picked[1 + which, other])
-            theirs = (0.5 * (rows + theirs)).astype(jnp.bfloat16).astype(jnp.float32)
-            own = local[0, start : start + HALF] + added[start : start + HALF]
-            own = (own * (1.0 - 0.5 * inside)).astype(jnp.bfloat16).astype(jnp.float32)
-            out[0, start : start + HALF] = (own + theirs * inside).astype(jnp.bfloat16)
-    out[0, 4 * HALF :] = (local[0, 4 * HALF :] + added[4 * HALF :]).astype(jnp.bfloat16)
+    for at in range(subs):
+        sub = step_at * subs + at
+        added = prolong(modes[at], picked[0, sub])
+        for which in range(2):
+            other = jnp.bitwise_xor(sub, table[2 + which])
+            for half in range(2):
+                start = (which * 2 + half) * HALF
+                rows, inside = arrived_rows(table, sub, which, half, arrived)
+                _, both = flags(table, sub, which)
+                theirs = prolong(their_modes[which * 2 + half * both, other], picked[1 + which, other])
+                theirs = (0.5 * (rows + theirs)).astype(jnp.bfloat16).astype(jnp.float32)
+                own = local[at, start : start + HALF] + added[start : start + HALF]
+                own = (own * (1.0 - 0.5 * inside)).astype(jnp.bfloat16).astype(jnp.float32)
+                out[at, start : start + HALF] = (own + theirs * inside).astype(jnp.bfloat16)
+        out[at, 4 * HALF :] = (local[at, 4 * HALF :] + added[4 * HALF :]).astype(jnp.bfloat16)
 
 
 def scatter_kernel(table, received, out, total, staged):
@@ -254,11 +271,11 @@
     @pl.when(at_step == 0)
     def _():
         def step(group, carry):
-            for inner in range(4):
-                rows = placed[group * 4 + inner, : 2 * tiles].astype(jnp.float32)
-                at = pl.multiple_of(group * 8, 8) + 2 * inner
-                for tile in range(tiles):
-                    pairs[tile, pl.ds(at, 2)] = rows[2 * tile : 2 * tile + 2]
+            rows = [placed[group * 4 + inner, : 2 * tiles].astype(jnp.float32) for inner in range(4)]
+            at = pl.multiple_of(group * 8, 8)
+            for tile in range(tiles):
+                taken = [piece[2 * tile : 2 * tile + 2] for piece in rows]
+                pairs[tile, pl.ds(at, 8)] = jnp.concatenate(taken, 0)
             return carry
 
         lax.fori_loop(0, groups, step, 0)
@@ -365,9 +382,9 @@
     return pl.BlockSpec(memory_space=pltpu.VMEM)
 
 
-def per_sub(*shape):
+def per_sub(*shape, subs=1):
     zeros = (0,) * len(shape)
-    return pl.BlockSpec((1,) + shape, lambda sub: (sub,) + zeros)
+    return pl.BlockSpec((subs,) + shape, lambda step: (step,) + zeros)
 
 
 def same(*shape):
@@ -392,7 +409,6 @@
 
     turned_modes = modes.transpose(0, 2, 1)
     offsets = block_offsets.T
-    packed_spec = per_sub(2, HALF // 8, 4, 8, LANE)
     packed_shape = jax.ShapeDtypeStruct((count, 2, HALF // 8, 4, 8, LANE), jnp.bfloat16)
 
     tiles = residual.reshape(count, trace_len // 8, 8, 2, LANE).transpose(0, 1, 3, 2, 4)
@@ -402,9 +418,12 @@
         pltpu.HBM(packed_shape.shape, jnp.bfloat16),
         in_specs=[smem(), hbm],
         out_specs=hbm,
-        scratch_shapes=[pltpu.SemaphoreType.DMA((count, 2, 2))],
+        scratch_shapes=[
+            pltpu.VMEM((count * 4, HALF // 8, 2, 8, LANE), jnp.bfloat16),
+            pltpu.SemaphoreType.DMA((count * 4,)),
+            pltpu.SemaphoreType.DMA((count * 4,)),
+        ],
     )(offsets, in_hbm(tiles))
-    arrived = exchange(packed, table)
     digits = jnp.stack([coarse_map // LANE, coarse_map % LANE]).astype(jnp.bfloat16)
     digits = jnp.concatenate([jnp.zeros_like(digits), digits], 0)
     shared = turned_modes[:, :, : 4 * HALF].reshape(count, MODES, 2, 2, HALF)
@@ -413,23 +432,24 @@
         [jnp.where(second, shared[:, :, :, 1], shared[:, :, :, 0]), shared[:, :, :, 1]], 3
     ).reshape(devices, 4, HALF)
     base = jnp.concatenate([jnp.broadcast_to(digits[None], (devices,) + digits.shape), shared], 1)
+    arrived, base = exchange(packed, table, base)
     weighted, payload = call(
         weigh_kernel,
         (pltpu.HBM(residual.shape, jnp.bfloat16), jax.ShapeDtypeStruct(base.shape, jnp.bfloat16)),
-        grid=(count,),
+        grid=(count // SUBS,),
         in_specs=[
             smem(),
-            per_sub(trace_len, cases),
-            per_sub(MODES, trace_len),
+            per_sub(trace_len, cases, subs=SUBS),
+            per_sub(MODES, trace_len, subs=SUBS),
             same(*arrived.shape),
             same(*base.shape),
         ],
-        out_specs=(per_sub(trace_len, cases), same(*base.shape)),
+        out_specs=(per_sub(trace_len, cases, subs=SUBS), same(*base.shape)),
         scratch_shapes=[
             pltpu.VMEM((count * MODES, cases), jnp.float32),
             pltpu.VMEM((cases + 8, LANE), jnp.float32),
         ],
-    )(table, residual, turned_modes, arrived, in_hbm(base))
+    )(table, residual, turned_modes, arrived, base)
     received = spread(payload)
     weighted, received = lax.optimization_barrier((weighted, received))
 
@@ -441,7 +461,7 @@
         ),
         grid=(count,),
         in_specs=[smem(), per_sub(trace_len, trace_len), per_sub(trace_len, cases)],
-        out_specs=(per_sub(trace_len, cases), packed_spec),
+        out_specs=(per_sub(trace_len, cases), per_sub(*packed_shape.shape[1:])),
     )(offsets, in_hbm(interface_inverse), in_hbm(weighted))
     packed = packed.reshape(devices, 32, LANE)
 
@@ -457,7 +477,7 @@
         ],
     )(table, received)
     placed = spread(placed)
-    steps = 4
+    steps = 2
     joined_shape = (devices, 2 * rows // LANE + 32, LANE)
     modes_shape = (4, count, MODES, HALF)
     joined, their_modes = call(
@@ -494,15 +514,15 @@
     return call(
         finish_kernel,
         field,
-        grid=(count,),
+        grid=(count // SUBS,),
         in_specs=[
             smem(),
-            per_sub(trace_len, cases),
-            per_sub(MODES, trace_len),
+            per_sub(trace_len, cases, subs=SUBS),
+            per_sub(MODES, trace_len, subs=SUBS),
             same(*last.shape),
             same(*modes_shape),
         ],
-        out_specs=per_sub(trace_len, cases),
+        out_specs=per_sub(trace_len, cases, subs=SUBS),
         scratch_shapes=[
             pltpu.VMEM((3, cases, LANE), jnp.float32),
             pltpu.VMEM((3, count, MODES, cases), jnp.bfloat16),

time: 211 us -> 175 us (0.83)
  Pallas kernels: 66.8 us -> 31.4 us
  blocking collectives: 70.1 us -> 93.4 us
  waiting for transfers between devices: 48.1 us -> 30.6 us
  starting transfers between devices: 20.6 us -> 15.8 us
    pallas_call x1, Pallas kernels: 33.6 us -> 2.71 us  [shards(): call(pack_kernel, pltpu.HBM(packed_shape.shape, jnp.bfloat16), in_specs=[...]
    all_to_all x3 -> x4, blocking collectives: 70.1 us -> 93.4 us  [spread(): return lax.all_to_all(value, AXES, 0, 0, tiled=True)]
    all_to_all x3 -> x2, waiting for transfers between devices: 48.1 us -> 30.6 us  [spread(): return lax.all_to_all(value, AXES, 0, 0, tiled=True)]
    all_to_all x3 -> x2, starting transfers between devices: 20.6 us -> 15.8 us  [spread(): return lax.all_to_all(value, AXES, 0, 0, tiled=True)]
  transfers between devices with their start and end apart: 3 -> 2, of which waited for: 3 -> 2; matrix products, arithmetic and copies ran while one was open for 2% -> 1% of each run, Pallas kernels for 4% -> 4%
where the time goes in v9:
time: 175 us; the launch traced here: 174 us
  blocking collectives  93.4 us (53%)
  Pallas kernels  31.4 us (18%)
  waiting for transfers between devices  30.6 us (17%)
  starting transfers between devices  15.8 us (9%)
    all_to_all x4, blocking collectives, spread(): return lax.all_to_all(value, AXES, 0, 0, tiled=True)  93.4 us
    all_to_all x2, waiting for transfers between devices, spread(): return lax.all_to_all(value, AXES, 0, 0, tiled=True)  30.6 us
    all_to_all x2, starting transfers between devices, spread(): return lax.all_to_all(value, AXES, 0, 0, tiled=True)  15.8 us
    pallas_call x1, Pallas kernels, shards(): call(local_kernel, (pltpu.HBM(residual.shape, jnp.float32), pltpu.HBM(pac...  7.67 us
    pallas_call x1, Pallas kernels, shards(): call(product_kernel, (jax.ShapeDtypeStruct(joined_shape, jnp.bfloat16), j...  4.83 us
    pallas_call x1, Pallas kernels, shards(): call(scatter_kernel, jax.ShapeDtypeStruct((devices, 2 * columns // LANE +...  4.69 us
    pallas_call x1, Pallas kernels, shards(): call(finish_kernel, field, grid=(count // SUBS,), in_specs=[smem(), per_s...  4.37 us
    pallas_call x1, Pallas kernels, shards(): call(functools.partial(gather_kernel, row_blocks=lax.axis_size('row')), j...  3.64 us
  transfers between devices with their start and end apart: 2, of which 2 were waited for; matrix products, arithmetic and copies ran while one was open for 1% of the time, Pallas kernels for 4%

profile of v9, /device:TPU:1, one launch (start us, length us, event | category | flops | bytes accessed | tf_op | source)
XLA Modules:
  0.0 174.3 jit_solution(14835961378182077062)
XLA Ops:
  0.0 0.7 copy-done.3
  0.7 2.7 %shard_map.82 = bf16[4,2,16,4,8,128]{5,4,3,2,1,0:T(8,128)(2,1)} custom-call(s32[2,4]{1,0:T(2,128)S(1)} %bitcast.20, bf16[4,128,2,8,128]{4,3,2,1,0:T(8,128)(2,1)} %bitcast.14), custom_call_target="tpu_custom_call" | custom-call | tf_op jit(solution)/shard_map/pallas_call | solution.py:416
  3.4 0.0 copy-start.7
  3.4 11.5 %all-to-all-start = ((bf16[128,32,128]{2,1,0:T(8,128)(2,1)}), bf16[128,32,128]{2,1,0:T(8,128)(2,1)S(1)}, u32[]{:S(2)}, u32[]{:S(2)}) async-start(bf16[128,32,128]{2,1,0:T(8,128)(2,1)} %bitcast.22), calls=%async_computation | async-start | bytes 2097152 | tf_op jit(solution)/shard_map/all_to_all | solution.py:20
  14.9 0.0 copy-done.4
  15.0 0.0 copy-done.5
  15.0 0.1 copy.13
  15.1 0.1 reshape.31
  15.2 0.1 copy.12
  15.3 0.1 reshape.30
  15.4 0.0 copy-done.6
  15.4 0.1 slice_reduce_fusion
  15.5 0.1 copy.14
  15.7 0.1 pad_add_fusion.table
  15.8 0.3 broadcast_select_fusion
  16.1 0.3 pad_maximum_fusion.1
  16.4 0.8 pad_maximum_fusion.base
  17.2 16.6 %all-to-all-done.chunks = bf16[128,32,128]{2,1,0:T(8,128)(2,1)S(1)} async-done(((bf16[128,32,128]{2,1,0:T(8,128)(2,1)}), bf16[128,32,128]{2,1,0:T(8,128)(2,1)S(1)}, u32[]{:S(2)}, u32[]{:S(2)}) %all-to-all-start) | async-done | bytes 1048608 | tf_op jit(solution)/shard_map/all_to_all | solution.py:20
  33.8 0.9 shard_map.83
  34.7 23.3 %all_to_all.30 = bf16[128,32,128]{2,1,0:T(8,128)(2,1)S(1)} all-to-all(bf16[128,32,128]{2,1,0:T(8,128)(2,1)S(1)} %shard_map.83), channel_id=1, replica_groups=mesh['row'=16,'col'=8] {'row','col'}, dimensions={0} | all-to-all | bytes 2097152 | tf_op jit(solution)/shard_map/all_to_all | solution.py:20
  58.0 0.0 copy-done
  58.0 2.6 %shard_map.84 = (bf16[4,1024,256]{2,1,0:T(8,128)(2,1)}, bf16[128,8,128]{2,1,0:T(8,128)(2,1)S(1)}) custom-call(s32[20]{0:T(128)S(1)} %pad_add_fusion.table, bf16[4,1024,256]{2,1,0:T(8,128)(2,1)S(1)} %copy-done, bf16[4,32,1024]{2,1,0:T(8,128)(2,1)S(1)} %bitcast.18, bf16[4,2,16,4,8,128]{5,4,3,2,1,0:T(8,128)(2,1)S(1)} %bitcast.16, bf16[128,8,128]{2,1,0:T(8,128)(2,1)S(1)} %copy-done.2), custom_call_target="tpu_custom_call" | custom-call | tf_op jit(solution)/shard_map/pallas_call | solution.py:436
  60.6 15.5 %all_to_all.31.received = bf16[128,8,128]{2,1,0:T(8,128)(2,1)S(1)} all-to-all(bf16[128,8,128]{2,1,0:T(8,128)(2,1)S(1)} %get-tuple-element.18), channel_id=1, replica_groups=mesh['row'=16,'col'=8] {'row','col'}, dimensions={0} | all-to-all | bytes 524288 | tf_op jit(solution)/shard_map/all_to_all | solution.py:20
  76.1 4.7 %shard_map.86 = bf16[128,40,128]{2,1,0:T(8,128)(2,1)} custom-call(s32[20]{0:T(128)S(1)} %pad_add_fusion.table, bf16[128,8,128]{2,1,0:T(8,128)(2,1)S(1)} %all_to_all.31.received), custom_call_target="tpu_custom_call" | custom-call | tf_op jit(solution)/shard_map/pallas_call | solution.py:469
  80.8 4.3 %all-to-all-start.3 = ((bf16[128,40,128]{2,1,0:T(8,128)(2,1)}), bf16[128,40,128]{2,1,0:T(8,128)(2,1)S(1)}, u32[]{:S(2)}, u32[]{:S(2)}) async-start(bf16[128,40,128]{2,1,0:T(8,128)(2,1)} %shard_map.86), calls=%async_computation.3 | async-start | bytes 2621440 | tf_op jit(solution)/shard_map/all_to_all | solution.py:20
  85.1 7.7 %shard_map.85 = (f32[4,1024,256]{2,1,0:T(8,128)}, bf16[4,2,16,4,8,128]{5,4,3,2,1,0:T(8,128)(2,1)}) custom-call(s32[2,4]{1,0:T(2,128)S(1)} %bitcast.21, bf16[4,1024,1024]{2,1,0:T(8,128)(2,1)} %inverse.2, bf16[4,1024,256]{2,1,0:T(8,128)(2,1)} %get-tuple-element.19.weighted), custom_call_target="tpu_custom_call" | custom-call | tf_op jit(solution)/shard_map/pallas_call | solution.py:456
  92.8 14.0 %all-to-all-done.3.placed = bf16[128,40,128]{2,1,0:T(8,128)(2,1)S(1)} async-done(((bf16[128,40,128]{2,1,0:T(8,128)(2,1)}), bf16[128,40,128]{2,1,0:T(8,128)(2,1)S(1)}, u32[]{:S(2)}, u32[]{:S(2)}) %all-to-all-start.3) | async-done | bytes 1310752 | tf_op jit(solution)/shard_map/all_to_all | solution.py:20
  106.8 4.8 %shard_map.87 = (bf16[128,48,128]{2,1,0:T(8,128)(2,1)S(1)}, bf16[4,4,32,128]{3,2,1,0:T(8,128)(2,1)S(1)}) custom-call(bf16[128,40,128]{2,1,0:T(8,128)(2,1)S(1)} %all-to-all-done.3.placed, bf16[1024,2048]{1,0:T(8,128)(2,1)} %inverse.3, bf16[128,32,128]{2,1,0:T(8,128)(2,1)} %bitcast.23), custom_call_target="tpu_custom_call" | custom-call | tf_op jit(solution)/shard_map/pallas_call | solution.py:483
  111.6 28.8 %all_to_all.32.partial = bf16[128,48,128]{2,1,0:T(8,128)(2,1)S(1)} all-to-all(bf16[128,48,128]{2,1,0:T(8,128)(2,1)S(1)} %get-tuple-element.23), channel_id=1, replica_groups=mesh['row'=16,'col'=8] {'row','col'}, dimensions={0} | all-to-all | bytes 3145728 | tf_op jit(solution)/shard_map/all_to_all | solution.py:20
  140.4 3.6 %shard_map.88 = bf16[128,40,128]{2,1,0:T(8,128)(2,1)S(1)} custom-call(s32[20]{0:T(128)S(1)} %pad_add_fusion.table, bf16[128,8,128]{2,1,0:T(8,128)(2,1)S(1)} %all_to_all.31.received, bf16[128,48,128]{2,1,0:T(8,128)(2,1)S(1)} %all_to_all.32.partial), custom_call_target="tpu_custom_call" | custom-call | tf_op jit(solution)/shard_map/pallas_call | solution.py:503
  144.1 25.9 %all_to_all.33 = bf16[128,40,128]{2,1,0:T(8,128)(2,1)S(1)} all-to-all(bf16[128,40,128]{2,1,0:T(8,128)(2,1)S(1)} %shard_map.88), channel_id=1, replica_groups=mesh['row'=16,'col'=8] {'row','col'}, dimensions={0} | all-to-all | bytes 2621440 | tf_op jit(solution)/shard_map/all_to_all | solution.py:20
  169.9 4.4 %shard_map.89 = bf16[4,1024,256]{2,1,0:T(8,128)(2,1)} custom-call(s32[20]{0:T(128)S(1)} %pad_add_fusion.table, f32[4,1024,256]{2,1,0:T(8,128)} %get-tuple-element.20.local, bf16[4,32,1024]{2,1,0:T(8,128)(2,1)S(1)} %bitcast.19, bf16[4,2,16,5,8,128]{5,4,3,2,1,0:T(8,128)(2,1)S(1)} %bitcast.15, bf16[4,4,32,128]{3,2,1,0:T(8,128)(2,1)S(1)} %get-tuple-element.24.their_modes), custom_call_target="tpu_custom_call" | custom-call | tf_op jit(solution)/shard_map/pallas_call | solution.py:514
  (18 shorter events, 0.2 us)
Async XLA Ops:
  0.0 0.7 copy-start.3
  0.7 14.3 %copy-start.4 = (s32[4,2]{0,1:T(2,128)S(1)}, s32[4,2]{0,1:T(2,128)}, u32[]{:S(2)}) copy-start(s32[4,2]{0,1:T(2,128)} %param.15) | copy-start | bytes 100
  0.7 14.3 %copy-start.5 = (s32[4,2]{0,1:T(2,128)S(1)}, s32[4,2]{0,1:T(2,128)}, u32[]{:S(2)}) copy-start(s32[4,2]{0,1:T(2,128)} %param.14) | copy-start | bytes 100
  0.7 14.7 %copy-start.6 = (s32[4,2]{0,1:T(2,128)S(1)}, s32[4,2]{0,1:T(2,128)}, u32[]{:S(2)}) copy-start(s32[4,2]{0,1:T(2,128)} %param.13) | copy-start | bytes 100
  0.7 14.9 %copy-start.1 = (bf16[4,1024,32]{1,2,0:T(8,128)(2,1)S(1)}, bf16[4,1024,32]{1,2,0:T(8,128)(2,1)}, u32[]{:S(2)}) copy-start(bf16[4,1024,32]{1,2,0:T(8,128)(2,1)} %param.10) | copy-start | bytes 786436
  3.4 12.3 %copy-start.7 = (s32[128]{0:T(128)S(1)}, s32[128]{0:T(128)}, u32[]{:S(2)}) copy-start(s32[128]{0:T(128)} %param.11) | copy-start | bytes 1540
  3.4 30.4 %all-to-all-start = ((bf16[128,32,128]{2,1,0:T(8,128)(2,1)}), bf16[128,32,128]{2,1,0:T(8,128)(2,1)S(1)}, u32[]{:S(2)}, u32[]{:S(2)}) async-start(bf16[128,32,128]{2,1,0:T(8,128)(2,1)} %bitcast.22), calls=%async_computation | async-start | bytes 2097152 | tf_op jit(solution)/shard_map/all_to_all | solution.py:20
  17.2 40.8 %copy-start = (bf16[4,1024,256]{2,1,0:T(8,128)(2,1)S(1)}, bf16[4,1024,256]{2,1,0:T(8,128)(2,1)}, u32[]{:S(2)}) copy-start(bf16[4,1024,256]{2,1,0:T(8,128)(2,1)} %residual.1) | copy-start | bytes 6291460
  33.8 24.2 %copy-start.2 = (bf16[128,8,128]{2,1,0:T(8,128)(2,1)S(1)}, bf16[128,8,128]{2,1,0:T(8,128)(2,1)}, u32[]{:S(2)}) copy-start(bf16[128,8,128]{2,1,0:T(8,128)(2,1)} %pad_maximum_fusion.base) | copy-start | bytes 786436
  80.8 26.0 %all-to-all-start.3 = ((bf16[128,40,128]{2,1,0:T(8,128)(2,1)}), bf16[128,40,128]{2,1,0:T(8,128)(2,1)S(1)}, u32[]{:S(2)}, u32[]{:S(2)}) async-start(bf16[128,40,128]{2,1,0:T(8,128)(2,1)} %shard_map.86), calls=%async_computation.3 | async-start | bytes 2621440 | tf_op jit(solution)/shard_map/all_to_all | solution.py:20

commit v10 on v9

--- a/solution.py
+++ b/solution.py
@@ -172,30 +172,35 @@
     )
 
 
-def finish_kernel(table, local, modes, arrived, their_modes, out, pairs, picked):
-    step_at = pl.program_id(0)
+def finish_kernel(
+    table, local, modes, arrived, their_modes, out, pairs, picked, taken, given, read, sent
+):
     subs = local.shape[0]
-
-    @pl.when(step_at == 0)
-    def _():
-        for first in range(4):
-            for half in range(2):
-
-                def step(piece, carry, first=first, half=half):
-                    for inner in range(4):
-                        tile = arrived[first, half, piece * 4 + inner, 4].astype(jnp.float32)
-                        at = (first * 2 + half) * 32 + pl.multiple_of(piece * 8, 8) + inner * 2
-                        for kind in range(3):
-                            pairs[kind, pl.ds(at, 2)] = tile[kind * 2 : kind * 2 + 2]
-                    return carry
-
-                lax.fori_loop(0, 4, step, 0)
-        for kind in range(3):
-            picked[kind] = pairs[kind].T.reshape(picked.shape[1:]).astype(jnp.bfloat16)
-
-    for at in range(subs):
-        sub = step_at * subs + at
-        added = prolong(modes[at], picked[0, sub])
+    loads, leaves = (
+        [pltpu.make_async_copy(source.at[sub], target.at[sub], done.at[sub]) for sub in range(subs)]
+        for source, target, done in ((local, taken, read), (given, out, sent))
+    )
+    for load in loads:
+        load.start()
+
+    for first in range(4):
+        for half in range(2):
+
+            def step(piece, carry, first=first, half=half):
+                for inner in range(4):
+                    tile = arrived[first, half, piece * 4 + inner, 4].astype(jnp.float32)
+                    at = (first * 2 + half) * 32 + pl.multiple_of(piece * 8, 8) + inner * 2
+                    for kind in range(3):
+                        pairs[kind, pl.ds(at, 2)] = tile[kind * 2 : kind * 2 + 2]
+                return carry
+
+            lax.fori_loop(0, 4, step, 0)
+    for kind in range(3):
+        picked[kind] = pairs[kind].T.reshape(picked.shape[1:]).astype(jnp.bfloat16)
+
+    for sub in range(subs):
+        loads[sub].wait()
+        added = prolong(modes[sub], picked[0, sub])
         for which in range(2):
             other = jnp.bitwise_xor(sub, table[2 + which])
             for half in range(2):
@@ -204,15 +209,30 @@
                 _, both = flags(table, sub, which)
                 theirs = prolong(their_modes[which * 2 + half * both, other], picked[1 + which, other])
                 theirs = (0.5 * (rows + theirs)).astype(jnp.bfloat16).astype(jnp.float32)
-                own = local[at, start : start + HALF] + added[start : start + HALF]
+                own = taken[sub, start : start + HALF] + added[start : start + HALF]
                 own = (own * (1.0 - 0.5 * inside)).astype(jnp.bfloat16).astype(jnp.float32)
-                out[at, start : start + HALF] = (own + theirs * inside).astype(jnp.bfloat16)
-        out[at, 4 * HALF :] = (local[at, 4 * HALF :] + added[4 * HALF :]).astype(jnp.bfloat16)
-
-
-def scatter_kernel(table, received, out, total, staged):
+                given[sub, start : start + HALF] = (own + theirs * inside).astype(jnp.bfloat16)
+        given[sub, 4 * HALF :] = (taken[sub, 4 * HALF :] + added[4 * HALF :]).astype(jnp.bfloat16)
+        leaves[sub].start()
+    for leave in leaves:
+        leave.wait()
+
+
+def scatter_kernel(table, received, out, total, staged, ready, shared, sent, shared_sent):
     devices = received.shape[0]
     place = lax.broadcasted_iota(jnp.int32, (LANE, LANE), 0).astype(jnp.float32)
+    first = lax.broadcasted_iota(jnp.int32, (8, LANE), 0) < 6
+
+    def forward(device, carry):
+        pieces = [
+            received[jnp.bitwise_xor(device, table[which])].astype(jnp.float32) for which in range(2)
+        ]
+        shared[device] = jnp.where(first, pieces[0], pieces[1]).astype(jnp.bfloat16)
+        return carry
+
+    lax.fori_loop(0, devices, forward, 0, unroll=4)
+    shares = pltpu.make_async_copy(shared, out.at[:, pl.ds(staged.shape[1], 8)], shared_sent)
+    shares.start()
     total[...] = jnp.zeros_like(total)
 
     def step(block, carry):
@@ -243,82 +263,80 @@
             for piece in range(pieces):
                 at = case * LANE + block * pieces + piece
                 staged[block, piece * 2 + case : piece * 2 + case + 1] = total[at : at + 1]
-    for block in range(blocks):
-        value = staged[block].astype(jnp.bfloat16)
-
-        def copies(row, carry, block=block, value=value):
-            out[row * blocks + block, :size] = value
-            return carry
-
-        lax.fori_loop(0, devices // blocks, copies, 0, unroll=4)
-    first = lax.broadcasted_iota(jnp.int32, (8, LANE), 0) < 6
-
-    def forward(device, carry):
-        pieces = [
-            received[jnp.bitwise_xor(device, table[which])].astype(jnp.float32) for which in range(2)
-        ]
-        out[device, size:] = jnp.where(first, pieces[0], pieces[1]).astype(jnp.bfloat16)
-        return carry
-
-    lax.fori_loop(0, devices, forward, 0, unroll=4)
-
-
-def product_kernel(placed, inverse, packed, out, their_modes, pairs, left, parts):
-    at_step = pl.program_id(0)
+    ready[...] = staged[...].astype(jnp.bfloat16)
+    copies = [
+        pltpu.make_async_copy(
+            ready, out.at[pl.ds(row * blocks, blocks), pl.ds(0, size)], sent.at[row]
+        )
+        for row in range(devices // blocks)
+    ]
+    for copy in copies:
+        copy.start()
+    for copy in copies:
+        copy.wait()
+    shares.wait()
+
+
+def product_kernel(
+    placed, inverse, packed, out, their_modes, pairs, left, parts, blocks, read, sent
+):
     groups = placed.shape[0] // 4
     tiles, steps = pairs.shape[0], parts.shape[0]
-
-    @pl.when(at_step == 0)
-    def _():
-        def step(group, carry):
-            rows = [placed[group * 4 + inner, : 2 * tiles].astype(jnp.float32) for inner in range(4)]
-            at = pl.multiple_of(group * 8, 8)
-            for tile in range(tiles):
-                taken = [piece[2 * tile : 2 * tile + 2] for piece in rows]
-                pairs[tile, pl.ds(at, 8)] = jnp.concatenate(taken, 0)
-            return carry
-
-        lax.fori_loop(0, groups, step, 0)
+    size = out.shape[1] - packed.shape[1]
+    taken = inverse.shape[0] // steps
+    loads = [
+        pltpu.make_async_copy(inverse.at[pl.ds(step * taken, taken)], blocks.at[step], read.at[step])
+        for step in range(steps)
+    ]
+    for load in loads:
+        load.start()
+    chunks = pltpu.make_async_copy(packed, out.at[:, pl.ds(size, packed.shape[1])], sent)
+    chunks.start()
+
+    def order(group, carry):
+        rows = [placed[group * 4 + inner, : 2 * tiles].astype(jnp.float32) for inner in range(4)]
+        at = pl.multiple_of(group * 8, 8)
         for tile in range(tiles):
-            left[:, tile * LANE : (tile + 1) * LANE] = pairs[tile].astype(jnp.bfloat16)
-
-    @pl.when(at_step == 1)
-    def _():
-        def step(group, carry):
-            for inner in range(8):
-                row = pl.multiple_of(group * 8, 8) + inner
-                tile = placed[row, 2 * tiles :].astype(jnp.float32)
-                for kind in range(4):
-                    pairs[kind, pl.ds(row, 1)] = tile[4 + kind : 5 + kind]
-            return carry
-
-        lax.fori_loop(0, placed.shape[0] // 8, step, 0)
-        for kind in range(4):
-            value = pairs[kind, : placed.shape[0]].astype(jnp.bfloat16)
-            their_modes[kind] = value.reshape(their_modes.shape[1:])
-
-    parts[at_step] = lax.dot_general(
-        left[...], inverse[...], (((1,), (1,)), ((), ())), preferred_element_type=jnp.float32
-    )
-
-    @pl.when(at_step == steps - 1)
-    def _():
-        size = steps * parts.shape[2] // LANE * 2
-
-        def step(group, carry):
-            at = pl.multiple_of(group * 8, 8)
-            tall = [
-                parts[part, pl.ds(at, 8), lane * LANE : (lane + 1) * LANE]
-                for part in range(steps)
-                for lane in range(parts.shape[2] // LANE)
-            ]
-            for inner in range(4):
-                rows = jnp.concatenate([tile[2 * inner : 2 * inner + 2] for tile in tall], 0)
-                out[group * 4 + inner, :size] = rows.astype(jnp.bfloat16)
-                out[group * 4 + inner, size:] = packed[group * 4 + inner]
-            return carry
-
-        lax.fori_loop(0, groups, step, 0)
+            piece = [row[2 * tile : 2 * tile + 2] for row in rows]
+            pairs[tile, pl.ds(at, 8)] = jnp.concatenate(piece, 0)
+        return carry
+
+    lax.fori_loop(0, groups, order, 0)
+    for tile in range(tiles):
+        left[:, tile * LANE : (tile + 1) * LANE] = pairs[tile].astype(jnp.bfloat16)
+
+    def order_modes(group, carry):
+        for inner in range(8):
+            row = pl.multiple_of(group * 8, 8) + inner
+            tile = placed[row, 2 * tiles :].astype(jnp.float32)
+            for kind in range(4):
+                pairs[kind, pl.ds(row, 1)] = tile[4 + kind : 5 + kind]
+        return carry
+
+    lax.fori_loop(0, placed.shape[0] // 8, order_modes, 0)
+    for kind in range(4):
+        value = pairs[kind, : placed.shape[0]].astype(jnp.bfloat16)
+        their_modes[kind] = value.reshape(their_modes.shape[1:])
+    for step in range(steps):
+        loads[step].wait()
+        parts[step] = lax.dot_general(
+            left[...], blocks[step], (((1,), (1,)), ((), ())), preferred_element_type=jnp.float32
+        )
+    chunks.wait()
+
+    def leave(group, carry):
+        at = pl.multiple_of(group * 8, 8)
+        tall = [
+            parts[part, pl.ds(at, 8), lane * LANE : (lane + 1) * LANE]
+            for part in range(steps)
+            for lane in range(parts.shape[2] // LANE)
+        ]
+        for inner in range(4):
+            rows = jnp.concatenate([tile[2 * inner : 2 * inner + 2] for tile in tall], 0)
+            out[group * 4 + inner, :size] = rows.astype(jnp.bfloat16)
+        return carry
+
+    lax.fori_loop(0, groups, leave, 0)
 
 
 def gather_kernel(table, received, partial, out, solved, chosen_rows, *, row_blocks):
@@ -466,14 +484,19 @@
     packed = packed.reshape(devices, 32, LANE)
 
     rows, columns = coarse_inverse.shape
+    blocks = LANE * LANE // columns
     placed = call(
         scatter_kernel,
-        jax.ShapeDtypeStruct((devices, 2 * columns // LANE + 8, LANE), jnp.bfloat16),
+        pltpu.HBM((devices, 2 * columns // LANE + 8, LANE), jnp.bfloat16),
         in_specs=[smem(), whole()],
-        out_specs=whole(),
+        out_specs=hbm,
         scratch_shapes=[
             pltpu.VMEM((2 * LANE, LANE), jnp.float32),
-            pltpu.VMEM((LANE * LANE // columns, 2 * columns // LANE, LANE), jnp.float32),
+            pltpu.VMEM((blocks, 2 * columns // LANE, LANE), jnp.float32),
+            pltpu.VMEM((blocks, 2 * columns // LANE, LANE), jnp.bfloat16),
+            pltpu.VMEM((devices, 8, LANE), jnp.bfloat16),
+            pltpu.SemaphoreType.DMA((devices // blocks,)),
+            pltpu.SemaphoreType.DMA(()),
         ],
     )(table, received)
     placed = spread(placed)
@@ -486,17 +509,15 @@
             jax.ShapeDtypeStruct(joined_shape, jnp.bfloat16),
             jax.ShapeDtypeStruct(modes_shape, jnp.bfloat16),
         ),
-        grid=(steps,),
-        in_specs=[
-            same(*placed.shape),
-            pl.BlockSpec((rows // steps, columns), lambda step: (step, 0)),
-            same(*packed.shape),
-        ],
-        out_specs=(same(*joined_shape), same(*modes_shape)),
+        in_specs=[whole(), hbm, hbm],
+        out_specs=(whole(), whole()),
         scratch_shapes=[
             pltpu.VMEM((columns // LANE, cases, LANE), jnp.float32),
             pltpu.VMEM((cases, columns), jnp.bfloat16),
             pltpu.VMEM((steps, cases, rows // steps), jnp.float32),
+            pltpu.VMEM((steps, rows // steps, columns), jnp.bfloat16),
+            pltpu.SemaphoreType.DMA((steps,)),
+            pltpu.SemaphoreType.DMA(()),
         ],
     )(placed, in_hbm(coarse_inverse), in_hbm(packed))
     joined = spread(joined)
@@ -514,18 +535,15 @@
     return call(
         finish_kernel,
         field,
-        grid=(count // SUBS,),
-        in_specs=[
-            smem(),
-            per_sub(trace_len, cases, subs=SUBS),
-            per_sub(MODES, trace_len, subs=SUBS),
-            same(*last.shape),
-            same(*modes_shape),
-        ],
-        out_specs=per_sub(trace_len, cases, subs=SUBS),
+        in_specs=[smem(), hbm, whole(), whole(), whole()],
+        out_specs=hbm,
         scratch_shapes=[
             pltpu.VMEM((3, cases, LANE), jnp.float32),
             pltpu.VMEM((3, count, MODES, cases), jnp.bfloat16),
+            pltpu.VMEM(residual.shape, jnp.float32),
+            pltpu.VMEM(residual.shape, jnp.bfloat16),
+            pltpu.SemaphoreType.DMA((count,)),
+            pltpu.SemaphoreType.DMA((count,)),
         ],
     )(table, in_hbm(local_part), turned_modes, last, their_modes)
 

time: 175 us -> 174 us (level)
  no operation moved by 1% of the time
where the time goes in v10:
time: 174 us; the launch traced here: 173 us
  blocking collectives  93.4 us (54%)
  waiting for transfers between devices  30.6 us (18%)
  Pallas kernels  30 us (17%)
  starting transfers between devices  15.8 us (9%)
    all_to_all x4, blocking collectives, spread(): return lax.all_to_all(value, AXES, 0, 0, tiled=True)  93.4 us
    all_to_all x2, waiting for transfers between devices, spread(): return lax.all_to_all(value, AXES, 0, 0, tiled=True)  30.6 us
    all_to_all x2, starting transfers between devices, spread(): return lax.all_to_all(value, AXES, 0, 0, tiled=True)  15.8 us
    pallas_call x1, Pallas kernels, shards(): call(local_kernel, (pltpu.HBM(residual.shape, jnp.float32), pltpu.HBM(pac...  7.67 us
    pallas_call x1, Pallas kernels, shards(): call(scatter_kernel, pltpu.HBM((devices, 2 * columns // LANE + 8, LANE),...  4.59 us
    pallas_call x1, Pallas kernels, shards(): call(finish_kernel, field, in_specs=[smem(), hbm, whole(), whole(), whole...  4.5 us
    pallas_call x1, Pallas kernels, shards(): call(functools.partial(gather_kernel, row_blocks=lax.axis_size('row')), j...  3.64 us
  transfers between devices with their start and end apart: 2, of which 2 were waited for; matrix products, arithmetic and copies ran while one was open for 1% of the time, Pallas kernels for 4%

profile of v10, /device:TPU:1, one launch (start us, length us, event | category | flops | bytes accessed | tf_op | source)
XLA Modules:
  0.0 173.1 jit_solution(14291938866531314736)
XLA Ops:
  0.0 0.7 copy-done.3
  0.7 2.7 %shard_map.82 = bf16[4,2,16,4,8,128]{5,4,3,2,1,0:T(8,128)(2,1)} custom-call(s32[2,4]{1,0:T(2,128)S(1)} %bitcast.20, bf16[4,128,2,8,128]{4,3,2,1,0:T(8,128)(2,1)} %bitcast.14), custom_call_target="tpu_custom_call" | custom-call | tf_op jit(solution)/shard_map/pallas_call | solution.py:434
  3.4 0.0 copy-start.7
  3.4 11.5 %all-to-all-start = ((bf16[128,32,128]{2,1,0:T(8,128)(2,1)}), bf16[128,32,128]{2,1,0:T(8,128)(2,1)S(1)}, u32[]{:S(2)}, u32[]{:S(2)}) async-start(bf16[128,32,128]{2,1,0:T(8,128)(2,1)} %bitcast.22), calls=%async_computation | async-start | bytes 2097152 | tf_op jit(solution)/shard_map/all_to_all | solution.py:20
  14.9 0.0 copy-done.4
  15.0 0.0 copy-done.5
  15.0 0.1 copy.13
  15.1 0.1 reshape.31
  15.2 0.1 copy.12
  15.3 0.1 reshape.30
  15.4 0.0 copy-done.6
  15.4 0.1 slice_reduce_fusion
  15.5 0.1 copy.14
  15.7 0.1 pad_add_fusion.table
  15.8 0.3 broadcast_select_fusion
  16.1 0.3 pad_maximum_fusion.1
  16.4 0.8 pad_maximum_fusion.base
  17.2 16.6 %all-to-all-done.chunks = bf16[128,32,128]{2,1,0:T(8,128)(2,1)S(1)} async-done(((bf16[128,32,128]{2,1,0:T(8,128)(2,1)}), bf16[128,32,128]{2,1,0:T(8,128)(2,1)S(1)}, u32[]{:S(2)}, u32[]{:S(2)}) %all-to-all-start) | async-done | bytes 1048608 | tf_op jit(solution)/shard_map/all_to_all | solution.py:20
  33.8 0.9 shard_map.83
  34.7 23.3 %all_to_all.30 = bf16[128,32,128]{2,1,0:T(8,128)(2,1)S(1)} all-to-all(bf16[128,32,128]{2,1,0:T(8,128)(2,1)S(1)} %shard_map.83), channel_id=1, replica_groups=mesh['row'=16,'col'=8] {'row','col'}, dimensions={0} | all-to-all | bytes 2097152 | tf_op jit(solution)/shard_map/all_to_all | solution.py:20
  58.0 0.0 copy-done
  58.0 2.6 %shard_map.84 = (bf16[4,1024,256]{2,1,0:T(8,128)(2,1)}, bf16[128,8,128]{2,1,0:T(8,128)(2,1)S(1)}) custom-call(s32[20]{0:T(128)S(1)} %pad_add_fusion.table, bf16[4,1024,256]{2,1,0:T(8,128)(2,1)S(1)} %copy-done, bf16[4,32,1024]{2,1,0:T(8,128)(2,1)S(1)} %bitcast.18, bf16[4,2,16,4,8,128]{5,4,3,2,1,0:T(8,128)(2,1)S(1)} %bitcast.16, bf16[128,8,128]{2,1,0:T(8,128)(2,1)S(1)} %copy-done.2), custom_call_target="tpu_custom_call" | custom-call | tf_op jit(solution)/shard_map/pallas_call | solution.py:454
  60.6 15.5 %all_to_all.31.received = bf16[128,8,128]{2,1,0:T(8,128)(2,1)S(1)} all-to-all(bf16[128,8,128]{2,1,0:T(8,128)(2,1)S(1)} %get-tuple-element.18), channel_id=1, replica_groups=mesh['row'=16,'col'=8] {'row','col'}, dimensions={0} | all-to-all | bytes 524288 | tf_op jit(solution)/shard_map/all_to_all | solution.py:20
  76.1 4.6 %shard_map.86 = bf16[128,40,128]{2,1,0:T(8,128)(2,1)} custom-call(s32[20]{0:T(128)S(1)} %pad_add_fusion.table, bf16[128,8,128]{2,1,0:T(8,128)(2,1)S(1)} %all_to_all.31.received), custom_call_target="tpu_custom_call" | custom-call | tf_op jit(solution)/shard_map/pallas_call | solution.py:488
  80.7 4.3 %all-to-all-start.3 = ((bf16[128,40,128]{2,1,0:T(8,128)(2,1)}), bf16[128,40,128]{2,1,0:T(8,128)(2,1)S(1)}, u32[]{:S(2)}, u32[]{:S(2)}) async-start(bf16[128,40,128]{2,1,0:T(8,128)(2,1)} %shard_map.86), calls=%async_computation.3 | async-start | bytes 2621440 | tf_op jit(solution)/shard_map/all_to_all | solution.py:20
  85.0 7.7 %shard_map.85 = (f32[4,1024,256]{2,1,0:T(8,128)}, bf16[4,2,16,4,8,128]{5,4,3,2,1,0:T(8,128)(2,1)}) custom-call(s32[2,4]{1,0:T(2,128)S(1)} %bitcast.21, bf16[4,1024,1024]{2,1,0:T(8,128)(2,1)} %inverse.2, bf16[4,1024,256]{2,1,0:T(8,128)(2,1)} %get-tuple-element.19.weighted), custom_call_target="tpu_custom_call" | custom-call | tf_op jit(solution)/shard_map/pallas_call | solution.py:474
  92.7 14.0 %all-to-all-done.3.placed = bf16[128,40,128]{2,1,0:T(8,128)(2,1)S(1)} async-done(((bf16[128,40,128]{2,1,0:T(8,128)(2,1)}), bf16[128,40,128]{2,1,0:T(8,128)(2,1)S(1)}, u32[]{:S(2)}, u32[]{:S(2)}) %all-to-all-start.3) | async-done | bytes 1310752 | tf_op jit(solution)/shard_map/all_to_all | solution.py:20
  106.7 3.5 %shard_map.87 = (bf16[128,48,128]{2,1,0:T(8,128)(2,1)S(1)}, bf16[4,4,32,128]{3,2,1,0:T(8,128)(2,1)S(1)}) custom-call(bf16[128,40,128]{2,1,0:T(8,128)(2,1)S(1)} %all-to-all-done.3.placed, bf16[1024,2048]{1,0:T(8,128)(2,1)} %inverse.3, bf16[128,32,128]{2,1,0:T(8,128)(2,1)} %bitcast.23), custom_call_target="tpu_custom_call" | custom-call | tf_op jit(solution)/shard_map/pallas_call | solution.py:506
  110.2 28.8 %all_to_all.32.partial = bf16[128,48,128]{2,1,0:T(8,128)(2,1)S(1)} all-to-all(bf16[128,48,128]{2,1,0:T(8,128)(2,1)S(1)} %get-tuple-element.23), channel_id=1, replica_groups=mesh['row'=16,'col'=8] {'row','col'}, dimensions={0} | all-to-all | bytes 3145728 | tf_op jit(solution)/shard_map/all_to_all | solution.py:20
  139.0 3.6 %shard_map.88 = bf16[128,40,128]{2,1,0:T(8,128)(2,1)S(1)} custom-call(s32[20]{0:T(128)S(1)} %pad_add_fusion.table, bf16[128,8,128]{2,1,0:T(8,128)(2,1)S(1)} %all_to_all.31.received, bf16[128,48,128]{2,1,0:T(8,128)(2,1)S(1)} %all_to_all.32.partial), custom_call_target="tpu_custom_call" | custom-call | tf_op jit(solution)/shard_map/pallas_call | solution.py:524
  142.6 25.9 %all_to_all.33 = bf16[128,40,128]{2,1,0:T(8,128)(2,1)S(1)} all-to-all(bf16[128,40,128]{2,1,0:T(8,128)(2,1)S(1)} %shard_map.88), channel_id=1, replica_groups=mesh['row'=16,'col'=8] {'row','col'}, dimensions={0} | all-to-all | bytes 2621440 | tf_op jit(solution)/shard_map/all_to_all | solution.py:20
  168.5 4.5 %shard_map.89 = bf16[4,1024,256]{2,1,0:T(8,128)(2,1)} custom-call(s32[20]{0:T(128)S(1)} %pad_add_fusion.table, f32[4,1024,256]{2,1,0:T(8,128)} %get-tuple-element.20.local, bf16[4,32,1024]{2,1,0:T(8,128)(2,1)S(1)} %bitcast.19, bf16[4,2,16,5,8,128]{5,4,3,2,1,0:T(8,128)(2,1)S(1)} %bitcast.15, bf16[4,4,32,128]{3,2,1,0:T(8,128)(2,1)S(1)} %get-tuple-element.24.their_modes), custom_call_target="tpu_custom_call" | custom-call | tf_op jit(solution)/shard_map/pallas_call | solution.py:535
  (18 shorter events, 0.2 us)
Async XLA Ops:
  0.0 0.7 copy-start.3
  0.7 14.3 %copy-start.4 = (s32[4,2]{0,1:T(2,128)S(1)}, s32[4,2]{0,1:T(2,128)}, u32[]{:S(2)}) copy-start(s32[4,2]{0,1:T(2,128)} %param.15) | copy-start | bytes 100
  0.7 14.3 %copy-start.5 = (s32[4,2]{0,1:T(2,128)S(1)}, s32[4,2]{0,1:T(2,128)}, u32[]{:S(2)}) copy-start(s32[4,2]{0,1:T(2,128)} %param.14) | copy-start | bytes 100
  0.7 14.7 %copy-start.6 = (s32[4,2]{0,1:T(2,128)S(1)}, s32[4,2]{0,1:T(2,128)}, u32[]{:S(2)}) copy-start(s32[4,2]{0,1:T(2,128)} %param.13) | copy-start | bytes 100
  0.7 14.9 %copy-start.1 = (bf16[4,1024,32]{1,2,0:T(8,128)(2,1)S(1)}, bf16[4,1024,32]{1,2,0:T(8,128)(2,1)}, u32[]{:S(2)}) copy-start(bf16[4,1024,32]{1,2,0:T(8,128)(2,1)} %param.10) | copy-start | bytes 786436
  3.4 12.3 %copy-start.7 = (s32[128]{0:T(128)S(1)}, s32[128]{0:T(128)}, u32[]{:S(2)}) copy-start(s32[128]{0:T(128)} %param.11) | copy-start | bytes 1540
  3.4 30.4 %all-to-all-start = ((bf16[128,32,128]{2,1,0:T(8,128)(2,1)}), bf16[128,32,128]{2,1,0:T(8,128)(2,1)S(1)}, u32[]{:S(2)}, u32[]{:S(2)}) async-start(bf16[128,32,128]{2,1,0:T(8,128)(2,1)} %bitcast.22), calls=%async_computation | async-start | bytes 2097152 | tf_op jit(solution)/shard_map/all_to_all | solution.py:20
  17.2 40.8 %copy-start = (bf16[4,1024,256]{2,1,0:T(8,128)(2,1)S(1)}, bf16[4,1024,256]{2,1,0:T(8,128)(2,1)}, u32[]{:S(2)}) copy-start(bf16[4,1024,256]{2,1,0:T(8,128)(2,1)} %residual.1) | copy-start | bytes 6291460
  33.8 24.2 %copy-start.2 = (bf16[128,8,128]{2,1,0:T(8,128)(2,1)S(1)}, bf16[128,8,128]{2,1,0:T(8,128)(2,1)}, u32[]{:S(2)}) copy-start(bf16[128,8,128]{2,1,0:T(8,128)(2,1)} %pad_maximum_fusion.base) | copy-start | bytes 786436
  80.7 26.0 %all-to-all-start.3 = ((bf16[128,40,128]{2,1,0:T(8,128)(2,1)}), bf16[128,40,128]{2,1,0:T(8,128)(2,1)S(1)}, u32[]{:S(2)}, u32[]{:S(2)}) async-start(bf16[128,40,128]{2,1,0:T(8,128)(2,1)} %shard_map.86), calls=%async_computation.3 | async-start | bytes 2621440 | tf_op jit(solution)/shard_map/all_to_all | solution.py:20

commit v11 on v10

--- a/solution.py
+++ b/solution.py
@@ -227,11 +227,11 @@
         pieces = [
             received[jnp.bitwise_xor(device, table[which])].astype(jnp.float32) for which in range(2)
         ]
-        shared[device] = jnp.where(first, pieces[0], pieces[1]).astype(jnp.bfloat16)
+        shared[device, 0] = jnp.where(first, pieces[0], pieces[1])[4:].astype(jnp.bfloat16)
         return carry
 
     lax.fori_loop(0, devices, forward, 0, unroll=4)
-    shares = pltpu.make_async_copy(shared, out.at[:, pl.ds(staged.shape[1], 8)], shared_sent)
+    shares = pltpu.make_async_copy(shared, out.at[:, pl.ds(staged.shape[1], 1)], shared_sent)
     shares.start()
     total[...] = jnp.zeros_like(total)
 
@@ -256,13 +256,14 @@
         return carry
 
     lax.fori_loop(0, devices // GROUP, step, 0)
-    blocks, size, _ = staged.shape
-    pieces = size // 2
+    blocks, size, rows, _ = staged.shape
+    pieces = size * rows // 2
     for block in range(blocks):
         for case in range(2):
             for piece in range(pieces):
                 at = case * LANE + block * pieces + piece
-                staged[block, piece * 2 + case : piece * 2 + case + 1] = total[at : at + 1]
+                tile, row = divmod(piece * 2 + case, rows)
+                staged[block, tile, row : row + 1] = total[at : at + 1]
     ready[...] = staged[...].astype(jnp.bfloat16)
     copies = [
         pltpu.make_async_copy(
@@ -294,10 +295,11 @@
     chunks.start()
 
     def order(group, carry):
-        rows = [placed[group * 4 + inner, : 2 * tiles].astype(jnp.float32) for inner in range(4)]
+        rows = [placed[group * 4 + inner, : tiles // 2].astype(jnp.float32) for inner in range(4)]
         at = pl.multiple_of(group * 8, 8)
         for tile in range(tiles):
-            piece = [row[2 * tile : 2 * tile + 2] for row in rows]
+            first = tile % 2 * 2
+            piece = [row[tile // 2, first : first + 2] for row in rows]
             pairs[tile, pl.ds(at, 8)] = jnp.concatenate(piece, 0)
         return carry
 
@@ -308,9 +310,9 @@
     def order_modes(group, carry):
         for inner in range(8):
             row = pl.multiple_of(group * 8, 8) + inner
-            tile = placed[row, 2 * tiles :].astype(jnp.float32)
+            tile = placed[row, tiles // 2].astype(jnp.float32)
             for kind in range(4):
-                pairs[kind, pl.ds(row, 1)] = tile[4 + kind : 5 + kind]
+                pairs[kind, pl.ds(row, 1)] = tile[kind : kind + 1]
         return carry
 
     lax.fori_loop(0, placed.shape[0] // 8, order_modes, 0)
@@ -485,16 +487,17 @@
 
     rows, columns = coarse_inverse.shape
     blocks = LANE * LANE // columns
+    tiles = columns // LANE // 2
     placed = call(
         scatter_kernel,
-        pltpu.HBM((devices, 2 * columns // LANE + 8, LANE), jnp.bfloat16),
+        pltpu.HBM((devices, tiles + 1, 4, LANE), jnp.bfloat16),
         in_specs=[smem(), whole()],
         out_specs=hbm,
         scratch_shapes=[
             pltpu.VMEM((2 * LANE, LANE), jnp.float32),
-            pltpu.VMEM((blocks, 2 * columns // LANE, LANE), jnp.float32),
-            pltpu.VMEM((blocks, 2 * columns // LANE, LANE), jnp.bfloat16),
-            pltpu.VMEM((devices, 8, LANE), jnp.bfloat16),
+            pltpu.VMEM((blocks, tiles, 4, LANE), jnp.float32),
+            pltpu.VMEM((blocks, tiles, 4, LANE), jnp.bfloat16),
+            pltpu.VMEM((devices, 1, 4, LANE), jnp.bfloat16),
             pltpu.SemaphoreType.DMA((devices // blocks,)),
             pltpu.SemaphoreType.DMA(()),
         ],

time: 174 us -> 172 us (0.989)
  no operation moved by 1% of the time
where the time goes in v11:
time: 172 us
  blocking collectives  93.5 us (54%)
  Pallas kernels  30.1 us (18%)
  waiting for transfers between devices  29.2 us (17%)
  starting transfers between devices  15.8 us (9%)
    all_to_all x4, blocking collectives, spread(): return lax.all_to_all(value, AXES, 0, 0, tiled=True)  93.5 us
    all_to_all x2, waiting for transfers between devices, spread(): return lax.all_to_all(value, AXES, 0, 0, tiled=True)  29.2 us
    all_to_all x2, starting transfers between devices, spread(): return lax.all_to_all(value, AXES, 0, 0, tiled=True)  15.8 us
    pallas_call x1, Pallas kernels, shards(): call(local_kernel, (pltpu.HBM(residual.shape, jnp.float32), pltpu.HBM(pac...  7.68 us
    pallas_call x1, Pallas kernels, shards(): call(scatter_kernel, pltpu.HBM((devices, tiles + 1, 4, LANE), jnp.bfloat1...  4.66 us
    pallas_call x1, Pallas kernels, shards(): call(finish_kernel, field, in_specs=[smem(), hbm, whole(), whole(), whole...  4.5 us
    pallas_call x1, Pallas kernels, shards(): call(functools.partial(gather_kernel, row_blocks=lax.axis_size('row')), j...  3.64 us
    pallas_call x1, Pallas kernels, shards(): call(product_kernel, (jax.ShapeDtypeStruct(joined_shape, jnp.bfloat16), j...  3.48 us
  transfers between devices with their start and end apart: 2, of which 2 were waited for; matrix products, arithmetic and copies ran while one was open for 1% of the time, Pallas kernels for 4%

profile of v11, /device:TPU:1, one launch (start us, length us, event | category | flops | bytes accessed | tf_op | source)
XLA Modules:
  0.0 171.9 jit_solution(14694045627741764881)
XLA Ops:
  0.0 0.7 copy-done.3
  0.7 2.7 %shard_map.82 = bf16[4,2,16,4,8,128]{5,4,3,2,1,0:T(8,128)(2,1)} custom-call(s32[2,4]{1,0:T(2,128)S(1)} %bitcast.20, bf16[4,128,2,8,128]{4,3,2,1,0:T(8,128)(2,1)} %bitcast.14), custom_call_target="tpu_custom_call" | custom-call | tf_op jit(solution)/shard_map/pallas_call | solution.py:436
  3.4 0.0 copy-start.7
  3.4 11.5 %all-to-all-start = ((bf16[128,32,128]{2,1,0:T(8,128)(2,1)}), bf16[128,32,128]{2,1,0:T(8,128)(2,1)S(1)}, u32[]{:S(2)}, u32[]{:S(2)}) async-start(bf16[128,32,128]{2,1,0:T(8,128)(2,1)} %bitcast.22), calls=%async_computation | async-start | bytes 2097152 | tf_op jit(solution)/shard_map/all_to_all | solution.py:20
  14.9 0.0 copy-done.4
  15.0 0.0 copy-done.5
  15.0 0.1 copy.13
  15.1 0.1 reshape.31
  15.2 0.1 copy.12
  15.3 0.1 reshape.30
  15.4 0.0 copy-done.6
  15.4 0.1 slice_reduce_fusion
  15.5 0.1 copy.14
  15.6 0.0 copy-done.1
  15.7 0.1 pad_add_fusion.table
  15.8 0.3 broadcast_select_fusion
  16.1 0.3 pad_maximum_fusion.1
  16.4 0.8 pad_maximum_fusion.base
  17.2 16.6 %all-to-all-done.chunks = bf16[128,32,128]{2,1,0:T(8,128)(2,1)S(1)} async-done(((bf16[128,32,128]{2,1,0:T(8,128)(2,1)}), bf16[128,32,128]{2,1,0:T(8,128)(2,1)S(1)}, u32[]{:S(2)}, u32[]{:S(2)}) %all-to-all-start) | async-done | bytes 1048608 | tf_op jit(solution)/shard_map/all_to_all | solution.py:20
  33.8 0.9 shard_map.83
  34.7 23.3 %all_to_all.30 = bf16[128,32,128]{2,1,0:T(8,128)(2,1)S(1)} all-to-all(bf16[128,32,128]{2,1,0:T(8,128)(2,1)S(1)} %shard_map.83), channel_id=1, replica_groups=mesh['row'=16,'col'=8] {'row','col'}, dimensions={0} | all-to-all | bytes 2097152 | tf_op jit(solution)/shard_map/all_to_all | solution.py:20
  58.0 2.6 %shard_map.84 = (bf16[4,1024,256]{2,1,0:T(8,128)(2,1)}, bf16[128,8,128]{2,1,0:T(8,128)(2,1)S(1)}) custom-call(s32[20]{0:T(128)S(1)} %pad_add_fusion.table, bf16[4,1024,256]{2,1,0:T(8,128)(2,1)S(1)} %copy-done, bf16[4,32,1024]{2,1,0:T(8,128)(2,1)S(1)} %bitcast.18, bf16[4,2,16,4,8,128]{5,4,3,2,1,0:T(8,128)(2,1)S(1)} %bitcast.16, bf16[128,8,128]{2,1,0:T(8,128)(2,1)S(1)} %copy-done.2), custom_call_target="tpu_custom_call" | custom-call | tf_op jit(solution)/shard_map/pallas_call | solution.py:456
  60.6 15.5 %all_to_all.31.received = bf16[128,8,128]{2,1,0:T(8,128)(2,1)S(1)} all-to-all(bf16[128,8,128]{2,1,0:T(8,128)(2,1)S(1)} %get-tuple-element.18), channel_id=1, replica_groups=mesh['row'=16,'col'=8] {'row','col'}, dimensions={0} | all-to-all | bytes 524288 | tf_op jit(solution)/shard_map/all_to_all | solution.py:20
  76.1 4.7 %shard_map.86 = bf16[128,9,4,128]{3,2,1,0:T(4,128)(2,1)} custom-call(s32[20]{0:T(128)S(1)} %pad_add_fusion.table, bf16[128,8,128]{2,1,0:T(8,128)(2,1)S(1)} %all_to_all.31.received), custom_call_target="tpu_custom_call" | custom-call | tf_op jit(solution)/shard_map/pallas_call | solution.py:491
  80.7 4.3 %all-to-all-start.3 = ((bf16[128,9,4,128]{3,2,1,0:T(4,128)(2,1)}), bf16[128,9,4,128]{3,2,1,0:T(4,128)(2,1)S(1)}, u32[]{:S(2)}, u32[]{:S(2)}) async-start(bf16[128,9,4,128]{3,2,1,0:T(4,128)(2,1)} %shard_map.86), calls=%async_computation.3 | async-start | bytes 2359296 | tf_op jit(solution)/shard_map/all_to_all | solution.py:20
  85.1 7.7 %shard_map.85 = (f32[4,1024,256]{2,1,0:T(8,128)}, bf16[4,2,16,4,8,128]{5,4,3,2,1,0:T(8,128)(2,1)}) custom-call(s32[2,4]{1,0:T(2,128)S(1)} %bitcast.21, bf16[4,1024,1024]{2,1,0:T(8,128)(2,1)} %inverse.2, bf16[4,1024,256]{2,1,0:T(8,128)(2,1)} %get-tuple-element.19.weighted), custom_call_target="tpu_custom_call" | custom-call | tf_op jit(solution)/shard_map/pallas_call | solution.py:476
  92.7 12.6 %all-to-all-done.3.placed = bf16[128,9,4,128]{3,2,1,0:T(4,128)(2,1)S(1)} async-done(((bf16[128,9,4,128]{3,2,1,0:T(4,128)(2,1)}), bf16[128,9,4,128]{3,2,1,0:T(4,128)(2,1)S(1)}, u32[]{:S(2)}, u32[]{:S(2)}) %all-to-all-start.3) | async-done | bytes 1179680 | tf_op jit(solution)/shard_map/all_to_all | solution.py:20
  105.4 3.5 %shard_map.87 = (bf16[128,48,128]{2,1,0:T(8,128)(2,1)S(1)}, bf16[4,4,32,128]{3,2,1,0:T(8,128)(2,1)S(1)}) custom-call(bf16[128,9,4,128]{3,2,1,0:T(4,128)(2,1)S(1)} %all-to-all-done.3.placed, bf16[1024,2048]{1,0:T(8,128)(2,1)} %inverse.3, bf16[128,32,128]{2,1,0:T(8,128)(2,1)} %bitcast.23), custom_call_target="tpu_custom_call" | custom-call | tf_op jit(solution)/shard_map/pallas_call | solution.py:509
  108.9 28.9 %all_to_all.32.partial = bf16[128,48,128]{2,1,0:T(8,128)(2,1)S(1)} all-to-all(bf16[128,48,128]{2,1,0:T(8,128)(2,1)S(1)} %get-tuple-element.23), channel_id=1, replica_groups=mesh['row'=16,'col'=8] {'row','col'}, dimensions={0} | all-to-all | bytes 3145728 | tf_op jit(solution)/shard_map/all_to_all | solution.py:20
  137.7 3.6 %shard_map.88 = bf16[128,40,128]{2,1,0:T(8,128)(2,1)S(1)} custom-call(s32[20]{0:T(128)S(1)} %pad_add_fusion.table, bf16[128,8,128]{2,1,0:T(8,128)(2,1)S(1)} %all_to_all.31.received, bf16[128,48,128]{2,1,0:T(8,128)(2,1)S(1)} %all_to_all.32.partial), custom_call_target="tpu_custom_call" | custom-call | tf_op jit(solution)/shard_map/pallas_call | solution.py:527
  141.4 25.9 %all_to_all.33 = bf16[128,40,128]{2,1,0:T(8,128)(2,1)S(1)} all-to-all(bf16[128,40,128]{2,1,0:T(8,128)(2,1)S(1)} %shard_map.88), channel_id=1, replica_groups=mesh['row'=16,'col'=8] {'row','col'}, dimensions={0} | all-to-all | bytes 2621440 | tf_op jit(solution)/shard_map/all_to_all | solution.py:20
  167.2 4.5 %shard_map.89 = bf16[4,1024,256]{2,1,0:T(8,128)(2,1)} custom-call(s32[20]{0:T(128)S(1)} %pad_add_fusion.table, f32[4,1024,256]{2,1,0:T(8,128)} %get-tuple-element.20.local, bf16[4,32,1024]{2,1,0:T(8,128)(2,1)S(1)} %bitcast.19, bf16[4,2,16,5,8,128]{5,4,3,2,1,0:T(8,128)(2,1)S(1)} %bitcast.15, bf16[4,4,32,128]{3,2,1,0:T(8,128)(2,1)S(1)} %get-tuple-element.24.their_modes), custom_call_target="tpu_custom_call" | custom-call | tf_op jit(solution)/shard_map/pallas_call | solution.py:538
  (18 shorter events, 0.2 us)
Async XLA Ops:
  0.0 0.7 copy-start.3
  0.7 14.3 %copy-start.4 = (s32[4,2]{0,1:T(2,128)S(1)}, s32[4,2]{0,1:T(2,128)}, u32[]{:S(2)}) copy-start(s32[4,2]{0,1:T(2,128)} %param.15) | copy-start | bytes 100
  0.7 14.3 %copy-start.5 = (s32[4,2]{0,1:T(2,128)S(1)}, s32[4,2]{0,1:T(2,128)}, u32[]{:S(2)}) copy-start(s32[4,2]{0,1:T(2,128)} %param.14) | copy-start | bytes 100
  0.7 14.7 %copy-start.6 = (s32[4,2]{0,1:T(2,128)S(1)}, s32[4,2]{0,1:T(2,128)}, u32[]{:S(2)}) copy-start(s32[4,2]{0,1:T(2,128)} %param.13) | copy-start | bytes 100
  0.7 14.9 %copy-start.1 = (bf16[4,1024,32]{1,2,0:T(8,128)(2,1)S(1)}, bf16[4,1024,32]{1,2,0:T(8,128)(2,1)}, u32[]{:S(2)}) copy-start(bf16[4,1024,32]{1,2,0:T(8,128)(2,1)} %param.10) | copy-start | bytes 786436
  3.4 12.3 %copy-start.7 = (s32[128]{0:T(128)S(1)}, s32[128]{0:T(128)}, u32[]{:S(2)}) copy-start(s32[128]{0:T(128)} %param.11) | copy-start | bytes 1540
  3.4 30.4 %all-to-all-start = ((bf16[128,32,128]{2,1,0:T(8,128)(2,1)}), bf16[128,32,128]{2,1,0:T(8,128)(2,1)S(1)}, u32[]{:S(2)}, u32[]{:S(2)}) async-start(bf16[128,32,128]{2,1,0:T(8,128)(2,1)} %bitcast.22), calls=%async_computation | async-start | bytes 2097152 | tf_op jit(solution)/shard_map/all_to_all | solution.py:20
  17.2 40.8 %copy-start = (bf16[4,1024,256]{2,1,0:T(8,128)(2,1)S(1)}, bf16[4,1024,256]{2,1,0:T(8,128)(2,1)}, u32[]{:S(2)}) copy-start(bf16[4,1024,256]{2,1,0:T(8,128)(2,1)} %residual.1) | copy-start | bytes 6291460
  33.8 24.2 %copy-start.2 = (bf16[128,8,128]{2,1,0:T(8,128)(2,1)S(1)}, bf16[128,8,128]{2,1,0:T(8,128)(2,1)}, u32[]{:S(2)}) copy-start(bf16[128,8,128]{2,1,0:T(8,128)(2,1)} %pad_maximum_fusion.base) | copy-start | bytes 786436
  80.7 24.6 %all-to-all-start.3 = ((bf16[128,9,4,128]{3,2,1,0:T(4,128)(2,1)}), bf16[128,9,4,128]{3,2,1,0:T(4,128)(2,1)S(1)}, u32[]{:S(2)}, u32[]{:S(2)}) async-start(bf16[128,9,4,128]{3,2,1,0:T(4,128)(2,1)} %shard_map.86), calls=%async_computation.3 | async-start | bytes 2359296 | tf_op jit(solution)/shard_map/all_to_all | solution.py:20

commit v12 on v11

--- a/solution.py
+++ b/solution.py
@@ -187,11 +187,14 @@
         for half in range(2):
 
             def step(piece, carry, first=first, half=half):
-                for inner in range(4):
-                    tile = arrived[first, half, piece * 4 + inner, 4].astype(jnp.float32)
-                    at = (first * 2 + half) * 32 + pl.multiple_of(piece * 8, 8) + inner * 2
-                    for kind in range(3):
-                        pairs[kind, pl.ds(at, 2)] = tile[kind * 2 : kind * 2 + 2]
+                tall = [
+                    arrived[first, half, piece * 4 + inner, 4].astype(jnp.float32)
+                    for inner in range(4)
+                ]
+                at = pl.multiple_of((first * 2 + half) * 32 + piece * 8, 8)
+                for kind in range(3):
+                    taken_rows = [tile[kind * 2 : kind * 2 + 2] for tile in tall]
+                    pairs[kind, pl.ds(at, 8)] = jnp.concatenate(taken_rows, 0)
                 return carry
 
             lax.fori_loop(0, 4, step, 0)
@@ -443,7 +446,7 @@
             pltpu.SemaphoreType.DMA((count * 4,)),
             pltpu.SemaphoreType.DMA((count * 4,)),
         ],
-    )(offsets, in_hbm(tiles))
+    )(in_hbm(offsets), in_hbm(tiles))
     digits = jnp.stack([coarse_map // LANE, coarse_map % LANE]).astype(jnp.bfloat16)
     digits = jnp.concatenate([jnp.zeros_like(digits), digits], 0)
     shared = turned_modes[:, :, : 4 * HALF].reshape(count, MODES, 2, 2, HALF)

time: 172 us -> 172 us (level)
  no operation moved by 1% of the time
where the time goes in v12:
time: 172 us; the launch traced here: 171 us
  blocking collectives  93.5 us (54%)
  Pallas kernels  30.4 us (18%)
  waiting for transfers between devices  29.2 us (17%)
  starting transfers between devices  15.8 us (9%)
    all_to_all x4, blocking collectives, spread(): return lax.all_to_all(value, AXES, 0, 0, tiled=True)  93.5 us
    all_to_all x2, waiting for transfers between devices, spread(): return lax.all_to_all(value, AXES, 0, 0, tiled=True)  29.2 us
    all_to_all x2, starting transfers between devices, spread(): return lax.all_to_all(value, AXES, 0, 0, tiled=True)  15.8 us
    pallas_call x1, Pallas kernels, shards(): call(local_kernel, (pltpu.HBM(residual.shape, jnp.float32), pltpu.HBM(pac...  7.66 us
    pallas_call x1, Pallas kernels, shards(): call(scatter_kernel, pltpu.HBM((devices, tiles + 1, 4, LANE), jnp.bfloat1...  4.64 us
    pallas_call x1, Pallas kernels, shards(): call(finish_kernel, field, in_specs=[smem(), hbm, whole(), whole(), whole...  4.49 us
    pallas_call x1, Pallas kernels, shards(): call(functools.partial(gather_kernel, row_blocks=lax.axis_size('row')), j...  3.64 us
    pallas_call x1, Pallas kernels, shards(): call(product_kernel, (jax.ShapeDtypeStruct(joined_shape, jnp.bfloat16), j...  3.48 us
  transfers between devices with their start and end apart: 2, of which 2 were waited for; matrix products, arithmetic and copies ran while one was open for 1% of the time, Pallas kernels for 4%

profile of v12, /device:TPU:1, one launch (start us, length us, event | category | flops | bytes accessed | tf_op | source)
XLA Modules:
  0.0 171.5 jit_solution(4927438676163588800)
XLA Ops:
  0.0 0.0 copy-start.1
  0.0 3.0 %shard_map.82 = bf16[4,2,16,4,8,128]{5,4,3,2,1,0:T(8,128)(2,1)} custom-call(s32[2,4]{1,0:T(2,128)} %bitcast.20, bf16[4,128,2,8,128]{4,3,2,1,0:T(8,128)(2,1)} %bitcast.14), custom_call_target="tpu_custom_call" | custom-call | tf_op jit(solution)/shard_map/pallas_call | solution.py:439
  3.0 0.0 copy-start.6
  3.0 11.5 %all-to-all-start = ((bf16[128,32,128]{2,1,0:T(8,128)(2,1)}), bf16[128,32,128]{2,1,0:T(8,128)(2,1)S(1)}, u32[]{:S(2)}, u32[]{:S(2)}) async-start(bf16[128,32,128]{2,1,0:T(8,128)(2,1)} %bitcast.22), calls=%async_computation | async-start | bytes 2097152 | tf_op jit(solution)/shard_map/all_to_all | solution.py:20
  14.5 0.0 copy-done.3
  14.6 0.0 copy-done.4
  14.6 0.1 copy.13
  14.7 0.1 reshape.31
  14.8 0.1 copy.12
  14.9 0.1 reshape.30
  14.9 0.0 copy-done.5
  15.0 0.1 slice_reduce_fusion
  15.1 0.1 copy.14
  15.3 0.1 pad_add_fusion.table
  15.4 0.3 broadcast_select_fusion
  15.7 0.3 pad_maximum_fusion.1
  16.0 0.8 pad_maximum_fusion.base
  16.8 16.6 %all-to-all-done.chunks = bf16[128,32,128]{2,1,0:T(8,128)(2,1)S(1)} async-done(((bf16[128,32,128]{2,1,0:T(8,128)(2,1)}), bf16[128,32,128]{2,1,0:T(8,128)(2,1)S(1)}, u32[]{:S(2)}, u32[]{:S(2)}) %all-to-all-start) | async-done | bytes 1048608 | tf_op jit(solution)/shard_map/all_to_all | solution.py:20
  33.4 0.9 shard_map.83
  34.3 23.3 %all_to_all.30 = bf16[128,32,128]{2,1,0:T(8,128)(2,1)S(1)} all-to-all(bf16[128,32,128]{2,1,0:T(8,128)(2,1)S(1)} %shard_map.83), channel_id=1, replica_groups=mesh['row'=16,'col'=8] {'row','col'}, dimensions={0} | all-to-all | bytes 2097152 | tf_op jit(solution)/shard_map/all_to_all | solution.py:20
  57.6 0.0 copy-done
  57.6 2.6 %shard_map.84 = (bf16[4,1024,256]{2,1,0:T(8,128)(2,1)}, bf16[128,8,128]{2,1,0:T(8,128)(2,1)S(1)}) custom-call(s32[20]{0:T(128)S(1)} %pad_add_fusion.table, bf16[4,1024,256]{2,1,0:T(8,128)(2,1)S(1)} %copy-done, bf16[4,32,1024]{2,1,0:T(8,128)(2,1)S(1)} %bitcast.18, bf16[4,2,16,4,8,128]{5,4,3,2,1,0:T(8,128)(2,1)S(1)} %bitcast.16, bf16[128,8,128]{2,1,0:T(8,128)(2,1)S(1)} %copy-done.2), custom_call_target="tpu_custom_call" | custom-call | tf_op jit(solution)/shard_map/pallas_call | solution.py:459
  60.2 15.5 %all_to_all.31.received = bf16[128,8,128]{2,1,0:T(8,128)(2,1)S(1)} all-to-all(bf16[128,8,128]{2,1,0:T(8,128)(2,1)S(1)} %get-tuple-element.18), channel_id=1, replica_groups=mesh['row'=16,'col'=8] {'row','col'}, dimensions={0} | all-to-all | bytes 524288 | tf_op jit(solution)/shard_map/all_to_all | solution.py:20
  75.7 4.6 %shard_map.86 = bf16[128,9,4,128]{3,2,1,0:T(4,128)(2,1)} custom-call(s32[20]{0:T(128)S(1)} %pad_add_fusion.table, bf16[128,8,128]{2,1,0:T(8,128)(2,1)S(1)} %all_to_all.31.received), custom_call_target="tpu_custom_call" | custom-call | tf_op jit(solution)/shard_map/pallas_call | solution.py:494
  80.3 4.3 %all-to-all-start.3 = ((bf16[128,9,4,128]{3,2,1,0:T(4,128)(2,1)}), bf16[128,9,4,128]{3,2,1,0:T(4,128)(2,1)S(1)}, u32[]{:S(2)}, u32[]{:S(2)}) async-start(bf16[128,9,4,128]{3,2,1,0:T(4,128)(2,1)} %shard_map.86), calls=%async_computation.3 | async-start | bytes 2359296 | tf_op jit(solution)/shard_map/all_to_all | solution.py:20
  84.7 7.7 %shard_map.85 = (f32[4,1024,256]{2,1,0:T(8,128)}, bf16[4,2,16,4,8,128]{5,4,3,2,1,0:T(8,128)(2,1)}) custom-call(s32[2,4]{1,0:T(2,128)S(1)} %bitcast.21, bf16[4,1024,1024]{2,1,0:T(8,128)(2,1)} %inverse.2, bf16[4,1024,256]{2,1,0:T(8,128)(2,1)} %get-tuple-element.19.weighted), custom_call_target="tpu_custom_call" | custom-call | tf_op jit(solution)/shard_map/pallas_call | solution.py:479
  92.3 12.6 %all-to-all-done.3.placed = bf16[128,9,4,128]{3,2,1,0:T(4,128)(2,1)S(1)} async-done(((bf16[128,9,4,128]{3,2,1,0:T(4,128)(2,1)}), bf16[128,9,4,128]{3,2,1,0:T(4,128)(2,1)S(1)}, u32[]{:S(2)}, u32[]{:S(2)}) %all-to-all-start.3) | async-done | bytes 1179680 | tf_op jit(solution)/shard_map/all_to_all | solution.py:20
  104.9 3.5 %shard_map.87 = (bf16[128,48,128]{2,1,0:T(8,128)(2,1)S(1)}, bf16[4,4,32,128]{3,2,1,0:T(8,128)(2,1)S(1)}) custom-call(bf16[128,9,4,128]{3,2,1,0:T(4,128)(2,1)S(1)} %all-to-all-done.3.placed, bf16[1024,2048]{1,0:T(8,128)(2,1)} %inverse.3, bf16[128,32,128]{2,1,0:T(8,128)(2,1)} %bitcast.23), custom_call_target="tpu_custom_call" | custom-call | tf_op jit(solution)/shard_map/pallas_call | solution.py:512
  108.4 28.9 %all_to_all.32.partial = bf16[128,48,128]{2,1,0:T(8,128)(2,1)S(1)} all-to-all(bf16[128,48,128]{2,1,0:T(8,128)(2,1)S(1)} %get-tuple-element.23), channel_id=1, replica_groups=mesh['row'=16,'col'=8] {'row','col'}, dimensions={0} | all-to-all | bytes 3145728 | tf_op jit(solution)/shard_map/all_to_all | solution.py:20
  137.3 3.6 %shard_map.88 = bf16[128,40,128]{2,1,0:T(8,128)(2,1)S(1)} custom-call(s32[20]{0:T(128)S(1)} %pad_add_fusion.table, bf16[128,8,128]{2,1,0:T(8,128)(2,1)S(1)} %all_to_all.31.received, bf16[128,48,128]{2,1,0:T(8,128)(2,1)S(1)} %all_to_all.32.partial), custom_call_target="tpu_custom_call" | custom-call | tf_op jit(solution)/shard_map/pallas_call | solution.py:530
  141.0 25.9 %all_to_all.33 = bf16[128,40,128]{2,1,0:T(8,128)(2,1)S(1)} all-to-all(bf16[128,40,128]{2,1,0:T(8,128)(2,1)S(1)} %shard_map.88), channel_id=1, replica_groups=mesh['row'=16,'col'=8] {'row','col'}, dimensions={0} | all-to-all | bytes 2621440 | tf_op jit(solution)/shard_map/all_to_all | solution.py:20
  166.8 4.5 %shard_map.89 = bf16[4,1024,256]{2,1,0:T(8,128)(2,1)} custom-call(s32[20]{0:T(128)S(1)} %pad_add_fusion.table, f32[4,1024,256]{2,1,0:T(8,128)} %get-tuple-element.20.local, bf16[4,32,1024]{2,1,0:T(8,128)(2,1)S(1)} %bitcast.19, bf16[4,2,16,5,8,128]{5,4,3,2,1,0:T(8,128)(2,1)S(1)} %bitcast.15, bf16[4,4,32,128]{3,2,1,0:T(8,128)(2,1)S(1)} %get-tuple-element.24.their_modes), custom_call_target="tpu_custom_call" | custom-call | tf_op jit(solution)/shard_map/pallas_call | solution.py:541
  (16 shorter events, 0.2 us)
Async XLA Ops:
  0.0 14.5 %copy-start.3 = (s32[4,2]{0,1:T(2,128)S(1)}, s32[4,2]{0,1:T(2,128)}, u32[]{:S(2)}) copy-start(s32[4,2]{0,1:T(2,128)} %param.15) | copy-start | bytes 100
  0.0 14.6 %copy-start.4 = (s32[4,2]{0,1:T(2,128)S(1)}, s32[4,2]{0,1:T(2,128)}, u32[]{:S(2)}) copy-start(s32[4,2]{0,1:T(2,128)} %param.14) | copy-start | bytes 100
  0.0 14.9 %copy-start.5 = (s32[4,2]{0,1:T(2,128)S(1)}, s32[4,2]{0,1:T(2,128)}, u32[]{:S(2)}) copy-start(s32[4,2]{0,1:T(2,128)} %param.13) | copy-start | bytes 100
  0.0 15.2 %copy-start.1 = (bf16[4,1024,32]{1,2,0:T(8,128)(2,1)S(1)}, bf16[4,1024,32]{1,2,0:T(8,128)(2,1)}, u32[]{:S(2)}) copy-start(bf16[4,1024,32]{1,2,0:T(8,128)(2,1)} %param.10) | copy-start | bytes 786436
  3.0 12.3 %copy-start.6 = (s32[128]{0:T(128)S(1)}, s32[128]{0:T(128)}, u32[]{:S(2)}) copy-start(s32[128]{0:T(128)} %param.11) | copy-start | bytes 1540
  3.0 30.4 %all-to-all-start = ((bf16[128,32,128]{2,1,0:T(8,128)(2,1)}), bf16[128,32,128]{2,1,0:T(8,128)(2,1)S(1)}, u32[]{:S(2)}, u32[]{:S(2)}) async-start(bf16[128,32,128]{2,1,0:T(8,128)(2,1)} %bitcast.22), calls=%async_computation | async-start | bytes 2097152 | tf_op jit(solution)/shard_map/all_to_all | solution.py:20
  16.8 40.8 %copy-start = (bf16[4,1024,256]{2,1,0:T(8,128)(2,1)S(1)}, bf16[4,1024,256]{2,1,0:T(8,128)(2,1)}, u32[]{:S(2)}) copy-start(bf16[4,1024,256]{2,1,0:T(8,128)(2,1)} %residual.1) | copy-start | bytes 6291460
  33.4 24.2 %copy-start.2 = (bf16[128,8,128]{2,1,0:T(8,128)(2,1)S(1)}, bf16[128,8,128]{2,1,0:T(8,128)(2,1)}, u32[]{:S(2)}) copy-start(bf16[128,8,128]{2,1,0:T(8,128)(2,1)} %pad_maximum_fusion.base) | copy-start | bytes 786436
  80.3 24.6 %all-to-all-start.3 = ((bf16[128,9,4,128]{3,2,1,0:T(4,128)(2,1)}), bf16[128,9,4,128]{3,2,1,0:T(4,128)(2,1)S(1)}, u32[]{:S(2)}, u32[]{:S(2)}) async-start(bf16[128,9,4,128]{3,2,1,0:T(4,128)(2,1)} %shard_map.86), calls=%async_computation.3 | async-start | bytes 2359296 | tf_op jit(solution)/shard_map/all_to_all | solution.py:20
